TPU v7x, 256 devices: a whole 4x4x8 slice. The times are simulated.
256 devices in a mesh: blk: 32 (over z, y), lblk: 8 (over x, core).
Axes of the slice: x: 4, y: 4, z: 8, core: 2. Of those that a mesh axis runs over, the one named last changes fastest.
Arguments:
- partial_rows: bfloat16 [8, 32768, 1024], P('lblk', 'blk'), may hold values from -5 to 5
- row_owner: int32 [8, 32768, 1], P('lblk', 'blk'), may hold values from 0 to 31; in each aligned block of 1024 rows (0 to 1023, 1024 to 2047, ..., all dimensions but the last counted through in order) at most 128 rows name the same one
- row_key: int32 [8, 32768], P('lblk', 'blk'), may hold values from 0 to 127
- azimuth_orders: int32 [32], replicated, may hold values from 1 to 4095, as said below
- legendre_table: bfloat16 [32, 4096, 2048], P('blk', 'lblk'), may hold values from -0.125 to 0.125
- spin_even: bfloat16 [32, 4096, 2048], P('blk', 'lblk'), may hold values from -0.125 to 0.125
- spin_odd: bfloat16 [32, 4096, 2048], P('blk', 'lblk'), may hold values from -0.125 to 0.125
Outputs:
- eigenvalues: float32 [2, 2, 8, 256, 8192], P(None, None, 'lblk', 'blk')
- cycle_maps: float32 [2, 8, 256, 8192], P(None, 'lblk', 'blk')
Inputs may be any that keep to these rules, and one draw needn't show every extreme that they name: `row_owner`: no more than 128 rows of one device name the same owner; some device sends exactly 128 rows to some owner in every draw. `azimuth_orders`: all distinct; 1 and 4095 are always among them.
All inputs are finite; a program needn't handle non-finite values.
Results may differ from a plain program's by a relative error of at most 0.0041.
Values may be sent and summed in bfloat16 or wider, within the bound.
No kernel may reach another device: no remote copies, remote signals or barrier semaphores. Data moves between devices by JAX's collectives and lax.ppermute only.
A program may use at most 128 MiB of HBM per device.

v0:
```python
import functools
import math

import jax
import jax.numpy as jnp
from jax import lax
from jax.experimental import pallas as pl
from jax.experimental.pallas import tpu as pltpu
from jax.sharding import Mesh
from jax.sharding import PartitionSpec as P


NPHI = 8192
L = 4096
SEG = 1024
R_DEV = 8
PR = 1024
KEYS = 128
POS = NPHI // SEG
BLK = ("blk_0", "blk_1")

NT = (((1,), (1,)), ((), ()))
NN = (((1,), (0,)), ((), ()))


def halves(x):
    high = x.astype(jnp.bfloat16)
    low = (x - high.astype(jnp.float32)).astype(jnp.bfloat16)
    return high, low


def dot32(a, b, dims):
    return lax.dot_general(a, b, dims, preferred_element_type=jnp.float32)


def wave_tables(azimuth_orders):
    phase = lax.broadcasted_iota(jnp.int32, (azimuth_orders.shape[0], SEG), 1)
    phase = phase * azimuth_orders[:, None] % NPHI
    angles = phase.astype(jnp.float32) * (2.0 * math.pi / NPHI)
    return jnp.concatenate([jnp.cos(angles), jnp.sin(angles)], axis=0)


def eighth_turn(index):
    angle = (index & (POS - 1)).astype(jnp.float32) * (2.0 * math.pi / POS)
    return jnp.cos(angle), jnp.sin(angle)


def modes_kernel(slices, rows_ref, owner_ref, key_ref, order_ref, wave_ref, out_ref):
    orders = order_ref.shape[0]
    w_high, w_low = halves(wave_ref[...])
    rows = rows_ref[...]
    seg = dot32(w_high, rows, NT) + dot32(w_low, rows, NT)
    cos_part, sin_part = seg[:orders], seg[orders:]
    key = key_ref[...]
    turn_cos, turn_sin = eighth_turn(order_ref[...] * (key & (POS - 1)))
    modes = jnp.concatenate(
        [
            cos_part * turn_cos - sin_part * turn_sin,
            sin_part * turn_cos + cos_part * turn_sin,
        ],
        axis=0,
    )
    cycles = slices * R_DEV
    slot = (key >> 6) * cycles + owner_ref[...] * R_DEV + ((key >> 3) & (R_DEV - 1))
    pick = lax.broadcasted_iota(jnp.int32, (2 * cycles, PR), 0) == slot
    pick = jnp.where(pick, 1.0, 0.0).astype(jnp.bfloat16)
    m_high, m_low = halves(modes)
    sums = dot32(m_high, pick, NT) + dot32(m_low, pick, NT)
    parts = cycles // 128
    for trig in range(2):
        for shell in range(2):
            for part in range(parts):
                out_ref[:, part * 4 + trig * 2 + shell, :] = sums[
                    trig * orders : (trig + 1) * orders,
                    shell * cycles + part * 128 : shell * cycles + (part + 1) * 128,
                ]


def local_modes(rows, owners, keys, azimuth_orders, waves, groups):
    orders = azimuth_orders.shape[0]
    return pl.pallas_call(
        functools.partial(modes_kernel, groups),
        out_shape=jax.ShapeDtypeStruct((orders, groups * R_DEV * 4 // 128, 128), jnp.float32),
        name="modes",
    )(rows, owners, keys, azimuth_orders[:, None], waves)


def harmonics_kernel(in_ref, out_ref):
    total = jnp.sum(in_ref[...], axis=0) * (1.0 / math.sqrt(NPHI))
    row = lax.broadcasted_iota(jnp.int32, total.shape, 0)
    total = jnp.where((row & 2) == 0, total, -total)
    out_ref[...] = jnp.broadcast_to(total[None], out_ref.shape).astype(out_ref.dtype)


def harmonics_for_all(arrived, copies):
    return pl.pallas_call(
        harmonics_kernel,
        out_shape=jax.ShapeDtypeStruct((copies, *arrived.shape[1:]), jnp.bfloat16),
        name="harmonics",
    )(arrived)


def legendre_kernel(first_ref, modes_ref, leg_ref, even_hbm, odd_hbm, out_ref, even, odd, sem):
    even_copy = pltpu.make_async_copy(even_hbm, even, sem.at[0])
    odd_copy = pltpu.make_async_copy(odd_hbm, odd, sem.at[1])
    even_copy.start()
    odd_copy.start()
    blocks, rows = modes_ref.shape[0], modes_ref.shape[1]
    pieces = []
    for block in range(blocks):
        value = modes_ref[block].astype(jnp.float32)
        for part in range(rows // 4):
            pieces.append(value[part * 4 : (part + 1) * 4])
    spectrum = jnp.concatenate(pieces, axis=1).astype(jnp.bfloat16)
    coefficients = dot32(spectrum, leg_ref[0], NT)
    width = coefficients.shape[1]
    degree = first_ref[0] + lax.broadcasted_iota(jnp.int32, (1, width), 1)
    degree = degree.astype(jnp.float32)
    smoothing = jnp.exp(-2.0 * degree * (degree + 1.0) / (L * L))
    factor = jnp.sqrt(
        jnp.maximum((degree - 1.0) * (degree + 2.0), 0.0)
        / jnp.maximum(degree * (degree + 1.0), 1.0)
    )
    trace_terms = (smoothing * coefficients).astype(jnp.bfloat16)
    shear_terms = ((-0.5 * smoothing * factor) * coefficients).astype(jnp.bfloat16)
    own = out_ref.shape[2]

    def put(kind, value):
        for block in range(blocks):
            out_ref[block, kind * 4 : kind * 4 + 4, :] = value[:, block * own : (block + 1) * own]

    put(0, dot32(trace_terms, leg_ref[0], NN))
    even_copy.wait()
    put(1, dot32(shear_terms, even[0], NN))
    odd_copy.wait()
    put(2, dot32(shear_terms, odd[0], NN))


def legendre_pair(first_degree, modes, legendre_table, spin_even, spin_odd):
    vmem = pl.BlockSpec(memory_space=pltpu.VMEM)
    left = pl.BlockSpec(memory_space=pl.ANY)
    blocks = modes.shape[0]
    cycles = legendre_table.shape[2]
    return pl.pallas_call(
        legendre_kernel,
        out_shape=jax.ShapeDtypeStruct((blocks, 12, cycles // blocks), jnp.float32),
        in_specs=[pl.BlockSpec(memory_space=pltpu.SMEM), vmem, vmem, left, left],
        out_specs=vmem,
        scratch_shapes=[
            pltpu.VMEM(spin_even.shape, spin_even.dtype),
            pltpu.VMEM(spin_odd.shape, spin_odd.dtype),
            pltpu.SemaphoreType.DMA((2,)),
        ],
        name="legendre",
    )(first_degree, modes, legendre_table, spin_even, spin_odd)


def fields_kernel(scale, terms_ref, order_ref, wave_ref, out_ref):
    position = pl.program_id(0)
    turn_cos, turn_sin = eighth_turn(order_ref[...] * position)
    real, imag = [], []
    for kind in range(3):
        for shell in range(2):
            cos_term, sin_term = terms_ref[kind * 4 + shell], terms_ref[kind * 4 + 2 + shell]
            real.append(-sin_term if kind == 2 else cos_term)
            imag.append(cos_term if kind == 2 else sin_term)
    real = jnp.concatenate(real, axis=0)
    imag = jnp.concatenate(imag, axis=0)
    turned = jnp.concatenate(
        [real * turn_cos - imag * turn_sin, -(real * turn_sin + imag * turn_cos)], axis=1
    )
    t_high, t_low = halves(turned)
    w_high, w_low = halves(wave_ref[...])
    fields = (dot32(t_high, w_high, NN) + (dot32(t_high, w_low, NN) + dot32(t_low, w_high, NN))) * scale
    fields = fields.reshape(3, 2, R_DEV, SEG)
    for shell in range(2):
        half_trace = 0.5 * fields[0, shell]
        first, second = fields[1, shell], fields[2, shell]
        size = jnp.sqrt(first * first + second * second)
        out_ref[0, shell, 0] = half_trace + size
        out_ref[1, shell, 0] = half_trace - size


def eigenvalues(terms, azimuth_orders, waves):
    orders = azimuth_orders.shape[0]
    whole = lambda *shape: pl.BlockSpec(shape, lambda p: (0,) * len(shape))
    return pl.pallas_call(
        functools.partial(fields_kernel, 2.0 / math.sqrt(orders)),
        out_shape=jax.ShapeDtypeStruct((2, 2, 1, R_DEV, NPHI), jnp.float32),
        grid=(POS,),
        in_specs=[whole(12, R_DEV, orders), whole(1, orders), whole(2 * orders, SEG)],
        out_specs=pl.BlockSpec((2, 2, 1, R_DEV, SEG), lambda p: (0, 0, 0, 0, p)),
        name="fields",
    )(terms, azimuth_orders[None], waves)


def shifted(x, axis, by):
    size = lax.axis_size(axis)
    return lax.ppermute(x, axis, [(i, (i + by) % size) for i in range(size)])


def ring_sums(chunk, axis):
    size = lax.axis_size(axis)
    middle = size // 2
    half = chunk(middle).shape[0] // 2

    def toward(by, first):
        far = chunk(middle)
        moving = far[:half] if first else far[half:]
        for distance in range(middle - 1, -1, -1):
            moving = shifted(moving.astype(jnp.bfloat16), axis, by).astype(jnp.float32)
            if distance == 0:
                return moving
            own = chunk(distance if by == 1 else size - distance)
            if distance == middle - 1:
                if first:
                    moving = jnp.concatenate([own[:half] + moving, own[half:]], axis=0)
                else:
                    moving = jnp.concatenate([own[:half], own[half:] + moving], axis=0)
            else:
                moving = own + moving

    return chunk(0), toward(1, True), toward(-1, False)


def row_slots(owners, keys):
    place = (keys & 64) + (keys & 7) * R_DEV + ((keys >> 3) & 7)
    return owners * KEYS + place


def picked(slots, base, count, rows):
    pick = lax.broadcasted_iota(jnp.int32, (count, slots.shape[0]), 0) == (slots - base)[None, :]
    return jnp.dot(pick.astype(jnp.bfloat16), rows, preferred_element_type=jnp.float32)


def after(x, token):
    return lax.optimization_barrier((x, token))[0]


class ColumnSums:
    def __init__(self, rows, owners, keys):
        self.slots = row_slots(owners, keys)
        self.rows = rows
        half = PR // 2
        axis = BLK[1]
        self.up_slots = shifted(self.slots, axis, 1)
        self.down_slots = shifted(self.slots, axis, -1)
        self.far_slots = shifted(self.slots, axis, 2)
        first, last = rows[:half], rows[half:]
        self.up = [shifted(first, axis, 1), shifted(last, axis, 1)]
        self.down = [shifted(last, axis, -1), shifted(first, axis, -1)]

    def forward(self, token):
        self.up_far = shifted(after(self.up[0], token), BLK[1], 1)
        self.down_far = shifted(after(self.down[0], token), BLK[1], -1)

    def column_sums(self, slot, values):
        ny, nz = lax.axis_size(BLK[1]), lax.axis_size(BLK[0])
        my_y, my_z = lax.axis_index(BLK[1]), lax.axis_index(BLK[0])
        owner, place = slot // KEYS, slot % KEYS
        distance = (owner // ny - my_z) % nz
        mine = jnp.where(owner % ny == my_y, distance * KEYS + place, -1)
        return picked(mine, 0, nz * KEYS, values)

    def finish(self, token):
        half = PR // 2
        up, down, far = self.up_slots, self.down_slots, self.far_slots
        near = self.column_sums(self.slots, self.rows)
        near = near + self.column_sums(up[:half], self.up[0])
        near = near + self.column_sums(down[half:], self.down[0])
        near = near + self.column_sums(up[half:], self.up[1])
        near = near + self.column_sums(down[:half], self.down[1])
        sums = near + self.column_sums(far[:half], self.up_far)
        sums = sums + self.column_sums(far[half:], self.down_far)
        sums = after(sums, token)
        return ring_sums(lambda d: sums[d * KEYS : (d + 1) * KEYS], BLK[0])


def maps_kernel(own_ref, up_ref, down_ref, out_ref):
    total = own_ref[...] + up_ref[...].astype(jnp.float32) + down_ref[...].astype(jnp.float32)
    for shell in range(2):
        for position in range(POS):
            row = (shell * POS + position) * R_DEV
            out_ref[shell, 0, :, position * SEG : (position + 1) * SEG] = total[row : row + R_DEV]


def map_output(own, up, down):
    return pl.pallas_call(
        maps_kernel,
        out_shape=jax.ShapeDtypeStruct((2, 1, R_DEV, NPHI), jnp.float32),
        name="maps",
    )(own, up.astype(jnp.bfloat16), down.astype(jnp.bfloat16))


def body(partial_rows, row_owner, row_key, azimuth_orders, legendre_table, spin_even, spin_odd):
    groups = lax.axis_size(BLK)
    blocks = lax.axis_size("lblk")
    rows = partial_rows[0]
    owners = row_owner[0, :, 0]
    keys = row_key[0]
    orders = azimuth_orders.shape[0]
    waves = wave_tables(azimuth_orders)

    columns = ColumnSums(rows, owners, keys)
    sums = local_modes(rows, owners[None], keys[None], azimuth_orders, waves, groups)
    arrived = lax.all_to_all(sums, BLK, split_axis=0, concat_axis=0, tiled=True)
    columns.forward(arrived)
    modes = harmonics_for_all(arrived, blocks)
    modes = lax.all_to_all(modes, "lblk", 0, 0, tiled=True)
    first_degree = (lax.axis_index("lblk") * legendre_table.shape[1]).astype(jnp.int32)[None]
    pieces = legendre_pair(first_degree, modes, legendre_table, spin_even, spin_odd)
    pieces = lax.all_to_all(pieces, "lblk", split_axis=0, concat_axis=0, tiled=True)
    summed = pieces.sum(axis=0).astype(jnp.bfloat16)
    summed = summed.reshape(12, groups, R_DEV).transpose(1, 0, 2).reshape(groups, 12 * R_DEV)
    returned = lax.all_to_all(summed, BLK, split_axis=0, concat_axis=0, tiled=True)
    terms = returned.astype(jnp.float32).T.reshape(12, R_DEV, orders)
    eigen = eigenvalues(terms, azimuth_orders, waves)
    return (eigen, map_output(*columns.finish(returned)))


def solution(mesh):
    finer = Mesh(mesh.devices.reshape(8, 4, mesh.shape["lblk"]), ("blk_0", "blk_1", "lblk"))
    placed = (
        P("lblk", BLK, None),
        P("lblk", BLK, None),
        P("lblk", BLK),
        P(),
        P(BLK, "lblk", None),
        P(BLK, "lblk", None),
        P(BLK, "lblk", None),
    )
    return jax.shard_map(
        body,
        mesh=finer,
        in_specs=placed,
        out_specs=(P(None, None, "lblk", BLK, None), P(None, "lblk", BLK, None)),
        check_vma=False,
    )
```

profile of v0, /device:TPU:2, one launch (start us, length us, event | category | flops | bytes accessed | tf_op | source)
XLA Modules:
  0.0 162.9 jit_solution(10513373921696218343)
XLA Ops:
  2.3 3.3 %collective-permute-start.6 = (s32[1024]{0:T(1024)S(1)}, s32[1024]{0:T(1024)S(1)}, u32[]{:S(2)}, u32[]{:S(2)}) collective-permute-start(s32[1024]{0:T(1024)S(1)} %add.198), channel_id=1, source_target_pairs={{0,16},{8,24},{16,0},{24,8},{1,17},{9,25},{17,1},{25,9},{2,18},{10... | collective-permute-start | bytes 12296 | tf_op jit(solution)/shard_map/ppermute | solution.py:199
  6.3 2.6 %collective-permute-start.2 = (s32[1024]{0:T(1024)S(1)}, s32[1024]{0:T(1024)S(1)}, u32[]{:S(2)}, u32[]{:S(2)}) collective-permute-start(s32[1024]{0:T(1024)S(1)} %add.198), channel_id=1, source_target_pairs={{0,24},{8,0},{16,8},{24,16},{1,25},{9,1},{17,9},{25,17},{2,26},{10... | collective-permute-start | bytes 12296 | tf_op jit(solution)/shard_map/ppermute | solution.py:199
  12.1 4.6 %modes.1 = f32[32,8,128]{2,1,0:T(8,128)} custom-call(bf16[1024,1024]{1,0:T(8,128)(2,1)} %bitcast.29, s32[1,1024]{1,0:T(1,128)} %bitcast.33, s32[1,1024]{1,0:T(1,128)} %key_ref.1, s32[32,1]{1,0:T(8,128)} %copy.17.order_ref, f32[64,1024]{1,0:T(8,128)} %pad_maximum_fusion.wave_ref), custom_call_target="tpu_custom_call" | custom-call | tf_op jit(solution)/shard_map/modes/pallas_call | solution.py:81
  16.8 8.9 %all-to-all-start = ((f32[32,8,128]{2,1,0:T(8,128)}), f32[32,8,128]{2,1,0:T(8,128)S(1)}, u32[]{:S(2)}, u32[]{:S(2)}) async-start(f32[32,8,128]{2,1,0:T(8,128)} %modes.1), calls=%async_computation | async-start | bytes 262144 | tf_op jit(solution)/shard_map/all_to_all | solution.py:306
  26.8 1.8 %collective-permute-start.1 = (bf16[512,1024]{1,0:T(8,128)(2,1)S(1)}, bf16[512,1024]{1,0:T(8,128)(2,1)}, u32[]{:S(2)}, u32[]{:S(2)}) collective-permute-start(bf16[512,1024]{1,0:T(8,128)(2,1)S(1)} %get-tuple-element.22), channel_id=1, source_target_pairs={{0,8},{8,16},{16,24},{24,0},{1,9},{9,17},{17,25},{25,1},{2,10},{10... | collective-permute-start | bytes 3145736 | tf_op jit(solution)/shard_map/ppermute | solution.py:199
  30.0 4.3 %fusion = f32[1024,1024]{1,0:T(8,128)} fusion(s32[1024]{0:T(1024)S(1)} %bitcast.38, bf16[1,1024,1024]{2,1,0:T(8,128)(2,1)S(1)} %copy-done), kind=kOutput, calls=%fused_computation.2 | convolution fusion | flops 2148532224 | bytes 6295552 | tf_op jit(solution)/shard_map/dot_general | solution.py:233
  34.3 1.9 %all-to-all-done.in_ref = f32[32,8,128]{2,1,0:T(8,128)S(1)} async-done(((f32[32,8,128]{2,1,0:T(8,128)}), f32[32,8,128]{2,1,0:T(8,128)S(1)}, u32[]{:S(2)}, u32[]{:S(2)}) %all-to-all-start) | async-done | bytes 131104 | tf_op jit(solution)/shard_map/all_to_all | solution.py:306
  36.9 1.5 harmonics.1
  38.5 4.8 %all-to-all-start.1 = ((bf16[8,8,128]{2,1,0:T(8,128)(2,1)}), bf16[8,8,128]{2,1,0:T(8,128)(2,1)S(1)}, u32[]{:S(2)}, u32[]{:S(2)}) async-start(bf16[8,8,128]{2,1,0:T(8,128)(2,1)} %harmonics.1), calls=%async_computation.1 | async-start | bytes 32768 | tf_op jit(solution)/shard_map/all_to_all | solution.py:309
  43.5 3.7 %all-to-all-done.1.modes_ref = bf16[8,8,128]{2,1,0:T(8,128)(2,1)S(1)} async-done(((bf16[8,8,128]{2,1,0:T(8,128)(2,1)}), bf16[8,8,128]{2,1,0:T(8,128)(2,1)S(1)}, u32[]{:S(2)}, u32[]{:S(2)}) %all-to-all-start.1) | async-done | bytes 16416 | tf_op jit(solution)/shard_map/all_to_all | solution.py:309
  47.8 5.4 %legendre.1 = f32[8,12,256]{2,1,0:T(8,128)} custom-call(s32[1]{0:T(128)} %bitcast.first_ref, bf16[8,8,128]{2,1,0:T(8,128)(2,1)} %copy-done.5, bf16[1,512,2048]{2,1,0:T(8,128)(2,1)} %leg_ref.1, bf16[1,512,2048]{2,1,0:T(8,128)(2,1)} %even_hbm.1, bf16[1,512,2048]{2,1,0:T(8,128)(2,1)} %odd_hbm.1), custom_call_target="tpu_custom_call" | custom-call | tf_op jit(solution)/shard_map/legendre/pallas_call | solution.py:144
  53.2 4.8 %all-to-all-start.2 = ((f32[8,12,256]{2,1,0:T(8,128)}), f32[8,12,256]{2,1,0:T(8,128)S(1)}, u32[]{:S(2)}, u32[]{:S(2)}) async-start(f32[8,12,256]{2,1,0:T(8,128)} %legendre.1), calls=%async_computation.2 | async-start | bytes 262144 | tf_op jit(solution)/shard_map/all_to_all | solution.py:312
  59.4 3.3 %all-to-all-done.2 = f32[8,12,256]{2,1,0:T(8,128)S(1)} async-done(((f32[8,12,256]{2,1,0:T(8,128)}), f32[8,12,256]{2,1,0:T(8,128)S(1)}, u32[]{:S(2)}, u32[]{:S(2)}) %all-to-all-start.2) | async-done | bytes 98336 | tf_op jit(solution)/shard_map/all_to_all | solution.py:312
  63.6 6.6 %all-to-all-start.3 = ((bf16[32,1,96]{2,1,0:T(2,128)(2,1)}), bf16[32,1,96]{2,1,0:T(2,128)(2,1)S(1)}, u32[]{:S(2)}, u32[]{:S(2)}) async-start(bf16[32,1,96]{2,1,0:T(2,128)(2,1)} %copy.19), calls=%async_computation.3 | async-start | bytes 32768 | tf_op jit(solution)/shard_map/all_to_all | solution.py:315
  70.3 13.1 %all-to-all-done.3 = bf16[32,1,96]{2,1,0:T(2,128)(2,1)S(1)} async-done(((bf16[32,1,96]{2,1,0:T(2,128)(2,1)}), bf16[32,1,96]{2,1,0:T(2,128)(2,1)S(1)}, u32[]{:S(2)}, u32[]{:S(2)}) %all-to-all-start.3) | async-done | bytes 6176 | tf_op jit(solution)/shard_map/all_to_all | solution.py:315
  83.9 2.8 %collective-permute-start.8 = (bf16[512,1024]{1,0:T(8,128)(2,1)}, bf16[512,1024]{1,0:T(8,128)(2,1)S(1)}, u32[]{:S(2)}, u32[]{:S(2)}) collective-permute-start(bf16[512,1024]{1,0:T(8,128)(2,1)} %collective-permute-done.3), channel_id=1, source_target_pairs={{0,24},{8,0},{16,8},{24,16},{1,25},{9,1},{17,9},{25,17},{2,26},{10... | collective-permute-start | bytes 3145736 | tf_op jit(solution)/shard_map/ppermute | solution.py:199
  86.7 2.5 %fusion.2 = f32[1024,1024]{1,0:T(8,128)S(1)} fusion(bf16[512,1024]{1,0:T(8,128)(2,1)} %collective-permute-done.1, s32[512]{0:T(512)S(1)} %get-tuple-element.25), kind=kOutput, calls=%fused_computation.10 | convolution fusion | flops 1074266112 | bytes 5244928 | tf_op jit(solution)/shard_map/dot_general | solution.py:233
  89.2 2.5 %fusion.3 = f32[1024,1024]{1,0:T(8,128)S(1)} fusion(bf16[512,1024]{1,0:T(8,128)(2,1)} %collective-permute-done.3, s32[512]{0:T(512)S(1)} %get-tuple-element.27), kind=kOutput, calls=%fused_computation.11 | convolution fusion | flops 1074266112 | bytes 5244928 | tf_op jit(solution)/shard_map/dot_general | solution.py:233
  92.9 4.5 %fusion.5 = f32[1024,1024]{1,0:T(8,128)} fusion(bf16[512,1024]{1,0:T(8,128)(2,1)} %collective-permute-done.5, s32[512]{0:T(512)S(1)} %get-tuple-element.28), kind=kOutput, calls=%fused_computation.13 | convolution fusion | flops 1074266112 | bytes 5244928 | tf_op jit(solution)/shard_map/dot_general | solution.py:233
  97.4 11.8 %collective-permute-done.7 = bf16[512,1024]{1,0:T(8,128)(2,1)S(1)} collective-permute-done((bf16[512,1024]{1,0:T(8,128)(2,1)}, bf16[512,1024]{1,0:T(8,128)(2,1)S(1)}, u32[]{:S(2)}, u32[]{:S(2)}) %collective-permute-start.7) | collective-permute-done | bytes 1048608 | tf_op jit(solution)/shard_map/ppermute | solution.py:199
  109.2 3.3 %fusion.6 = f32[1024,1024]{1,0:T(8,128)} fusion(bf16[512,1024]{1,0:T(8,128)(2,1)S(1)} %collective-permute-done.7, s32[512]{0:T(512)S(1)} %get-tuple-element.24), kind=kOutput, calls=%fused_computation.14 | convolution fusion | flops 1074266112 | bytes 5244928 | tf_op jit(solution)/shard_map/dot_general | solution.py:233
  112.5 6.0 %add_add_fusion = f32[1024,1024]{1,0:T(8,128)S(1)} fusion(f32[1024,1024]{1,0:T(8,128)} %fusion.6, f32[1024,1024]{1,0:T(8,128)} %fusion.5, f32[1024,1024]{1,0:T(8,128)S(1)} %fusion.4, f32[1024,1024]{1,0:T(8,128)S(1)} %fusion.3, f32[1024,1024]{1,0:T(8,128)S(1)} %copy-done.1, f32[1024,1024]{1,0:T(8,128)S(1)} %fusion.2, ...), kind=kOutput, calls=%fused_computation | convolution fusion | flops 1080557568 | bytes 30410752 | tf_op jit(solution)/shard_map/dot_general | solution.py:233
  120.9 2.9 %collective-permute-done.13 = bf16[64,1024]{1,0:T(8,128)(2,1)S(1)} collective-permute-done((bf16[64,1024]{1,0:T(8,128)(2,1)S(1)}, bf16[64,1024]{1,0:T(8,128)(2,1)S(1)}, u32[]{:S(2)}, u32[]{:S(2)}) %collective-permute-start.13) | collective-permute-done | bytes 131104 | tf_op jit(solution)/shard_map/ppermute | solution.py:199
  123.9 2.3 %collective-permute-done.9 = bf16[64,1024]{1,0:T(8,128)(2,1)S(1)} collective-permute-done((bf16[64,1024]{1,0:T(8,128)(2,1)S(1)}, bf16[64,1024]{1,0:T(8,128)(2,1)S(1)}, u32[]{:S(2)}, u32[]{:S(2)}) %collective-permute-start.9) | collective-permute-done | bytes 131104 | tf_op jit(solution)/shard_map/ppermute | solution.py:199
  126.6 1.9 %collective-permute-start.10 = (bf16[128,1024]{1,0:T(8,128)(2,1)S(1)}, bf16[128,1024]{1,0:T(8,128)(2,1)S(1)}, u32[]{:S(2)}, u32[]{:S(2)}) collective-permute-start(bf16[128,1024]{1,0:T(8,128)(2,1)S(1)} %pad_maximum_fusion.1), channel_id=1, source_target_pairs={{0,32},{32,64},{64,96},{96,128},{128,160},{160,192},{192,224},{224... | collective-permute-start | bytes 786440 | tf_op jit(solution)/shard_map/ppermute | solution.py:199
  128.5 5.7 %collective-permute-done.14 = bf16[128,1024]{1,0:T(8,128)(2,1)S(1)} collective-permute-done((bf16[128,1024]{1,0:T(8,128)(2,1)S(1)}, bf16[128,1024]{1,0:T(8,128)(2,1)S(1)}, u32[]{:S(2)}, u32[]{:S(2)}) %collective-permute-start.14) | collective-permute-done | bytes 262176 | tf_op jit(solution)/shard_map/ppermute | solution.py:199
  134.5 7.9 %collective-permute-done.15 = bf16[128,1024]{1,0:T(8,128)(2,1)S(1)} collective-permute-done((bf16[128,1024]{1,0:T(8,128)(2,1)S(1)}, bf16[128,1024]{1,0:T(8,128)(2,1)S(1)}, u32[]{:S(2)}, u32[]{:S(2)}) %collective-permute-start.15) | collective-permute-done | bytes 262176 | tf_op jit(solution)/shard_map/ppermute | solution.py:199
  143.4 3.2 %collective-permute-start.16 = (bf16[128,1024]{1,0:T(8,128)(2,1)S(1)}, bf16[128,1024]{1,0:T(8,128)(2,1)S(1)}, u32[]{:S(2)}, u32[]{:S(2)}) collective-permute-start(bf16[128,1024]{1,0:T(8,128)(2,1)S(1)} %get-tuple-element.12), channel_id=1, source_target_pairs={{0,224},{32,0},{64,32},{96,64},{128,96},{160,128},{192,160},{224,1... | collective-permute-start | bytes 786440 | tf_op jit(solution)/shard_map/ppermute | solution.py:199
  146.7 5.7 %collective-permute-done.11 = bf16[128,1024]{1,0:T(8,128)(2,1)S(1)} collective-permute-done((bf16[128,1024]{1,0:T(8,128)(2,1)S(1)}, bf16[128,1024]{1,0:T(8,128)(2,1)S(1)}, u32[]{:S(2)}, u32[]{:S(2)}) %collective-permute-start.11) | collective-permute-done | bytes 262176 | tf_op jit(solution)/shard_map/ppermute | solution.py:199
  153.3 5.4 %fields.1 = f32[2,2,1,8,8192]{4,3,2,1,0:T(8,128)} custom-call(f32[12,8,32]{2,1,0:T(8,128)} %bitcast.31, s32[1,32]{1,0:T(1,128)} %bitcast.37, f32[64,1024]{1,0:T(8,128)} %pad_maximum_fusion.wave_ref), custom_call_target="tpu_custom_call" | custom-call | tf_op jit(solution)/shard_map/fields/pallas_call | solution.py:187
  158.7 1.4 collective-permute-done.12.up_ref
  160.8 2.0 %maps.1 = f32[2,1,8,8192]{3,2,1,0:T(8,128)} custom-call(f32[128,1024]{1,0:T(8,128)} %get-tuple-element.14.own_ref, bf16[128,1024]{1,0:T(8,128)(2,1)} %copy-done.4, bf16[128,1024]{1,0:T(8,128)(2,1)} %copy-done.3), custom_call_target="tpu_custom_call" | custom-call | tf_op jit(solution)/shard_map/maps/pallas_call | solution.py:288
  (58 shorter events, 19.5 us)
Async XLA Ops:
  0.6 25.0 %copy-start = (bf16[1,1024,1024]{2,1,0:T(8,128)(2,1)S(1)}, bf16[1,1024,1024]{2,1,0:T(8,128)(2,1)}, u32[]{:S(2)}) copy-start(bf16[1,1024,1024]{2,1,0:T(8,128)(2,1)} %param.7) | copy-start | bytes 6291460
  2.3 41.0 %collective-permute-start.6 = (s32[1024]{0:T(1024)S(1)}, s32[1024]{0:T(1024)S(1)}, u32[]{:S(2)}, u32[]{:S(2)}) collective-permute-start(s32[1024]{0:T(1024)S(1)} %add.198), channel_id=1, source_target_pairs={{0,16},{8,24},{16,0},{24,8},{1,17},{9,25},{17,1},{25,9},{2,18},{10... | collective-permute-start | bytes 12296 | tf_op jit(solution)/shard_map/ppermute | solution.py:199
  5.6 52.4 %collective-permute-start = (s32[1024]{0:T(1024)S(1)}, s32[1024]{0:T(1024)S(1)}, u32[]{:S(2)}, u32[]{:S(2)}) collective-permute-start(s32[1024]{0:T(1024)S(1)} %add.198), channel_id=1, source_target_pairs={{0,8},{8,16},{16,24},{24,0},{1,9},{9,17},{17,25},{25,1},{2,10},{10... | collective-permute-start | bytes 12296 | tf_op jit(solution)/shard_map/ppermute | solution.py:199
  6.3 64.0 %collective-permute-start.2 = (s32[1024]{0:T(1024)S(1)}, s32[1024]{0:T(1024)S(1)}, u32[]{:S(2)}, u32[]{:S(2)}) collective-permute-start(s32[1024]{0:T(1024)S(1)} %add.198), channel_id=1, source_target_pairs={{0,24},{8,0},{16,8},{24,16},{1,25},{9,1},{17,9},{25,17},{2,26},{10... | collective-permute-start | bytes 12296 | tf_op jit(solution)/shard_map/ppermute | solution.py:199
  16.8 19.5 %all-to-all-start = ((f32[32,8,128]{2,1,0:T(8,128)}), f32[32,8,128]{2,1,0:T(8,128)S(1)}, u32[]{:S(2)}, u32[]{:S(2)}) async-start(f32[32,8,128]{2,1,0:T(8,128)} %modes.1), calls=%async_computation | async-start | bytes 262144 | tf_op jit(solution)/shard_map/all_to_all | solution.py:306
  26.8 56.7 %collective-permute-start.1 = (bf16[512,1024]{1,0:T(8,128)(2,1)S(1)}, bf16[512,1024]{1,0:T(8,128)(2,1)}, u32[]{:S(2)}, u32[]{:S(2)}) collective-permute-start(bf16[512,1024]{1,0:T(8,128)(2,1)S(1)} %get-tuple-element.22), channel_id=1, source_target_pairs={{0,8},{8,16},{16,24},{24,0},{1,9},{9,17},{17,25},{25,1},{2,10},{10... | collective-permute-start | bytes 3145736 | tf_op jit(solution)/shard_map/ppermute | solution.py:199
  28.6 55.3 %collective-permute-start.3 = (bf16[512,1024]{1,0:T(8,128)(2,1)}, bf16[512,1024]{1,0:T(8,128)(2,1)}, u32[]{:S(2)}, u32[]{:S(2)}) collective-permute-start(bf16[512,1024]{1,0:T(8,128)(2,1)} %get-tuple-element.21), channel_id=1, source_target_pairs={{0,24},{8,0},{16,8},{24,16},{1,25},{9,1},{17,9},{25,17},{2,26},{10... | collective-permute-start | bytes 3145736 | tf_op jit(solution)/shard_map/ppermute | solution.py:199
  36.3 0.6 copy-start.2
  38.5 8.7 %all-to-all-start.1 = ((bf16[8,8,128]{2,1,0:T(8,128)(2,1)}), bf16[8,8,128]{2,1,0:T(8,128)(2,1)S(1)}, u32[]{:S(2)}, u32[]{:S(2)}) async-start(bf16[8,8,128]{2,1,0:T(8,128)(2,1)} %harmonics.1), calls=%async_computation.1 | async-start | bytes 32768 | tf_op jit(solution)/shard_map/all_to_all | solution.py:309
  43.3 48.4 %collective-permute-start.4 = (bf16[512,1024]{1,0:T(8,128)(2,1)}, bf16[512,1024]{1,0:T(8,128)(2,1)S(1)}, u32[]{:S(2)}, u32[]{:S(2)}) collective-permute-start(bf16[512,1024]{1,0:T(8,128)(2,1)} %get-tuple-element.21), channel_id=1, source_target_pairs={{0,8},{8,16},{16,24},{24,0},{1,9},{9,17},{17,25},{25,1},{2,10},{10... | collective-permute-start | bytes 3145736 | tf_op jit(solution)/shard_map/ppermute | solution.py:199
  47.2 0.6 copy-start.5
  53.2 9.4 %all-to-all-start.2 = ((f32[8,12,256]{2,1,0:T(8,128)}), f32[8,12,256]{2,1,0:T(8,128)S(1)}, u32[]{:S(2)}, u32[]{:S(2)}) async-start(f32[8,12,256]{2,1,0:T(8,128)} %legendre.1), calls=%async_computation.2 | async-start | bytes 262144 | tf_op jit(solution)/shard_map/all_to_all | solution.py:312
  58.0 34.9 %collective-permute-start.5 = (bf16[512,1024]{1,0:T(8,128)(2,1)S(1)}, bf16[512,1024]{1,0:T(8,128)(2,1)}, u32[]{:S(2)}, u32[]{:S(2)}) collective-permute-start(bf16[512,1024]{1,0:T(8,128)(2,1)S(1)} %get-tuple-element.22), channel_id=1, source_target_pairs={{0,24},{8,0},{16,8},{24,16},{1,25},{9,1},{17,9},{25,17},{2,26},{10... | collective-permute-start | bytes 3145736 | tf_op jit(solution)/shard_map/ppermute | solution.py:199
  63.6 19.8 %all-to-all-start.3 = ((bf16[32,1,96]{2,1,0:T(2,128)(2,1)}), bf16[32,1,96]{2,1,0:T(2,128)(2,1)S(1)}, u32[]{:S(2)}, u32[]{:S(2)}) async-start(bf16[32,1,96]{2,1,0:T(2,128)(2,1)} %copy.19), calls=%async_computation.3 | async-start | bytes 32768 | tf_op jit(solution)/shard_map/all_to_all | solution.py:315
  83.5 25.8 %collective-permute-start.7 = (bf16[512,1024]{1,0:T(8,128)(2,1)}, bf16[512,1024]{1,0:T(8,128)(2,1)S(1)}, u32[]{:S(2)}, u32[]{:S(2)}) collective-permute-start(bf16[512,1024]{1,0:T(8,128)(2,1)} %collective-permute-done.1), channel_id=1, source_target_pairs={{0,8},{8,16},{16,24},{24,0},{1,9},{9,17},{17,25},{25,1},{2,10},{10... | collective-permute-start | bytes 3145736 | tf_op jit(solution)/shard_map/ppermute | solution.py:199
  83.9 28.6 %collective-permute-start.8 = (bf16[512,1024]{1,0:T(8,128)(2,1)}, bf16[512,1024]{1,0:T(8,128)(2,1)S(1)}, u32[]{:S(2)}, u32[]{:S(2)}) collective-permute-start(bf16[512,1024]{1,0:T(8,128)(2,1)} %collective-permute-done.3), channel_id=1, source_target_pairs={{0,24},{8,0},{16,8},{24,16},{1,25},{9,1},{17,9},{25,17},{2,26},{10... | collective-permute-start | bytes 3145736 | tf_op jit(solution)/shard_map/ppermute | solution.py:199
  109.2 3.3 %copy-start.1 = (f32[1024,1024]{1,0:T(8,128)S(1)}, f32[1024,1024]{1,0:T(8,128)}, u32[]{:S(2)}) copy-start(f32[1024,1024]{1,0:T(8,128)} %fusion) | copy-start | bytes 12582916
  118.8 5.0 %collective-permute-start.13 = (bf16[64,1024]{1,0:T(8,128)(2,1)S(1)}, bf16[64,1024]{1,0:T(8,128)(2,1)S(1)}, u32[]{:S(2)}, u32[]{:S(2)}) collective-permute-start(bf16[64,1024]{1,0:T(8,128)(2,1)S(1)} %get-tuple-element.18), channel_id=1, source_target_pairs={{0,224},{32,0},{64,32},{96,64},{128,96},{160,128},{192,160},{224,1... | collective-permute-start | bytes 393224 | tf_op jit(solution)/shard_map/ppermute | solution.py:199
  120.0 6.2 %collective-permute-start.9 = (bf16[64,1024]{1,0:T(8,128)(2,1)S(1)}, bf16[64,1024]{1,0:T(8,128)(2,1)S(1)}, u32[]{:S(2)}, u32[]{:S(2)}) collective-permute-start(bf16[64,1024]{1,0:T(8,128)(2,1)S(1)} %get-tuple-element.20), channel_id=1, source_target_pairs={{0,32},{32,64},{64,96},{96,128},{128,160},{160,192},{192,224},{224... | collective-permute-start | bytes 393224 | tf_op jit(solution)/shard_map/ppermute | solution.py:199
  126.3 7.9 %collective-permute-start.14 = (bf16[128,1024]{1,0:T(8,128)(2,1)S(1)}, bf16[128,1024]{1,0:T(8,128)(2,1)S(1)}, u32[]{:S(2)}, u32[]{:S(2)}) collective-permute-start(bf16[128,1024]{1,0:T(8,128)(2,1)S(1)} %pad_maximum_fusion.2), channel_id=1, source_target_pairs={{0,224},{32,0},{64,32},{96,64},{128,96},{160,128},{192,160},{224,1... | collective-permute-start | bytes 786440 | tf_op jit(solution)/shard_map/ppermute | solution.py:199
  126.6 7.9 %collective-permute-start.10 = (bf16[128,1024]{1,0:T(8,128)(2,1)S(1)}, bf16[128,1024]{1,0:T(8,128)(2,1)S(1)}, u32[]{:S(2)}, u32[]{:S(2)}) collective-permute-start(bf16[128,1024]{1,0:T(8,128)(2,1)S(1)} %pad_maximum_fusion.1), channel_id=1, source_target_pairs={{0,32},{32,64},{64,96},{96,128},{128,160},{160,192},{192,224},{224... | collective-permute-start | bytes 786440 | tf_op jit(solution)/shard_map/ppermute | solution.py:199
  134.3 8.2 %collective-permute-start.15 = (bf16[128,1024]{1,0:T(8,128)(2,1)S(1)}, bf16[128,1024]{1,0:T(8,128)(2,1)S(1)}, u32[]{:S(2)}, u32[]{:S(2)}) collective-permute-start(bf16[128,1024]{1,0:T(8,128)(2,1)S(1)} %add_convert_fusion.1), channel_id=1, source_target_pairs={{0,224},{32,0},{64,32},{96,64},{128,96},{160,128},{192,160},{224,1... | collective-permute-start | bytes 786440 | tf_op jit(solution)/shard_map/ppermute | solution.py:199
  143.4 9.0 %collective-permute-start.11 = (bf16[128,1024]{1,0:T(8,128)(2,1)S(1)}, bf16[128,1024]{1,0:T(8,128)(2,1)S(1)}, u32[]{:S(2)}, u32[]{:S(2)}) collective-permute-start(bf16[128,1024]{1,0:T(8,128)(2,1)S(1)} %get-tuple-element.13), channel_id=1, source_target_pairs={{0,32},{32,64},{64,96},{96,128},{128,160},{160,192},{192,224},{224... | collective-permute-start | bytes 786440 | tf_op jit(solution)/shard_map/ppermute | solution.py:199
  143.4 15.3 %collective-permute-start.16 = (bf16[128,1024]{1,0:T(8,128)(2,1)S(1)}, bf16[128,1024]{1,0:T(8,128)(2,1)S(1)}, u32[]{:S(2)}, u32[]{:S(2)}) collective-permute-start(bf16[128,1024]{1,0:T(8,128)(2,1)S(1)} %get-tuple-element.12), channel_id=1, source_target_pairs={{0,224},{32,0},{64,32},{96,64},{128,96},{160,128},{192,160},{224,1... | collective-permute-start | bytes 786440 | tf_op jit(solution)/shard_map/ppermute | solution.py:199
  152.5 7.7 %collective-permute-start.12 = (bf16[128,1024]{1,0:T(8,128)(2,1)S(1)}, bf16[128,1024]{1,0:T(8,128)(2,1)S(1)}, u32[]{:S(2)}, u32[]{:S(2)}) collective-permute-start(bf16[128,1024]{1,0:T(8,128)(2,1)S(1)} %add_convert_fusion.2), channel_id=1, source_target_pairs={{0,32},{32,64},{64,96},{96,128},{128,160},{160,192},{192,224},{224... | collective-permute-start | bytes 786440 | tf_op jit(solution)/shard_map/ppermute | solution.py:199
  158.7 1.5 copy-start.3
  160.1 0.7 copy-start.4
where the time goes:
time: 164 us; the launch traced here: 163 us
  waiting for transfers between devices  59.8 us (36%)
  starting transfers between devices  47.5 us (29%)
  matrix products  24.2 us (15%)
  Pallas kernels  19.1 us (12%)
  local copies, waits for them, and re-layouts  6.13 us (4%)
  other arithmetic  5.26 us (3%)
    ppermute x17, waiting for transfers between devices, shifted(): return lax.ppermute(x, axis, [(i, (i + by) % size) for i in range(size)])  37.9 us
    dot_general x7, matrix products, picked(): jnp.dot(pick.astype(jnp.bfloat16), rows, preferred_element_type=jnp.float32)  24.2 us
    ppermute x17, starting transfers between devices, shifted(): return lax.ppermute(x, axis, [(i, (i + by) % size) for i in range(size)])  22.4 us
    all_to_all x1, waiting for transfers between devices, body(): lax.all_to_all(summed, BLK, split_axis=0, concat_axis=0, tiled=True)  13.1 us
    all_to_all x1, starting transfers between devices, body(): arrived = lax.all_to_all(sums, BLK, split_axis=0, concat_axis=0, tiled=True)  8.86 us
    all_to_all x1, starting transfers between devices, body(): lax.all_to_all(summed, BLK, split_axis=0, concat_axis=0, tiled=True)  6.62 us
    pallas_call x1, Pallas kernels, legendre_pair(): pl.pallas_call(legendre_kernel, out_shape=jax.ShapeDtypeStruct((blocks, 1...  5.43 us
    pallas_call x1, Pallas kernels, eigenvalues(): pl.pallas_call(functools.partial(fields_kernel, 2.0 / math.sqrt(orders)),...  5.4 us
  transfers between devices with their start and end apart: 21, of which 11 were waited for; matrix products, arithmetic and copies ran while one was open for 15% of the time, Pallas kernels for 10%

commit v1 on v0

--- a/solution.py
+++ b/solution.py
@@ -199,7 +199,7 @@
     return lax.ppermute(x, axis, [(i, (i + by) % size) for i in range(size)])
 
 
-def ring_sums(chunk, axis):
+def ring_sums(chunk, axis, token):
     size = lax.axis_size(axis)
     middle = size // 2
     half = chunk(middle).shape[0] // 2
@@ -213,6 +213,7 @@
                 return moving
             own = chunk(distance if by == 1 else size - distance)
             if distance == middle - 1:
+                own = after(own, token)
                 if first:
                     moving = jnp.concatenate([own[:half] + moving, own[half:]], axis=0)
                 else:
@@ -223,30 +224,73 @@
     return chunk(0), toward(1, True), toward(-1, False)
 
 
-def row_slots(owners, keys):
-    place = (keys & 64) + (keys & 7) * R_DEV + ((keys >> 3) & 7)
-    return owners * KEYS + place
-
-
-def picked(slots, base, count, rows):
-    pick = lax.broadcasted_iota(jnp.int32, (count, slots.shape[0]), 0) == (slots - base)[None, :]
-    return jnp.dot(pick.astype(jnp.bfloat16), rows, preferred_element_type=jnp.float32)
-
-
 def after(x, token):
     return lax.optimization_barrier((x, token))[0]
 
 
+DIGIT = 64
+EXTRA = 16
+
+
+def pack_kernel(rows_ref, owner_ref, key_ref, *out_refs):
+    size = rows_ref.shape[0] // len(out_refs)
+    key = key_ref[...]
+    place = (key & 64) + (key & 7) * R_DEV + ((key >> 3) & 7)
+    slot = owner_ref[...] * KEYS + place
+    for part, out_ref in enumerate(out_refs):
+        own = slot[:, part * size : (part + 1) * size]
+        row = lax.broadcasted_iota(jnp.int32, (EXTRA, size), 0)
+        tail = jnp.where(row == 0, own // DIGIT, jnp.where(row == 1, own % DIGIT, 0))
+        out_ref[:size] = rows_ref[part * size : (part + 1) * size]
+        out_ref[size:] = jnp.zeros((EXTRA, rows_ref.shape[1]), out_ref.dtype)
+        out_ref[size:, :size] = tail.astype(jnp.float32).astype(out_ref.dtype)
+
+
+def row_pieces(rows, owners, keys, parts):
+    piece = jax.ShapeDtypeStruct((rows.shape[0] // parts + EXTRA, rows.shape[1]), rows.dtype)
+    return pl.pallas_call(pack_kernel, out_shape=(piece,) * parts, name="pack")(
+        rows, owners[None], keys[None]
+    )
+
+
+def sums_kernel(count, has_base, columns, rings, place_ref, *refs):
+    pieces, out_ref = refs[:count], refs[-1]
+    my_z, my_y = place_ref[0], place_ref[1]
+    slots = out_ref.shape[0]
+    for index, piece in enumerate(pieces):
+        size = piece.shape[0] - EXTRA
+        tail = piece[size : size + EXTRA, :size].astype(jnp.float32).astype(jnp.int32)
+        slot = tail[0:1] * DIGIT + tail[1:2]
+        owner = slot // KEYS
+        distance = (owner // columns - my_z) & (rings - 1)
+        mine = jnp.where((owner & (columns - 1)) == my_y, distance * KEYS + (slot & (KEYS - 1)), -1)
+        pick = lax.broadcasted_iota(jnp.int32, (slots, size), 0) == mine
+        pick = jnp.where(pick, 1.0, 0.0).astype(jnp.bfloat16)
+        add = dot32(pick, piece[:size], NN)
+        if index == 0:
+            out_ref[...] = refs[count][...] + add if has_base else add
+        else:
+            out_ref[...] += add
+
+
+def sum_pieces(pieces, base, place):
+    columns, rings = lax.axis_size(BLK[1]), lax.axis_size(BLK[0])
+    smem = pl.BlockSpec(memory_space=pltpu.SMEM)
+    vmem = pl.BlockSpec(memory_space=pltpu.VMEM)
+    operands = list(pieces) + ([] if base is None else [base])
+    return pl.pallas_call(
+        functools.partial(sums_kernel, len(pieces), base is not None, columns, rings),
+        out_shape=jax.ShapeDtypeStruct((rings * KEYS, pieces[0].shape[1]), jnp.float32),
+        in_specs=[smem] + [vmem] * len(operands),
+        out_specs=vmem,
+    )(place, *operands)
+
+
 class ColumnSums:
     def __init__(self, rows, owners, keys):
-        self.slots = row_slots(owners, keys)
-        self.rows = rows
-        half = PR // 2
         axis = BLK[1]
-        self.up_slots = shifted(self.slots, axis, 1)
-        self.down_slots = shifted(self.slots, axis, -1)
-        self.far_slots = shifted(self.slots, axis, 2)
-        first, last = rows[:half], rows[half:]
+        self.place = jnp.stack([lax.axis_index(BLK[0]), lax.axis_index(BLK[1])]).astype(jnp.int32)
+        self.pieces = first, last = row_pieces(rows, owners, keys, 2)
         self.up = [shifted(first, axis, 1), shifted(last, axis, 1)]
         self.down = [shifted(last, axis, -1), shifted(first, axis, -1)]
 
@@ -254,26 +298,11 @@
         self.up_far = shifted(after(self.up[0], token), BLK[1], 1)
         self.down_far = shifted(after(self.down[0], token), BLK[1], -1)
 
-    def column_sums(self, slot, values):
-        ny, nz = lax.axis_size(BLK[1]), lax.axis_size(BLK[0])
-        my_y, my_z = lax.axis_index(BLK[1]), lax.axis_index(BLK[0])
-        owner, place = slot // KEYS, slot % KEYS
-        distance = (owner // ny - my_z) % nz
-        mine = jnp.where(owner % ny == my_y, distance * KEYS + place, -1)
-        return picked(mine, 0, nz * KEYS, values)
-
     def finish(self, token):
-        half = PR // 2
-        up, down, far = self.up_slots, self.down_slots, self.far_slots
-        near = self.column_sums(self.slots, self.rows)
-        near = near + self.column_sums(up[:half], self.up[0])
-        near = near + self.column_sums(down[half:], self.down[0])
-        near = near + self.column_sums(up[half:], self.up[1])
-        near = near + self.column_sums(down[:half], self.down[1])
-        sums = near + self.column_sums(far[:half], self.up_far)
-        sums = sums + self.column_sums(far[half:], self.down_far)
-        sums = after(sums, token)
-        return ring_sums(lambda d: sums[d * KEYS : (d + 1) * KEYS], BLK[0])
+        sums = sum_pieces(self.pieces, None, self.place)
+        sums = sum_pieces(self.up + self.down, sums, self.place)
+        sums = sum_pieces([self.up_far, self.down_far], sums, self.place)
+        return ring_sums(lambda d: sums[d * KEYS : (d + 1) * KEYS], BLK[0], token)
 
 
 def maps_kernel(own_ref, up_ref, down_ref, out_ref):

time: 164 us -> 150 us (0.915)
  Pallas kernels: 19.1 us -> 45.3 us
  waiting for transfers between devices: 59.8 us -> 35.1 us
  matrix products: 24.2 us -> 0 us
  starting transfers between devices: 47.5 us -> 53 us
  other arithmetic: 5.26 us -> 10.2 us
    pallas_call x0 -> x4, Pallas kernels: none -> 26.2 us  [the longest x3 23.2 us: sum_pieces(): pl.pallas_call(functools.partial(sums_kernel, len(pieces), base is not No...]
    dot_general x7 -> x0, matrix products: 24.2 us -> none  [picked(): jnp.dot(pick.astype(jnp.bfloat16), rows, preferred_element_type=jnp.float32)]
    ppermute x17 -> x14, waiting for transfers between devices: 37.9 us -> 23.9 us  [shifted(): return lax.ppermute(x, axis, [(i, (i + by) % size) for i in range(size)])]
    all_to_all x1, waiting for transfers between devices: 13.1 us -> 0.01 us  [body(): lax.all_to_all(summed, BLK, split_axis=0, concat_axis=0, tiled=True)]
    all_to_all x1, waiting for transfers between devices: 1.94 us -> 7.3 us  [body(): arrived = lax.all_to_all(sums, BLK, split_axis=0, concat_axis=0, tiled=True)]
    convert_element_type x3 -> x4, other arithmetic: 1.12 us -> 5.63 us  [toward(): moving = shifted(moving.astype(jnp.bfloat16), axis, by).astype(jnp.float32)]
    all_to_all x1, waiting for transfers between devices: 3.25 us -> 0.01 us  [body(): lax.all_to_all(pieces, 'lblk', split_axis=0, concat_axis=0, tiled=True)]
    another operation x2 -> x4, other arithmetic: 0.38 us -> 3.19 us
  transfers between devices with their start and end apart: 21 -> 18, of which waited for: 11 -> 8; matrix products, arithmetic and copies ran while one was open for 15% -> 8% of each run, Pallas kernels for 10% -> 27%
where the time goes in v1:
time: 150 us; the launch traced here: 149 us
  starting transfers between devices  53 us (35%)
  Pallas kernels  45.3 us (30%)
  waiting for transfers between devices  35.1 us (23%)
  other arithmetic  10.2 us (7%)
  local copies, waits for them, and re-layouts  4.82 us (3%)
    ppermute x14, waiting for transfers between devices, shifted(): return lax.ppermute(x, axis, [(i, (i + by) % size) for i in range(size)])  23.9 us
    ppermute x14, starting transfers between devices, shifted(): return lax.ppermute(x, axis, [(i, (i + by) % size) for i in range(size)])  23.8 us
    pallas_call x3, Pallas kernels, sum_pieces(): pl.pallas_call(functools.partial(sums_kernel, len(pieces), base is not No...  23.2 us
    all_to_all x1, starting transfers between devices, body(): arrived = lax.all_to_all(sums, BLK, split_axis=0, concat_axis=0, tiled=True)  10.3 us
    all_to_all x1, starting transfers between devices, body(): lax.all_to_all(summed, BLK, split_axis=0, concat_axis=0, tiled=True)  9.28 us
    all_to_all x1, waiting for transfers between devices, body(): arrived = lax.all_to_all(sums, BLK, split_axis=0, concat_axis=0, tiled=True)  7.3 us
    convert_element_type x4, other arithmetic, toward(): moving = shifted(moving.astype(jnp.bfloat16), axis, by).astype(jnp.float32)  5.63 us
    pallas_call x1, Pallas kernels, legendre_pair(): pl.pallas_call(legendre_kernel, out_shape=jax.ShapeDtypeStruct((blocks, 1...  5.43 us
  transfers between devices with their start and end apart: 18, of which 8 were waited for; matrix products, arithmetic and copies ran while one was open for 8% of the time, Pallas kernels for 27%

profile of v1, /device:TPU:2, one launch (start us, length us, event | category | flops | bytes accessed | tf_op | source)
XLA Modules:
  0.0 149.3 jit_solution(14388691818110583847)
XLA Ops:
  0.6 3.1 %pack.1 = (bf16[528,1024]{1,0:T(8,128)(2,1)}, bf16[528,1024]{1,0:T(8,128)(2,1)}) custom-call(bf16[1024,1024]{1,0:T(8,128)(2,1)} %bitcast.15, s32[1,1024]{1,0:T(1,128)} %bitcast.20, s32[1,1024]{1,0:T(1,128)} %key_ref.3), custom_call_target="tpu_custom_call" | custom-call | tf_op jit(solution)/shard_map/pack/pallas_call | solution.py:251
  3.7 1.6 %collective-permute-start = (bf16[528,1024]{1,0:T(8,128)(2,1)}, bf16[528,1024]{1,0:T(8,128)(2,1)S(1)}, u32[]{:S(2)}, u32[]{:S(2)}) collective-permute-start(bf16[528,1024]{1,0:T(8,128)(2,1)} %get-tuple-element.8.refs_0_), channel_id=1, source_target_pairs={{0,8},{8,16},{16,24},{24,0},{1,9},{9,17},{17,25},{25,1},{2,10},{10... | collective-permute-start | bytes 3244040 | tf_op jit(solution)/shard_map/ppermute | solution.py:199
  5.3 1.7 %collective-permute-start.2 = (bf16[528,1024]{1,0:T(8,128)(2,1)}, bf16[528,1024]{1,0:T(8,128)(2,1)S(1)}, u32[]{:S(2)}, u32[]{:S(2)}) collective-permute-start(bf16[528,1024]{1,0:T(8,128)(2,1)} %get-tuple-element.10.refs_1_), channel_id=1, source_target_pairs={{0,24},{8,0},{16,8},{24,16},{1,25},{9,1},{17,9},{25,17},{2,26},{10... | collective-permute-start | bytes 3244040 | tf_op jit(solution)/shard_map/ppermute | solution.py:199
  9.0 4.7 %modes.1 = f32[32,8,128]{2,1,0:T(8,128)} custom-call(bf16[1024,1024]{1,0:T(8,128)(2,1)} %bitcast.16, s32[1,1024]{1,0:T(1,128)} %bitcast.21, s32[1,1024]{1,0:T(1,128)} %key_ref.3, s32[32,1]{1,0:T(8,128)} %copy.17.order_ref, f32[64,1024]{1,0:T(8,128)} %pad_maximum_fusion.wave_ref), custom_call_target="tpu_custom_call" | custom-call | tf_op jit(solution)/shard_map/modes/pallas_call | solution.py:81
  13.6 10.3 %all-to-all-start = ((f32[32,8,128]{2,1,0:T(8,128)}), f32[32,8,128]{2,1,0:T(8,128)S(1)}, u32[]{:S(2)}, u32[]{:S(2)}) async-start(f32[32,8,128]{2,1,0:T(8,128)} %modes.1), calls=%async_computation | async-start | bytes 262144 | tf_op jit(solution)/shard_map/all_to_all | solution.py:335
  23.9 1.9 %collective-permute-start.4 = (bf16[528,1024]{1,0:T(8,128)(2,1)}, bf16[528,1024]{1,0:T(8,128)(2,1)}, u32[]{:S(2)}, u32[]{:S(2)}) collective-permute-start(bf16[528,1024]{1,0:T(8,128)(2,1)} %get-tuple-element.10.refs_1_), channel_id=1, source_target_pairs={{0,8},{8,16},{16,24},{24,0},{1,9},{9,17},{17,25},{25,1},{2,10},{10... | collective-permute-start | bytes 3244040 | tf_op jit(solution)/shard_map/ppermute | solution.py:199
  25.8 1.4 collective-permute-start.5
  27.2 7.3 %all-to-all-done.in_ref = f32[32,8,128]{2,1,0:T(8,128)S(1)} async-done(((f32[32,8,128]{2,1,0:T(8,128)}), f32[32,8,128]{2,1,0:T(8,128)S(1)}, u32[]{:S(2)}, u32[]{:S(2)}) %all-to-all-start) | async-done | bytes 131104 | tf_op jit(solution)/shard_map/all_to_all | solution.py:335
  35.9 1.9 %collective-permute-start.3 = (bf16[528,1024]{1,0:T(8,128)(2,1)S(1)}, bf16[528,1024]{1,0:T(8,128)(2,1)}, u32[]{:S(2)}, u32[]{:S(2)}) collective-permute-start(bf16[528,1024]{1,0:T(8,128)(2,1)S(1)} %collective-permute-done.2.refs_2_), channel_id=1, source_target_pairs={{0,24},{8,0},{16,8},{24,16},{1,25},{9,1},{17,9},{25,17},{2,26},{10... | collective-permute-start | bytes 3244040 | tf_op jit(solution)/shard_map/ppermute | solution.py:199
  37.8 1.5 %harmonics.1 = bf16[8,8,128]{2,1,0:T(8,128)(2,1)} custom-call(f32[32,8,128]{2,1,0:T(8,128)} %copy-done.3), custom_call_target="tpu_custom_call" | custom-call | tf_op jit(solution)/shard_map/harmonics/pallas_call | solution.py:96
  39.4 4.8 %all-to-all-start.1 = ((bf16[8,8,128]{2,1,0:T(8,128)(2,1)}), bf16[8,8,128]{2,1,0:T(8,128)(2,1)S(1)}, u32[]{:S(2)}, u32[]{:S(2)}) async-start(bf16[8,8,128]{2,1,0:T(8,128)(2,1)} %harmonics.1), calls=%async_computation.1 | async-start | bytes 32768 | tf_op jit(solution)/shard_map/all_to_all | solution.py:338
  44.2 3.9 %all-to-all-done.1.modes_ref = bf16[8,8,128]{2,1,0:T(8,128)(2,1)S(1)} async-done(((bf16[8,8,128]{2,1,0:T(8,128)(2,1)}), bf16[8,8,128]{2,1,0:T(8,128)(2,1)S(1)}, u32[]{:S(2)}, u32[]{:S(2)}) %all-to-all-start.1) | async-done | bytes 16416 | tf_op jit(solution)/shard_map/all_to_all | solution.py:338
  48.7 5.4 %legendre.1 = f32[8,12,256]{2,1,0:T(8,128)} custom-call(s32[1]{0:T(128)} %bitcast.first_ref, bf16[8,8,128]{2,1,0:T(8,128)(2,1)} %copy-done.6, bf16[1,512,2048]{2,1,0:T(8,128)(2,1)} %leg_ref.1, bf16[1,512,2048]{2,1,0:T(8,128)(2,1)} %even_hbm.1, bf16[1,512,2048]{2,1,0:T(8,128)(2,1)} %odd_hbm.1), custom_call_target="tpu_custom_call" | custom-call | tf_op jit(solution)/shard_map/legendre/pallas_call | solution.py:144
  54.2 4.8 %all-to-all-start.2 = ((f32[8,12,256]{2,1,0:T(8,128)}), f32[8,12,256]{2,1,0:T(8,128)S(1)}, u32[]{:S(2)}, u32[]{:S(2)}) async-start(f32[8,12,256]{2,1,0:T(8,128)} %legendre.1), calls=%async_computation.2 | async-start | bytes 262144 | tf_op jit(solution)/shard_map/all_to_all | solution.py:341
  59.6 5.9 %shard_map.86.refs_4_ = f32[1024,1024]{1,0:T(8,128)} custom-call(s32[2]{0:T(128)} %pad_add_fusion.place_ref, bf16[528,1024]{1,0:T(8,128)(2,1)} %get-tuple-element.8.refs_0_, bf16[528,1024]{1,0:T(8,128)(2,1)} %get-tuple-element.10.refs_1_), custom_call_target="tpu_custom_call" | custom-call | tf_op jit(solution)/shard_map/pallas_call | solution.py:281
  66.5 9.3 %all-to-all-start.3 = ((bf16[32,1,96]{2,1,0:T(2,128)(2,1)}), bf16[32,1,96]{2,1,0:T(2,128)(2,1)S(1)}, u32[]{:S(2)}, u32[]{:S(2)}) async-start(bf16[32,1,96]{2,1,0:T(2,128)(2,1)} %copy.19), calls=%async_computation.3 | async-start | bytes 32768 | tf_op jit(solution)/shard_map/all_to_all | solution.py:344
  75.8 10.0 %shard_map.87.refs_2_ = f32[1024,1024]{1,0:T(8,128)} custom-call(s32[2]{0:T(128)} %pad_add_fusion.place_ref, bf16[528,1024]{1,0:T(8,128)(2,1)} %copy-done, bf16[528,1024]{1,0:T(8,128)(2,1)} %collective-permute-done.4.refs_1_, bf16[528,1024]{1,0:T(8,128)(2,1)} %copy-done.1, bf16[528,1024]{1,0:T(8,128)(2,1)} %collective-permute-done.5.refs_3_, ...), custom_call_target="tpu_custom_call" | custom-call | tf_op jit(solution)/shard_map/pallas_call | solution.py:281
  85.8 7.2 %shard_map.88 = f32[1024,1024]{1,0:T(8,128)} custom-call(s32[2]{0:T(128)} %pad_add_fusion.place_ref, bf16[528,1024]{1,0:T(8,128)(2,1)} %collective-permute-done.1.refs_0_, bf16[528,1024]{1,0:T(8,128)(2,1)} %collective-permute-done.3.refs_1_, f32[1024,1024]{1,0:T(8,128)} %shard_map.87.refs_2_), custom_call_target="tpu_custom_call" | custom-call | tf_op jit(solution)/shard_map/pallas_call | solution.py:281
  93.0 2.5 %convert.20 = bf16[1024,1024]{1,0:T(8,128)(2,1)S(1)} convert(f32[1024,1024]{1,0:T(8,128)} %shard_map.88) | non-fusion elementwise | flops 1048576 | bytes 6291456 | tf_op jit(solution)/shard_map/convert.9
  95.6 3.0 %collective-permute-start.10 = (bf16[64,1024]{1,0:T(8,128)(2,1)S(1)}, bf16[64,1024]{1,0:T(8,128)(2,1)S(1)}, u32[]{:S(2)}, u32[]{:S(2)}) collective-permute-start(bf16[64,1024]{1,0:T(8,128)(2,1)S(1)} %get-tuple-element.19), channel_id=1, source_target_pairs={{0,224},{32,0},{64,32},{96,64},{128,96},{160,128},{192,160},{224,1... | collective-permute-start | bytes 393224 | tf_op jit(solution)/shard_map/ppermute | solution.py:199
  99.7 1.4 collective-permute-done.10
  101.1 3.7 %collective-permute-start.11 = (bf16[128,1024]{1,0:T(8,128)(2,1)S(1)}, bf16[128,1024]{1,0:T(8,128)(2,1)S(1)}, u32[]{:S(2)}, u32[]{:S(2)}) collective-permute-start(bf16[128,1024]{1,0:T(8,128)(2,1)S(1)} %pad_maximum_fusion.2), channel_id=1, source_target_pairs={{0,224},{32,0},{64,32},{96,64},{128,96},{160,128},{192,160},{224,1... | collective-permute-start | bytes 786440 | tf_op jit(solution)/shard_map/ppermute | solution.py:199
  104.9 4.1 %collective-permute-done.11 = bf16[128,1024]{1,0:T(8,128)(2,1)S(1)} collective-permute-done((bf16[128,1024]{1,0:T(8,128)(2,1)S(1)}, bf16[128,1024]{1,0:T(8,128)(2,1)S(1)}, u32[]{:S(2)}, u32[]{:S(2)}) %collective-permute-start.11) | collective-permute-done | bytes 262176 | tf_op jit(solution)/shard_map/ppermute | solution.py:199
  110.1 3.8 %collective-permute-start.12 = (bf16[128,1024]{1,0:T(8,128)(2,1)S(1)}, bf16[128,1024]{1,0:T(8,128)(2,1)S(1)}, u32[]{:S(2)}, u32[]{:S(2)}) collective-permute-start(bf16[128,1024]{1,0:T(8,128)(2,1)S(1)} %fusion), channel_id=1, source_target_pairs={{0,224},{32,0},{64,32},{96,64},{128,96},{160,128},{192,160},{224,1... | collective-permute-start | bytes 786440 | tf_op jit(solution)/shard_map/ppermute | solution.py:199
  113.9 3.9 %collective-permute-done.12 = bf16[128,1024]{1,0:T(8,128)(2,1)S(1)} collective-permute-done((bf16[128,1024]{1,0:T(8,128)(2,1)S(1)}, bf16[128,1024]{1,0:T(8,128)(2,1)S(1)}, u32[]{:S(2)}, u32[]{:S(2)}) %collective-permute-start.12) | collective-permute-done | bytes 262176 | tf_op jit(solution)/shard_map/ppermute | solution.py:199
  117.8 2.3 %fusion.1 = (bf16[128,1024]{1,0:T(8,128)(2,1)S(1)}, f32[128,1024]{1,0:T(8,128)S(1)}, f32[128,1024]{1,0:T(8,128)}) fusion(f32[1024,1024]{1,0:T(8,128)} %shard_map.88, bf16[128,1024]{1,0:T(8,128)(2,1)S(1)} %collective-permute-done.12), kind=kLoop, calls=%fused_computation.3 | loop fusion | flops 393216 | bytes 3145728 | tf_op jit(solution)/shard_map/convert_element_type | solution.py:211
  120.3 8.0 %collective-permute-done.7 = bf16[128,1024]{1,0:T(8,128)(2,1)S(1)} collective-permute-done((bf16[128,1024]{1,0:T(8,128)(2,1)S(1)}, bf16[128,1024]{1,0:T(8,128)(2,1)S(1)}, u32[]{:S(2)}, u32[]{:S(2)}) %collective-permute-start.7) | collective-permute-done | bytes 262176 | tf_op jit(solution)/shard_map/ppermute | solution.py:199
  129.5 3.2 %collective-permute-start.13 = (bf16[128,1024]{1,0:T(8,128)(2,1)S(1)}, bf16[128,1024]{1,0:T(8,128)(2,1)S(1)}, u32[]{:S(2)}, u32[]{:S(2)}) collective-permute-start(bf16[128,1024]{1,0:T(8,128)(2,1)S(1)} %get-tuple-element.16), channel_id=1, source_target_pairs={{0,224},{32,0},{64,32},{96,64},{128,96},{160,128},{192,160},{224,1... | collective-permute-start | bytes 786440 | tf_op jit(solution)/shard_map/ppermute | solution.py:199
  132.7 5.0 %collective-permute-done.8 = bf16[128,1024]{1,0:T(8,128)(2,1)S(1)} collective-permute-done((bf16[128,1024]{1,0:T(8,128)(2,1)S(1)}, bf16[128,1024]{1,0:T(8,128)(2,1)S(1)}, u32[]{:S(2)}, u32[]{:S(2)}) %collective-permute-start.8) | collective-permute-done | bytes 262176 | tf_op jit(solution)/shard_map/ppermute | solution.py:199
  139.6 5.4 %fields.1 = f32[2,2,1,8,8192]{4,3,2,1,0:T(8,128)} custom-call(f32[12,8,32]{2,1,0:T(8,128)} %bitcast.18, s32[1,32]{1,0:T(1,128)} %bitcast.22, f32[64,1024]{1,0:T(8,128)} %pad_maximum_fusion.wave_ref), custom_call_target="tpu_custom_call" | custom-call | tf_op jit(solution)/shard_map/fields/pallas_call | solution.py:187
  145.0 1.5 collective-permute-done.9.up_ref
  147.2 2.0 %maps.1 = f32[2,1,8,8192]{3,2,1,0:T(8,128)} custom-call(f32[128,1024]{1,0:T(8,128)} %get-tuple-element.18.own_ref, bf16[128,1024]{1,0:T(8,128)(2,1)} %copy-done.5, bf16[128,1024]{1,0:T(8,128)(2,1)} %copy-done.4), custom_call_target="tpu_custom_call" | custom-call | tf_op jit(solution)/shard_map/maps/pallas_call | solution.py:317
  (52 shorter events, 11.9 us)
Async XLA Ops:
  0.6 6.3 %copy-start.7 = (s32[32]{0:T(128)S(1)}, s32[32]{0:T(128)}, u32[]{:S(2)}) copy-start(s32[32]{0:T(128)} %param.10) | copy-start | bytes 388
  3.7 22.1 %copy-start.2 = (bf16[528,1024]{1,0:T(8,128)(2,1)S(1)}, bf16[528,1024]{1,0:T(8,128)(2,1)}, u32[]{:S(2)}) copy-start(bf16[528,1024]{1,0:T(8,128)(2,1)} %get-tuple-element.8.refs_0_) | copy-start | bytes 3244036
  3.7 30.8 %collective-permute-start = (bf16[528,1024]{1,0:T(8,128)(2,1)}, bf16[528,1024]{1,0:T(8,128)(2,1)S(1)}, u32[]{:S(2)}, u32[]{:S(2)}) collective-permute-start(bf16[528,1024]{1,0:T(8,128)(2,1)} %get-tuple-element.8.refs_0_), channel_id=1, source_target_pairs={{0,8},{8,16},{16,24},{24,0},{1,9},{9,17},{17,25},{25,1},{2,10},{10... | collective-permute-start | bytes 3244040 | tf_op jit(solution)/shard_map/ppermute | solution.py:199
  5.3 30.6 %collective-permute-start.2 = (bf16[528,1024]{1,0:T(8,128)(2,1)}, bf16[528,1024]{1,0:T(8,128)(2,1)S(1)}, u32[]{:S(2)}, u32[]{:S(2)}) collective-permute-start(bf16[528,1024]{1,0:T(8,128)(2,1)} %get-tuple-element.10.refs_1_), channel_id=1, source_target_pairs={{0,24},{8,0},{16,8},{24,16},{1,25},{9,1},{17,9},{25,17},{2,26},{10... | collective-permute-start | bytes 3244040 | tf_op jit(solution)/shard_map/ppermute | solution.py:199
  13.6 20.9 %all-to-all-start = ((f32[32,8,128]{2,1,0:T(8,128)}), f32[32,8,128]{2,1,0:T(8,128)S(1)}, u32[]{:S(2)}, u32[]{:S(2)}) async-start(f32[32,8,128]{2,1,0:T(8,128)} %modes.1), calls=%async_computation | async-start | bytes 262144 | tf_op jit(solution)/shard_map/all_to_all | solution.py:335
  23.9 51.9 %collective-permute-start.4 = (bf16[528,1024]{1,0:T(8,128)(2,1)}, bf16[528,1024]{1,0:T(8,128)(2,1)}, u32[]{:S(2)}, u32[]{:S(2)}) collective-permute-start(bf16[528,1024]{1,0:T(8,128)(2,1)} %get-tuple-element.10.refs_1_), channel_id=1, source_target_pairs={{0,8},{8,16},{16,24},{24,0},{1,9},{9,17},{17,25},{25,1},{2,10},{10... | collective-permute-start | bytes 3244040 | tf_op jit(solution)/shard_map/ppermute | solution.py:199
  25.8 50.0 %collective-permute-start.5 = (bf16[528,1024]{1,0:T(8,128)(2,1)S(1)}, bf16[528,1024]{1,0:T(8,128)(2,1)}, u32[]{:S(2)}, u32[]{:S(2)}) collective-permute-start(bf16[528,1024]{1,0:T(8,128)(2,1)S(1)} %copy-done.2), channel_id=1, source_target_pairs={{0,24},{8,0},{16,8},{24,16},{1,25},{9,1},{17,9},{25,17},{2,26},{10... | collective-permute-start | bytes 3244040 | tf_op jit(solution)/shard_map/ppermute | solution.py:199
  34.5 3.3 %copy-start.3 = (f32[32,8,128]{2,1,0:T(8,128)}, f32[32,8,128]{2,1,0:T(8,128)S(1)}, u32[]{:S(2)}) copy-start(f32[32,8,128]{2,1,0:T(8,128)S(1)} %all-to-all-done.in_ref) | copy-start | bytes 393220
  34.5 19.6 %copy-start = (bf16[528,1024]{1,0:T(8,128)(2,1)}, bf16[528,1024]{1,0:T(8,128)(2,1)S(1)}, u32[]{:S(2)}) copy-start(bf16[528,1024]{1,0:T(8,128)(2,1)S(1)} %collective-permute-done.refs_0_) | copy-start | bytes 3244036
  34.5 51.3 %collective-permute-start.1 = (bf16[528,1024]{1,0:T(8,128)(2,1)S(1)}, bf16[528,1024]{1,0:T(8,128)(2,1)}, u32[]{:S(2)}, u32[]{:S(2)}) collective-permute-start(bf16[528,1024]{1,0:T(8,128)(2,1)S(1)} %collective-permute-done.refs_0_), channel_id=1, source_target_pairs={{0,8},{8,16},{16,24},{24,0},{1,9},{9,17},{17,25},{25,1},{2,10},{10... | collective-permute-start | bytes 3244040 | tf_op jit(solution)/shard_map/ppermute | solution.py:199
  35.9 18.2 %copy-start.1 = (bf16[528,1024]{1,0:T(8,128)(2,1)}, bf16[528,1024]{1,0:T(8,128)(2,1)S(1)}, u32[]{:S(2)}) copy-start(bf16[528,1024]{1,0:T(8,128)(2,1)S(1)} %collective-permute-done.2.refs_2_) | copy-start | bytes 3244036
  35.9 49.9 %collective-permute-start.3 = (bf16[528,1024]{1,0:T(8,128)(2,1)S(1)}, bf16[528,1024]{1,0:T(8,128)(2,1)}, u32[]{:S(2)}, u32[]{:S(2)}) collective-permute-start(bf16[528,1024]{1,0:T(8,128)(2,1)S(1)} %collective-permute-done.2.refs_2_), channel_id=1, source_target_pairs={{0,24},{8,0},{16,8},{24,16},{1,25},{9,1},{17,9},{25,17},{2,26},{10... | collective-permute-start | bytes 3244040 | tf_op jit(solution)/shard_map/ppermute | solution.py:199
  39.4 8.7 %all-to-all-start.1 = ((bf16[8,8,128]{2,1,0:T(8,128)(2,1)}), bf16[8,8,128]{2,1,0:T(8,128)(2,1)S(1)}, u32[]{:S(2)}, u32[]{:S(2)}) async-start(bf16[8,8,128]{2,1,0:T(8,128)(2,1)} %harmonics.1), calls=%async_computation.1 | async-start | bytes 32768 | tf_op jit(solution)/shard_map/all_to_all | solution.py:338
  48.1 0.6 copy-start.6
  54.2 11.3 %all-to-all-start.2 = ((f32[8,12,256]{2,1,0:T(8,128)}), f32[8,12,256]{2,1,0:T(8,128)S(1)}, u32[]{:S(2)}, u32[]{:S(2)}) async-start(f32[8,12,256]{2,1,0:T(8,128)} %legendre.1), calls=%async_computation.2 | async-start | bytes 262144 | tf_op jit(solution)/shard_map/all_to_all | solution.py:341
  66.5 32.1 %all-to-all-start.3 = ((bf16[32,1,96]{2,1,0:T(2,128)(2,1)}), bf16[32,1,96]{2,1,0:T(2,128)(2,1)S(1)}, u32[]{:S(2)}, u32[]{:S(2)}) async-start(bf16[32,1,96]{2,1,0:T(2,128)(2,1)} %copy.19), calls=%async_computation.3 | async-start | bytes 32768 | tf_op jit(solution)/shard_map/all_to_all | solution.py:344
  95.6 5.5 %collective-permute-start.10 = (bf16[64,1024]{1,0:T(8,128)(2,1)S(1)}, bf16[64,1024]{1,0:T(8,128)(2,1)S(1)}, u32[]{:S(2)}, u32[]{:S(2)}) collective-permute-start(bf16[64,1024]{1,0:T(8,128)(2,1)S(1)} %get-tuple-element.19), channel_id=1, source_target_pairs={{0,224},{32,0},{64,32},{96,64},{128,96},{160,128},{192,160},{224,1... | collective-permute-start | bytes 393224 | tf_op jit(solution)/shard_map/ppermute | solution.py:199
  101.1 7.9 %collective-permute-start.11 = (bf16[128,1024]{1,0:T(8,128)(2,1)S(1)}, bf16[128,1024]{1,0:T(8,128)(2,1)S(1)}, u32[]{:S(2)}, u32[]{:S(2)}) collective-permute-start(bf16[128,1024]{1,0:T(8,128)(2,1)S(1)} %pad_maximum_fusion.2), channel_id=1, source_target_pairs={{0,224},{32,0},{64,32},{96,64},{128,96},{160,128},{192,160},{224,1... | collective-permute-start | bytes 786440 | tf_op jit(solution)/shard_map/ppermute | solution.py:199
  110.1 7.7 %collective-permute-start.12 = (bf16[128,1024]{1,0:T(8,128)(2,1)S(1)}, bf16[128,1024]{1,0:T(8,128)(2,1)S(1)}, u32[]{:S(2)}, u32[]{:S(2)}) collective-permute-start(bf16[128,1024]{1,0:T(8,128)(2,1)S(1)} %fusion), channel_id=1, source_target_pairs={{0,224},{32,0},{64,32},{96,64},{128,96},{160,128},{192,160},{224,1... | collective-permute-start | bytes 786440 | tf_op jit(solution)/shard_map/ppermute | solution.py:199
  113.9 6.2 %collective-permute-start.6 = (bf16[64,1024]{1,0:T(8,128)(2,1)S(1)}, bf16[64,1024]{1,0:T(8,128)(2,1)S(1)}, u32[]{:S(2)}, u32[]{:S(2)}) collective-permute-start(bf16[64,1024]{1,0:T(8,128)(2,1)S(1)} %get-tuple-element.20), channel_id=1, source_target_pairs={{0,32},{32,64},{64,96},{96,128},{128,160},{160,192},{192,224},{224... | collective-permute-start | bytes 393224 | tf_op jit(solution)/shard_map/ppermute | solution.py:199
  120.2 8.1 %collective-permute-start.7 = (bf16[128,1024]{1,0:T(8,128)(2,1)S(1)}, bf16[128,1024]{1,0:T(8,128)(2,1)S(1)}, u32[]{:S(2)}, u32[]{:S(2)}) collective-permute-start(bf16[128,1024]{1,0:T(8,128)(2,1)S(1)} %pad_maximum_fusion.1), channel_id=1, source_target_pairs={{0,32},{32,64},{64,96},{96,128},{128,160},{160,192},{192,224},{224... | collective-permute-start | bytes 786440 | tf_op jit(solution)/shard_map/ppermute | solution.py:199
  129.4 8.3 %collective-permute-start.8 = (bf16[128,1024]{1,0:T(8,128)(2,1)S(1)}, bf16[128,1024]{1,0:T(8,128)(2,1)S(1)}, u32[]{:S(2)}, u32[]{:S(2)}) collective-permute-start(bf16[128,1024]{1,0:T(8,128)(2,1)S(1)} %fusion.2), channel_id=1, source_target_pairs={{0,32},{32,64},{64,96},{96,128},{128,160},{160,192},{192,224},{224... | collective-permute-start | bytes 786440 | tf_op jit(solution)/shard_map/ppermute | solution.py:199
  129.5 15.5 %collective-permute-start.13 = (bf16[128,1024]{1,0:T(8,128)(2,1)S(1)}, bf16[128,1024]{1,0:T(8,128)(2,1)S(1)}, u32[]{:S(2)}, u32[]{:S(2)}) collective-permute-start(bf16[128,1024]{1,0:T(8,128)(2,1)S(1)} %get-tuple-element.16), channel_id=1, source_target_pairs={{0,224},{32,0},{64,32},{96,64},{128,96},{160,128},{192,160},{224,1... | collective-permute-start | bytes 786440 | tf_op jit(solution)/shard_map/ppermute | solution.py:199
  138.8 7.7 %collective-permute-start.9 = (bf16[128,1024]{1,0:T(8,128)(2,1)S(1)}, bf16[128,1024]{1,0:T(8,128)(2,1)S(1)}, u32[]{:S(2)}, u32[]{:S(2)}) collective-permute-start(bf16[128,1024]{1,0:T(8,128)(2,1)S(1)} %fusion.3), channel_id=1, source_target_pairs={{0,32},{32,64},{64,96},{96,128},{128,160},{160,192},{192,224},{224... | collective-permute-start | bytes 786440 | tf_op jit(solution)/shard_map/ppermute | solution.py:199
  145.0 1.5 copy-start.4
  146.5 0.7 copy-start.5

commit v2 on v1

--- a/solution.py
+++ b/solution.py
@@ -199,29 +199,40 @@
     return lax.ppermute(x, axis, [(i, (i + by) % size) for i in range(size)])
 
 
-def ring_sums(chunk, axis, token):
-    size = lax.axis_size(axis)
+def add_kernel(lead, moving_ref, own_ref, out_ref):
+    size = moving_ref.shape[0]
+    if size < own_ref.shape[0]:
+        other = size if lead == 0 else 0
+        out_ref[other : other + size] = own_ref[other : other + size].astype(out_ref.dtype)
+    added = own_ref[lead : lead + size] + moving_ref[...].astype(jnp.float32)
+    out_ref[lead : lead + size] = added.astype(out_ref.dtype)
+
+
+def ring_add(moving, own, lead):
+    return pl.pallas_call(
+        functools.partial(add_kernel, lead),
+        out_shape=jax.ShapeDtypeStruct(own.shape, moving.dtype),
+        name="ring_add",
+    )(moving, own)
+
+
+def ring_sums(chunks, far, axis, token):
+    size = len(chunks)
     middle = size // 2
-    half = chunk(middle).shape[0] // 2
-
-    def toward(by, first):
-        far = chunk(middle)
-        moving = far[:half] if first else far[half:]
+
+    def toward(by, moving, lead):
         for distance in range(middle - 1, -1, -1):
-            moving = shifted(moving.astype(jnp.bfloat16), axis, by).astype(jnp.float32)
+            moving = shifted(moving, axis, by)
             if distance == 0:
                 return moving
-            own = chunk(distance if by == 1 else size - distance)
+            own = chunks[distance if by == 1 else size - distance]
             if distance == middle - 1:
-                own = after(own, token)
-                if first:
-                    moving = jnp.concatenate([own[:half] + moving, own[half:]], axis=0)
-                else:
-                    moving = jnp.concatenate([own[:half], own[half:] + moving], axis=0)
+                moving = ring_add(moving, after(own, token), lead)
             else:
-                moving = own + moving
-
-    return chunk(0), toward(1, True), toward(-1, False)
+                moving = ring_add(moving, own, 0)
+
+    half = far[0].shape[0]
+    return chunks[0], toward(1, far[0], 0), toward(-1, far[1], half)
 
 
 def after(x, token):
@@ -232,57 +243,103 @@
 EXTRA = 16
 
 
-def pack_kernel(rows_ref, owner_ref, key_ref, *out_refs):
-    size = rows_ref.shape[0] // len(out_refs)
+def pack_kernel(rows_hbm, owner_ref, key_ref, *refs):
+    tail_ref, sems = refs[-2:]
+    outs = refs[:-2]
+    size = rows_hbm.shape[0] // len(outs)
+    copies = []
+    for part, out in enumerate(outs):
+        copy = pltpu.make_async_copy(
+            rows_hbm.at[pl.ds(part * size, size)], out.at[pl.ds(0, size)], sems.at[part]
+        )
+        copy.start()
+        copies.append(copy)
     key = key_ref[...]
     place = (key & 64) + (key & 7) * R_DEV + ((key >> 3) & 7)
     slot = owner_ref[...] * KEYS + place
-    for part, out_ref in enumerate(out_refs):
+    tail_ref[...] = jnp.zeros(tail_ref.shape, tail_ref.dtype)
+    for part, out in enumerate(outs):
         own = slot[:, part * size : (part + 1) * size]
         row = lax.broadcasted_iota(jnp.int32, (EXTRA, size), 0)
         tail = jnp.where(row == 0, own // DIGIT, jnp.where(row == 1, own % DIGIT, 0))
-        out_ref[:size] = rows_ref[part * size : (part + 1) * size]
-        out_ref[size:] = jnp.zeros((EXTRA, rows_ref.shape[1]), out_ref.dtype)
-        out_ref[size:, :size] = tail.astype(jnp.float32).astype(out_ref.dtype)
+        tail_ref[part, :, :size] = tail.astype(jnp.float32).astype(tail_ref.dtype)
+        copy = pltpu.make_async_copy(
+            tail_ref.at[part], out.at[pl.ds(size, EXTRA)], sems.at[len(outs) + part]
+        )
+        copy.start()
+        copies.append(copy)
+    for copy in copies:
+        copy.wait()
 
 
 def row_pieces(rows, owners, keys, parts):
     piece = jax.ShapeDtypeStruct((rows.shape[0] // parts + EXTRA, rows.shape[1]), rows.dtype)
-    return pl.pallas_call(pack_kernel, out_shape=(piece,) * parts, name="pack")(
-        rows, owners[None], keys[None]
-    )
-
-
-def sums_kernel(count, has_base, columns, rings, place_ref, *refs):
-    pieces, out_ref = refs[:count], refs[-1]
-    my_z, my_y = place_ref[0], place_ref[1]
-    slots = out_ref.shape[0]
+    vmem = pl.BlockSpec(memory_space=pltpu.VMEM)
+    left = pl.BlockSpec(memory_space=pl.ANY)
+    return pl.pallas_call(
+        pack_kernel,
+        out_shape=(piece,) * parts,
+        in_specs=[left, vmem, vmem],
+        out_specs=(left,) * parts,
+        scratch_shapes=[
+            pltpu.VMEM((parts, EXTRA, rows.shape[1]), rows.dtype),
+            pltpu.SemaphoreType.DMA((2 * parts,)),
+        ],
+        name="pack",
+    )(rows, owners[None], keys[None])
+
+
+def sums_kernel(count, has_base, columns, rings, first, place_ref, *refs):
+    pieces, tails = refs[:count], refs[count : 2 * count]
+    outs, pick_ref = refs[2 * count + has_base : -1], refs[-1]
+    slots = pick_ref.shape[0]
+    size = pieces[0].shape[0]
+
+    @pl.when(pl.program_id(0) == 0)
+    def _():
+        my_z, my_y = place_ref[0], place_ref[1]
+        for index, tail_ref in enumerate(tails):
+            tail = tail_ref[:, :size].astype(jnp.float32).astype(jnp.int32)
+            slot = tail[0:1] * DIGIT + tail[1:2]
+            owner = slot // KEYS
+            distance = (owner // columns - my_z) & (rings - 1)
+            mine = (distance - first) * KEYS + (slot & (KEYS - 1))
+            mine = jnp.where((owner & (columns - 1)) == my_y, mine, -1)
+            pick = lax.broadcasted_iota(jnp.int32, (slots, size), 0) == mine
+            pick_ref[:, index * size : (index + 1) * size] = jnp.where(pick, 1.0, 0.0).astype(
+                jnp.bfloat16
+            )
+
+    total = refs[2 * count][...] if has_base else 0.0
     for index, piece in enumerate(pieces):
-        size = piece.shape[0] - EXTRA
-        tail = piece[size : size + EXTRA, :size].astype(jnp.float32).astype(jnp.int32)
-        slot = tail[0:1] * DIGIT + tail[1:2]
-        owner = slot // KEYS
-        distance = (owner // columns - my_z) & (rings - 1)
-        mine = jnp.where((owner & (columns - 1)) == my_y, distance * KEYS + (slot & (KEYS - 1)), -1)
-        pick = lax.broadcasted_iota(jnp.int32, (slots, size), 0) == mine
-        pick = jnp.where(pick, 1.0, 0.0).astype(jnp.bfloat16)
-        add = dot32(pick, piece[:size], NN)
-        if index == 0:
-            out_ref[...] = refs[count][...] + add if has_base else add
-        else:
-            out_ref[...] += add
-
-
-def sum_pieces(pieces, base, place):
+        total = total + dot32(pick_ref[:, index * size : (index + 1) * size], piece[...], NN)
+    rows = slots // len(outs)
+    for index, out in enumerate(outs):
+        out[...] = total[index * rows : (index + 1) * rows].astype(out.dtype)
+
+
+TILE = 256
+
+
+def sum_pieces(pieces, base, place, outs, dtype, first=0, chunks=None):
     columns, rings = lax.axis_size(BLK[1]), lax.axis_size(BLK[0])
-    smem = pl.BlockSpec(memory_space=pltpu.SMEM)
-    vmem = pl.BlockSpec(memory_space=pltpu.VMEM)
-    operands = list(pieces) + ([] if base is None else [base])
-    return pl.pallas_call(
-        functools.partial(sums_kernel, len(pieces), base is not None, columns, rings),
-        out_shape=jax.ShapeDtypeStruct((rings * KEYS, pieces[0].shape[1]), jnp.float32),
-        in_specs=[smem] + [vmem] * len(operands),
-        out_specs=vmem,
+    chunks = rings if chunks is None else chunks
+    size, lanes = pieces[0].shape[0] - EXTRA, pieces[0].shape[1]
+    slots = chunks * KEYS
+    specs = [pl.BlockSpec(memory_space=pltpu.SMEM)]
+    specs += [pl.BlockSpec((size, TILE), lambda n: (0, n)) for _ in pieces]
+    specs += [pl.BlockSpec((EXTRA, lanes), lambda n: (size // EXTRA, 0)) for _ in pieces]
+    operands = [*pieces, *pieces]
+    if base is not None:
+        specs.append(pl.BlockSpec((slots, TILE), lambda n: (first // chunks, n)))
+        operands.append(base)
+    return pl.pallas_call(
+        functools.partial(sums_kernel, len(pieces), int(base is not None), columns, rings, first),
+        out_shape=tuple(jax.ShapeDtypeStruct((slots // outs, lanes), dtype) for _ in range(outs)),
+        grid=(lanes // TILE,),
+        in_specs=specs,
+        out_specs=tuple(pl.BlockSpec((slots // outs, TILE), lambda n: (0, n)) for _ in range(outs)),
+        scratch_shapes=[pltpu.VMEM((slots, size * len(pieces)), jnp.bfloat16)],
     )(place, *operands)
 
 
@@ -299,10 +356,17 @@
         self.down_far = shifted(after(self.down[0], token), BLK[1], -1)
 
     def finish(self, token):
-        sums = sum_pieces(self.pieces, None, self.place)
-        sums = sum_pieces(self.up + self.down, sums, self.place)
-        sums = sum_pieces([self.up_far, self.down_far], sums, self.place)
-        return ring_sums(lambda d: sums[d * KEYS : (d + 1) * KEYS], BLK[0], token)
+        def add(pieces, base):
+            return sum_pieces(pieces, base, self.place, 1, jnp.float32)[0]
+
+        sums = add(self.pieces, None)
+        sums = add([self.up[0], self.down[0]], sums)
+        sums = add([self.up[1], self.down[1]], sums)
+        rings = lax.axis_size(BLK[0])
+        last = [self.up_far, self.down_far]
+        far = sum_pieces(last, sums, self.place, 2, jnp.bfloat16, rings // 2, 1)
+        chunks = sum_pieces(last, sums, self.place, rings, jnp.float32)
+        return ring_sums(chunks, far, BLK[0], token)
 
 
 def maps_kernel(own_ref, up_ref, down_ref, out_ref):

time: 150 us -> 215 us (1.43)
  the two profiles are of different devices: /device:TPU:2 before, /device:TPU:8 now
where the time goes in v2:
time: 215 us; the launch traced here: 214 us
  Pallas kernels  127 us (59%)
  starting transfers between devices  49.6 us (23%)
  waiting for transfers between devices  24.9 us (12%)
  local copies, waits for them, and re-layouts  9.77 us (5%)
    pallas_call x1, Pallas kernels, row_pieces(): pl.pallas_call(pack_kernel, out_shape=(piece,) * parts, in_specs=[left, v...  65.4 us
    pallas_call x5, Pallas kernels, sum_pieces(): pl.pallas_call(functools.partial(sums_kernel, len(pieces), int(base is no...  31.3 us
    ppermute x14, starting transfers between devices, shifted(): return lax.ppermute(x, axis, [(i, (i + by) % size) for i in range(size)])  19.7 us
    all_to_all x1, starting transfers between devices, body(): arrived = lax.all_to_all(sums, BLK, split_axis=0, concat_axis=0, tiled=True)  11.5 us
    pallas_call x6, Pallas kernels, ring_add(): pl.pallas_call(functools.partial(add_kernel, lead), out_shape=jax.ShapeDt...  11.1 us
    all_to_all x1, starting transfers between devices, body(): lax.all_to_all(summed, BLK, split_axis=0, concat_axis=0, tiled=True)  10.8 us
    all_to_all x1, waiting for transfers between devices, body(): arrived = lax.all_to_all(sums, BLK, split_axis=0, concat_axis=0, tiled=True)  8.06 us
    unnamed x28, local copies, waits for them, and re-layouts  7.42 us
  transfers between devices with their start and end apart: 18, of which 6 were waited for; matrix products, arithmetic and copies ran while one was open for 2% of the time, Pallas kernels for 28%

profile of v2, /device:TPU:8, one launch (start us, length us, event | category | flops | bytes accessed | tf_op | source)
XLA Modules:
  0.0 213.9 jit_solution(839393228761029315)
XLA Ops:
  0.6 65.4 %pack.1 = (bf16[528,1024]{1,0:T(8,128)(2,1)}, bf16[528,1024]{1,0:T(8,128)(2,1)}) custom-call(bf16[1024,1024]{1,0:T(8,128)(2,1)} %bitcast.15, s32[1,1024]{1,0:T(1,128)} %bitcast.20, s32[1,1024]{1,0:T(1,128)} %key_ref.3), custom_call_target="tpu_custom_call" | custom-call | tf_op jit(solution)/shard_map/pack/pallas_call | solution.py:279
  66.0 1.7 collective-permute-start
  70.4 4.7 %modes.1 = f32[32,8,128]{2,1,0:T(8,128)} custom-call(bf16[1024,1024]{1,0:T(8,128)(2,1)} %bitcast.16, s32[1,1024]{1,0:T(1,128)} %bitcast.21, s32[1,1024]{1,0:T(1,128)} %key_ref.3, s32[32,1]{1,0:T(8,128)} %copy.17.order_ref, f32[64,1024]{1,0:T(8,128)} %pad_maximum_fusion.wave_ref), custom_call_target="tpu_custom_call" | custom-call | tf_op jit(solution)/shard_map/modes/pallas_call | solution.py:81
  75.0 11.5 %all-to-all-start = ((f32[32,8,128]{2,1,0:T(8,128)}), f32[32,8,128]{2,1,0:T(8,128)S(1)}, u32[]{:S(2)}, u32[]{:S(2)}) async-start(f32[32,8,128]{2,1,0:T(8,128)} %modes.1), calls=%async_computation | async-start | bytes 262144 | tf_op jit(solution)/shard_map/all_to_all | solution.py:399
  88.6 8.1 %all-to-all-done.in_ref = f32[32,8,128]{2,1,0:T(8,128)S(1)} async-done(((f32[32,8,128]{2,1,0:T(8,128)}), f32[32,8,128]{2,1,0:T(8,128)S(1)}, u32[]{:S(2)}, u32[]{:S(2)}) %all-to-all-start) | async-done | bytes 131104 | tf_op jit(solution)/shard_map/all_to_all | solution.py:399
  98.8 1.5 harmonics.1
  100.3 4.3 %all-to-all-start.1 = ((bf16[8,8,128]{2,1,0:T(8,128)(2,1)}), bf16[8,8,128]{2,1,0:T(8,128)(2,1)S(1)}, u32[]{:S(2)}, u32[]{:S(2)}) async-start(bf16[8,8,128]{2,1,0:T(8,128)(2,1)} %harmonics.1), calls=%async_computation.1 | async-start | bytes 32768 | tf_op jit(solution)/shard_map/all_to_all | solution.py:402
  104.6 5.4 %all-to-all-done.1.modes_ref = bf16[8,8,128]{2,1,0:T(8,128)(2,1)S(1)} async-done(((bf16[8,8,128]{2,1,0:T(8,128)(2,1)}), bf16[8,8,128]{2,1,0:T(8,128)(2,1)S(1)}, u32[]{:S(2)}, u32[]{:S(2)}) %all-to-all-start.1) | async-done | bytes 16416 | tf_op jit(solution)/shard_map/all_to_all | solution.py:402
  110.6 5.4 %legendre.1 = f32[8,12,256]{2,1,0:T(8,128)} custom-call(s32[1]{0:T(128)} %bitcast.first_ref, bf16[8,8,128]{2,1,0:T(8,128)(2,1)} %copy-done.12, bf16[1,512,2048]{2,1,0:T(8,128)(2,1)} %leg_ref.1, bf16[1,512,2048]{2,1,0:T(8,128)(2,1)} %even_hbm.1, bf16[1,512,2048]{2,1,0:T(8,128)(2,1)} %odd_hbm.1), custom_call_target="tpu_custom_call" | custom-call | tf_op jit(solution)/shard_map/legendre/pallas_call | solution.py:144
  116.0 3.4 %all-to-all-start.2 = ((f32[8,12,256]{2,1,0:T(8,128)}), f32[8,12,256]{2,1,0:T(8,128)S(1)}, u32[]{:S(2)}, u32[]{:S(2)}) async-start(f32[8,12,256]{2,1,0:T(8,128)} %legendre.1), calls=%async_computation.2 | async-start | bytes 262144 | tf_op jit(solution)/shard_map/all_to_all | solution.py:405
  119.4 6.0 %all-to-all-done.2 = f32[8,12,256]{2,1,0:T(8,128)S(1)} async-done(((f32[8,12,256]{2,1,0:T(8,128)}), f32[8,12,256]{2,1,0:T(8,128)S(1)}, u32[]{:S(2)}, u32[]{:S(2)}) %all-to-all-start.2) | async-done | bytes 98336 | tf_op jit(solution)/shard_map/all_to_all | solution.py:405
  126.4 10.8 %all-to-all-start.3 = ((bf16[32,1,96]{2,1,0:T(2,128)(2,1)}), bf16[32,1,96]{2,1,0:T(2,128)(2,1)S(1)}, u32[]{:S(2)}, u32[]{:S(2)}) async-start(bf16[32,1,96]{2,1,0:T(2,128)(2,1)} %copy.19), calls=%async_computation.3 | async-start | bytes 32768 | tf_op jit(solution)/shard_map/all_to_all | solution.py:408
  137.8 6.1 %shard_map.86.refs_4_ = f32[1024,1024]{1,0:T(8,128)} custom-call(s32[2]{0:T(128)} %pad_add_fusion.place_ref, bf16[528,1024]{1,0:T(8,128)(2,1)} %get-tuple-element.17.refs_0_.refs_2_, bf16[528,1024]{1,0:T(8,128)(2,1)} %get-tuple-element.19.refs_1_.refs_3_, bf16[528,1024]{1,0:T(8,128)(2,1)} %get-tuple-element.17.refs_0_.refs_2_, ...), custom_call_target="tpu_custom_call" | custom-call | tf_op jit(solution)/shard_map/pallas_call | solution.py:336
  143.9 7.2 %shard_map.87.refs_4_ = f32[1024,1024]{1,0:T(8,128)} custom-call(s32[2]{0:T(128)} %pad_add_fusion.place_ref, bf16[528,1024]{1,0:T(8,128)(2,1)} %copy-done.2, bf16[528,1024]{1,0:T(8,128)(2,1)} %collective-permute-done.2.refs_1_.refs_3_, bf16[528,1024]{1,0:T(8,128)(2,1)} %copy-done.2, bf16[528,1024]{1,0:T(8,128)(2,1)} %collective-permute-done.2.refs_1_.refs_3_, ...), custom_call_target="tpu_custom_call" | custom-call | tf_op jit(solution)/shard_map/pallas_call | solution.py:336
  151.1 7.1 %shard_map.88.refs_4_ = f32[1024,1024]{1,0:T(8,128)} custom-call(s32[2]{0:T(128)} %pad_add_fusion.place_ref, bf16[528,1024]{1,0:T(8,128)(2,1)} %collective-permute-done.4.refs_0_.refs_2_, bf16[528,1024]{1,0:T(8,128)(2,1)} %collective-permute-done.5.refs_1_.refs_3_, bf16[528,1024]{1,0:T(8,128)(2,1)} %collective-permute-done.4.refs_0_.refs_2_, ...), custom_call_target="tpu_custom_call" | custom-call | tf_op jit(solution)/shard_map/pallas_call | solution.py:336
  160.3 4.0 %shard_map.90 = (bf16[64,1024]{1,0:T(8,128)(2,1)}, bf16[64,1024]{1,0:T(8,128)(2,1)}) custom-call(s32[2]{0:T(128)} %pad_add_fusion.place_ref, bf16[528,1024]{1,0:T(8,128)(2,1)} %copy-done, bf16[528,1024]{1,0:T(8,128)(2,1)} %copy-done.1, bf16[528,1024]{1,0:T(8,128)(2,1)} %copy-done, bf16[528,1024]{1,0:T(8,128)(2,1)} %copy-done.1, f32[1024,1024]{1,0:T(8,128)} %shard_map.88.refs_4_), custom_call_target="tpu_custom_call" | custom-call | tf_op jit(solution)/shard_map/pallas_call | solution.py:336
  164.3 2.8 %collective-permute-start.10 = (bf16[64,1024]{1,0:T(8,128)(2,1)}, bf16[64,1024]{1,0:T(8,128)(2,1)S(1)}, u32[]{:S(2)}, u32[]{:S(2)}) collective-permute-start(bf16[64,1024]{1,0:T(8,128)(2,1)} %get-tuple-element.27), channel_id=1, source_target_pairs={{0,224},{32,0},{64,32},{96,64},{128,96},{160,128},{192,160},{224,1... | collective-permute-start | bytes 393224 | tf_op jit(solution)/shard_map/ppermute | solution.py:199
  167.1 6.9 %shard_map.89 = (f32[128,1024]{1,0:T(8,128)}, f32[128,1024]{1,0:T(8,128)}, f32[128,1024]{1,0:T(8,128)}, f32[128,1024]{1,0:T(8,128)}, f32[128,1024]{1,0:T(8,128)}...) custom-call(s32[2]{0:T(128)} %pad_add_fusion.place_ref, bf16[528,1024]{1,0:T(8,128)(2,1)} %copy-done, ...), custom_call_target="tpu_custom_call" | custom-call | tf_op jit(solution)/shard_map/pallas_call | solution.py:336
  174.6 1.9 ring_add.9
  176.5 3.2 %collective-permute-start.11 = (bf16[128,1024]{1,0:T(8,128)(2,1)}, bf16[128,1024]{1,0:T(8,128)(2,1)S(1)}, u32[]{:S(2)}, u32[]{:S(2)}) collective-permute-start(bf16[128,1024]{1,0:T(8,128)(2,1)} %ring_add.9), channel_id=1, source_target_pairs={{0,224},{32,0},{64,32},{96,64},{128,96},{160,128},{192,160},{224,1... | collective-permute-start | bytes 786440 | tf_op jit(solution)/shard_map/ppermute | solution.py:199
  180.3 1.8 ring_add.6
  182.2 2.1 collective-permute-done.11.moving_ref
  184.9 1.9 ring_add.10
  186.8 3.6 %collective-permute-start.12 = (bf16[128,1024]{1,0:T(8,128)(2,1)}, bf16[128,1024]{1,0:T(8,128)(2,1)S(1)}, u32[]{:S(2)}, u32[]{:S(2)}) collective-permute-start(bf16[128,1024]{1,0:T(8,128)(2,1)} %ring_add.10), channel_id=1, source_target_pairs={{0,224},{32,0},{64,32},{96,64},{128,96},{160,128},{192,160},{224,1... | collective-permute-start | bytes 786440 | tf_op jit(solution)/shard_map/ppermute | solution.py:199
  191.1 1.9 ring_add.7
  193.0 1.6 collective-permute-done.12.moving_ref
  195.3 1.9 ring_add.11
  197.2 3.6 %collective-permute-start.13 = (bf16[128,1024]{1,0:T(8,128)(2,1)}, bf16[128,1024]{1,0:T(8,128)(2,1)S(1)}, u32[]{:S(2)}, u32[]{:S(2)}) collective-permute-start(bf16[128,1024]{1,0:T(8,128)(2,1)} %ring_add.11), channel_id=1, source_target_pairs={{0,224},{32,0},{64,32},{96,64},{128,96},{160,128},{192,160},{224,1... | collective-permute-start | bytes 786440 | tf_op jit(solution)/shard_map/ppermute | solution.py:199
  201.5 1.9 ring_add.8
  204.1 5.4 %fields.1 = f32[2,2,1,8,8192]{4,3,2,1,0:T(8,128)} custom-call(f32[12,8,32]{2,1,0:T(8,128)} %bitcast.18, s32[1,32]{1,0:T(1,128)} %bitcast.22, f32[64,1024]{1,0:T(8,128)} %pad_maximum_fusion.wave_ref), custom_call_target="tpu_custom_call" | custom-call | tf_op jit(solution)/shard_map/fields/pallas_call | solution.py:187
  209.5 1.7 collective-permute-done.9.up_ref
  211.8 2.0 maps.1
  (59 shorter events, 16.6 us)
Async XLA Ops:
  0.6 67.7 %copy-start.13 = (s32[32]{0:T(128)S(1)}, s32[32]{0:T(128)}, u32[]{:S(2)}) copy-start(s32[32]{0:T(128)} %param.10) | copy-start | bytes 388
  66.0 30.6 %collective-permute-start = (bf16[528,1024]{1,0:T(8,128)(2,1)}, bf16[528,1024]{1,0:T(8,128)(2,1)S(1)}, u32[]{:S(2)}, u32[]{:S(2)}) collective-permute-start(bf16[528,1024]{1,0:T(8,128)(2,1)} %get-tuple-element.17.refs_0_.refs_2_), channel_id=1, source_target_pairs={{0,8},{8,16},{16,24},{24,0},{1,9},{9,17},{17,25},{25,1},{2,10},{10... | collective-permute-start | bytes 3244040 | tf_op jit(solution)/shard_map/ppermute | solution.py:199
  67.7 29.7 %collective-permute-start.2 = (bf16[528,1024]{1,0:T(8,128)(2,1)}, bf16[528,1024]{1,0:T(8,128)(2,1)}, u32[]{:S(2)}, u32[]{:S(2)}) collective-permute-start(bf16[528,1024]{1,0:T(8,128)(2,1)} %get-tuple-element.19.refs_1_.refs_3_), channel_id=1, source_target_pairs={{0,24},{8,0},{16,8},{24,16},{1,25},{9,1},{17,9},{25,17},{2,26},{10... | collective-permute-start | bytes 3244040 | tf_op jit(solution)/shard_map/ppermute | solution.py:199
  75.0 21.6 %all-to-all-start = ((f32[32,8,128]{2,1,0:T(8,128)}), f32[32,8,128]{2,1,0:T(8,128)S(1)}, u32[]{:S(2)}, u32[]{:S(2)}) async-start(f32[32,8,128]{2,1,0:T(8,128)} %modes.1), calls=%async_computation | async-start | bytes 262144 | tf_op jit(solution)/shard_map/all_to_all | solution.py:399
  86.5 64.6 %collective-permute-start.4 = (bf16[528,1024]{1,0:T(8,128)(2,1)}, bf16[528,1024]{1,0:T(8,128)(2,1)}, u32[]{:S(2)}, u32[]{:S(2)}) collective-permute-start(bf16[528,1024]{1,0:T(8,128)(2,1)} %get-tuple-element.19.refs_1_.refs_3_), channel_id=1, source_target_pairs={{0,8},{8,16},{16,24},{24,0},{1,9},{9,17},{17,25},{25,1},{2,10},{10... | collective-permute-start | bytes 3244040 | tf_op jit(solution)/shard_map/ppermute | solution.py:199
  88.0 63.0 %collective-permute-start.5 = (bf16[528,1024]{1,0:T(8,128)(2,1)}, bf16[528,1024]{1,0:T(8,128)(2,1)}, u32[]{:S(2)}, u32[]{:S(2)}) collective-permute-start(bf16[528,1024]{1,0:T(8,128)(2,1)} %get-tuple-element.17.refs_0_.refs_2_), channel_id=1, source_target_pairs={{0,24},{8,0},{16,8},{24,16},{1,25},{9,1},{17,9},{25,17},{2,26},{10... | collective-permute-start | bytes 3244040 | tf_op jit(solution)/shard_map/ppermute | solution.py:199
  96.7 2.1 copy-start.3
  96.7 19.4 %copy-start.2 = (bf16[528,1024]{1,0:T(8,128)(2,1)}, bf16[528,1024]{1,0:T(8,128)(2,1)S(1)}, u32[]{:S(2)}) copy-start(bf16[528,1024]{1,0:T(8,128)(2,1)S(1)} %collective-permute-done.refs_0_.refs_2_) | copy-start | bytes 3244036
  96.7 61.6 %collective-permute-start.1 = (bf16[528,1024]{1,0:T(8,128)(2,1)S(1)}, bf16[528,1024]{1,0:T(8,128)(2,1)S(1)}, u32[]{:S(2)}, u32[]{:S(2)}) collective-permute-start(bf16[528,1024]{1,0:T(8,128)(2,1)S(1)} %collective-permute-done.refs_0_.refs_2_), channel_id=1, source_target_pairs={{0,8},{8,16},{16,24},{24,0},{1,9},{9,17},{17,25},{25,1},{2,10},{10... | collective-permute-start | bytes 3244040 | tf_op jit(solution)/shard_map/ppermute | solution.py:199
  97.4 60.9 %collective-permute-start.3 = (bf16[528,1024]{1,0:T(8,128)(2,1)}, bf16[528,1024]{1,0:T(8,128)(2,1)S(1)}, u32[]{:S(2)}, u32[]{:S(2)}) collective-permute-start(bf16[528,1024]{1,0:T(8,128)(2,1)} %collective-permute-done.2.refs_1_.refs_3_), channel_id=1, source_target_pairs={{0,24},{8,0},{16,8},{24,16},{1,25},{9,1},{17,9},{25,17},{2,26},{10... | collective-permute-start | bytes 3244040 | tf_op jit(solution)/shard_map/ppermute | solution.py:199
  100.3 9.7 %all-to-all-start.1 = ((bf16[8,8,128]{2,1,0:T(8,128)(2,1)}), bf16[8,8,128]{2,1,0:T(8,128)(2,1)S(1)}, u32[]{:S(2)}, u32[]{:S(2)}) async-start(bf16[8,8,128]{2,1,0:T(8,128)(2,1)} %harmonics.1), calls=%async_computation.1 | async-start | bytes 32768 | tf_op jit(solution)/shard_map/all_to_all | solution.py:402
  110.0 0.6 copy-start.12
  116.0 9.4 %all-to-all-start.2 = ((f32[8,12,256]{2,1,0:T(8,128)}), f32[8,12,256]{2,1,0:T(8,128)S(1)}, u32[]{:S(2)}, u32[]{:S(2)}) async-start(f32[8,12,256]{2,1,0:T(8,128)} %legendre.1), calls=%async_computation.2 | async-start | bytes 262144 | tf_op jit(solution)/shard_map/all_to_all | solution.py:405
  126.4 40.6 %all-to-all-start.3 = ((bf16[32,1,96]{2,1,0:T(2,128)(2,1)}), bf16[32,1,96]{2,1,0:T(2,128)(2,1)S(1)}, u32[]{:S(2)}, u32[]{:S(2)}) async-start(bf16[32,1,96]{2,1,0:T(2,128)(2,1)} %copy.19), calls=%async_computation.3 | async-start | bytes 32768 | tf_op jit(solution)/shard_map/all_to_all | solution.py:408
  158.2 1.0 copy-start
  159.3 1.0 copy-start.1
  164.3 9.6 %collective-permute-start.10 = (bf16[64,1024]{1,0:T(8,128)(2,1)}, bf16[64,1024]{1,0:T(8,128)(2,1)S(1)}, u32[]{:S(2)}, u32[]{:S(2)}) collective-permute-start(bf16[64,1024]{1,0:T(8,128)(2,1)} %get-tuple-element.27), channel_id=1, source_target_pairs={{0,224},{32,0},{64,32},{96,64},{128,96},{160,128},{192,160},{224,1... | collective-permute-start | bytes 393224 | tf_op jit(solution)/shard_map/ppermute | solution.py:199
  167.1 12.6 %collective-permute-start.6 = (bf16[64,1024]{1,0:T(8,128)(2,1)}, bf16[64,1024]{1,0:T(8,128)(2,1)S(1)}, u32[]{:S(2)}, u32[]{:S(2)}) collective-permute-start(bf16[64,1024]{1,0:T(8,128)(2,1)} %get-tuple-element.22), channel_id=1, source_target_pairs={{0,32},{32,64},{64,96},{96,128},{128,160},{160,192},{192,224},{224... | collective-permute-start | bytes 393224 | tf_op jit(solution)/shard_map/ppermute | solution.py:199
  173.9 0.7 copy-start.11
  176.5 7.8 %collective-permute-start.11 = (bf16[128,1024]{1,0:T(8,128)(2,1)}, bf16[128,1024]{1,0:T(8,128)(2,1)S(1)}, u32[]{:S(2)}, u32[]{:S(2)}) collective-permute-start(bf16[128,1024]{1,0:T(8,128)(2,1)} %ring_add.9), channel_id=1, source_target_pairs={{0,224},{32,0},{64,32},{96,64},{128,96},{160,128},{192,160},{224,1... | collective-permute-start | bytes 786440 | tf_op jit(solution)/shard_map/ppermute | solution.py:199
  179.7 0.7 copy-start.10
  182.2 8.2 %collective-permute-start.7 = (bf16[128,1024]{1,0:T(8,128)(2,1)}, bf16[128,1024]{1,0:T(8,128)(2,1)S(1)}, u32[]{:S(2)}, u32[]{:S(2)}) collective-permute-start(bf16[128,1024]{1,0:T(8,128)(2,1)} %ring_add.6), channel_id=1, source_target_pairs={{0,32},{32,64},{64,96},{96,128},{128,160},{160,192},{192,224},{224... | collective-permute-start | bytes 786440 | tf_op jit(solution)/shard_map/ppermute | solution.py:199
  184.3 0.7 copy-start.5
  186.8 7.8 %collective-permute-start.12 = (bf16[128,1024]{1,0:T(8,128)(2,1)}, bf16[128,1024]{1,0:T(8,128)(2,1)S(1)}, u32[]{:S(2)}, u32[]{:S(2)}) collective-permute-start(bf16[128,1024]{1,0:T(8,128)(2,1)} %ring_add.10), channel_id=1, source_target_pairs={{0,224},{32,0},{64,32},{96,64},{128,96},{160,128},{192,160},{224,1... | collective-permute-start | bytes 786440 | tf_op jit(solution)/shard_map/ppermute | solution.py:199
  190.4 0.7 copy-start.6
  193.0 7.8 %collective-permute-start.8 = (bf16[128,1024]{1,0:T(8,128)(2,1)}, bf16[128,1024]{1,0:T(8,128)(2,1)S(1)}, u32[]{:S(2)}, u32[]{:S(2)}) collective-permute-start(bf16[128,1024]{1,0:T(8,128)(2,1)} %ring_add.7), channel_id=1, source_target_pairs={{0,32},{32,64},{64,96},{96,128},{128,160},{160,192},{192,224},{224... | collective-permute-start | bytes 786440 | tf_op jit(solution)/shard_map/ppermute | solution.py:199
  194.6 0.7 copy-start.7
  197.2 12.3 %collective-permute-start.13 = (bf16[128,1024]{1,0:T(8,128)(2,1)}, bf16[128,1024]{1,0:T(8,128)(2,1)S(1)}, u32[]{:S(2)}, u32[]{:S(2)}) collective-permute-start(bf16[128,1024]{1,0:T(8,128)(2,1)} %ring_add.11), channel_id=1, source_target_pairs={{0,224},{32,0},{64,32},{96,64},{128,96},{160,128},{192,160},{224,1... | collective-permute-start | bytes 786440 | tf_op jit(solution)/shard_map/ppermute | solution.py:199
  200.8 0.7 copy-start.8
  203.3 7.8 %collective-permute-start.9 = (bf16[128,1024]{1,0:T(8,128)(2,1)}, bf16[128,1024]{1,0:T(8,128)(2,1)S(1)}, u32[]{:S(2)}, u32[]{:S(2)}) collective-permute-start(bf16[128,1024]{1,0:T(8,128)(2,1)} %ring_add.8), channel_id=1, source_target_pairs={{0,32},{32,64},{64,96},{96,128},{128,160},{160,192},{192,224},{224... | collective-permute-start | bytes 786440 | tf_op jit(solution)/shard_map/ppermute | solution.py:199
  209.5 1.7 copy-start.4
  211.1 0.7 copy-start.9

commit v3 on v2

--- a/solution.py
+++ b/solution.py
@@ -199,40 +199,48 @@
     return lax.ppermute(x, axis, [(i, (i + by) % size) for i in range(size)])
 
 
-def add_kernel(lead, moving_ref, own_ref, out_ref):
-    size = moving_ref.shape[0]
-    if size < own_ref.shape[0]:
-        other = size if lead == 0 else 0
-        out_ref[other : other + size] = own_ref[other : other + size].astype(out_ref.dtype)
-    added = own_ref[lead : lead + size] + moving_ref[...].astype(jnp.float32)
-    out_ref[lead : lead + size] = added.astype(out_ref.dtype)
-
-
-def ring_add(moving, own, lead):
-    return pl.pallas_call(
-        functools.partial(add_kernel, lead),
-        out_shape=jax.ShapeDtypeStruct(own.shape, moving.dtype),
+def add_kernel(up_ref, down_ref, up_own_ref, down_own_ref, up_out, down_out):
+    size, whole = up_ref.shape[0], up_own_ref.shape[0]
+    for lead, moving_ref, own_ref, out in (
+        (0, up_ref, up_own_ref, up_out),
+        (whole - size, down_ref, down_own_ref, down_out),
+    ):
+        if size < whole:
+            other = size - lead
+            out[other : other + size] = own_ref[other : other + size].astype(out.dtype)
+        added = own_ref[lead : lead + size] + moving_ref[...].astype(jnp.float32)
+        out[lead : lead + size] = added.astype(out.dtype)
+
+
+def ring_add(up, down, up_own, down_own):
+    lanes = up.shape[1]
+    tile = lanes // 2
+    own = pl.BlockSpec((up_own.shape[0], tile), lambda n: (0, n))
+    moving = pl.BlockSpec((up.shape[0], tile), lambda n: (0, n))
+    result = jax.ShapeDtypeStruct(up_own.shape, up.dtype)
+    return pl.pallas_call(
+        add_kernel,
+        out_shape=(result, result),
+        grid=(2,),
+        in_specs=[moving, moving, own, own],
+        out_specs=(own, own),
         name="ring_add",
-    )(moving, own)
+    )(up, down, up_own, down_own)
 
 
 def ring_sums(chunks, far, axis, token):
     size = len(chunks)
     middle = size // 2
-
-    def toward(by, moving, lead):
-        for distance in range(middle - 1, -1, -1):
-            moving = shifted(moving, axis, by)
-            if distance == 0:
-                return moving
-            own = chunks[distance if by == 1 else size - distance]
+    up, down = far
+    for distance in range(middle - 1, -1, -1):
+        up = shifted(up, axis, 1)
+        down = shifted(down, axis, -1)
+        if distance > 0:
+            own = chunks[distance]
             if distance == middle - 1:
-                moving = ring_add(moving, after(own, token), lead)
-            else:
-                moving = ring_add(moving, own, 0)
-
-    half = far[0].shape[0]
-    return chunks[0], toward(1, far[0], 0), toward(-1, far[1], half)
+                own = after(own, token)
+            up, down = ring_add(up, down, own, chunks[size - distance])
+    return chunks[0], up, down
 
 
 def after(x, token):
@@ -240,51 +248,38 @@
 
 
 DIGIT = 64
+TILE = 256
 EXTRA = 16
 
 
-def pack_kernel(rows_hbm, owner_ref, key_ref, *refs):
-    tail_ref, sems = refs[-2:]
-    outs = refs[:-2]
-    size = rows_hbm.shape[0] // len(outs)
-    copies = []
-    for part, out in enumerate(outs):
-        copy = pltpu.make_async_copy(
-            rows_hbm.at[pl.ds(part * size, size)], out.at[pl.ds(0, size)], sems.at[part]
-        )
-        copy.start()
-        copies.append(copy)
+def pack_kernel(rows_ref, owner_ref, key_ref, *outs):
+    size, lanes = rows_ref.shape[0] // len(outs), rows_ref.shape[1]
     key = key_ref[...]
     place = (key & 64) + (key & 7) * R_DEV + ((key >> 3) & 7)
     slot = owner_ref[...] * KEYS + place
-    tail_ref[...] = jnp.zeros(tail_ref.shape, tail_ref.dtype)
+    step = pl.program_id(0)
+    row = lax.broadcasted_iota(jnp.int32, (EXTRA, lanes), 0)
     for part, out in enumerate(outs):
-        own = slot[:, part * size : (part + 1) * size]
-        row = lax.broadcasted_iota(jnp.int32, (EXTRA, size), 0)
-        tail = jnp.where(row == 0, own // DIGIT, jnp.where(row == 1, own % DIGIT, 0))
-        tail_ref[part, :, :size] = tail.astype(jnp.float32).astype(tail_ref.dtype)
-        copy = pltpu.make_async_copy(
-            tail_ref.at[part], out.at[pl.ds(size, EXTRA)], sems.at[len(outs) + part]
-        )
-        copy.start()
-        copies.append(copy)
-    for copy in copies:
-        copy.wait()
+        out[:size] = rows_ref[part * size : (part + 1) * size]
+        tail = jnp.zeros((EXTRA, lanes), jnp.int32)
+        for tile in range(size // lanes):
+            start = part * size + tile * lanes
+            own = slot[:, start : start + lanes]
+            digits = jnp.where(row == 0, own // DIGIT, jnp.where(row == 1, own % DIGIT, 0))
+            tail = jnp.where(step == tile, digits, tail)
+        out[size:] = tail.astype(jnp.float32).astype(out.dtype)
 
 
 def row_pieces(rows, owners, keys, parts):
-    piece = jax.ShapeDtypeStruct((rows.shape[0] // parts + EXTRA, rows.shape[1]), rows.dtype)
-    vmem = pl.BlockSpec(memory_space=pltpu.VMEM)
-    left = pl.BlockSpec(memory_space=pl.ANY)
+    count, lanes = rows.shape
+    piece = jax.ShapeDtypeStruct((count // parts + EXTRA, lanes), rows.dtype)
+    line = pl.BlockSpec((1, count), lambda n: (0, 0))
     return pl.pallas_call(
         pack_kernel,
         out_shape=(piece,) * parts,
-        in_specs=[left, vmem, vmem],
-        out_specs=(left,) * parts,
-        scratch_shapes=[
-            pltpu.VMEM((parts, EXTRA, rows.shape[1]), rows.dtype),
-            pltpu.SemaphoreType.DMA((2 * parts,)),
-        ],
+        grid=(lanes // TILE,),
+        in_specs=[pl.BlockSpec((count, TILE), lambda n: (0, n)), line, line],
+        out_specs=(pl.BlockSpec((piece.shape[0], TILE), lambda n: (0, n)),) * parts,
         name="pack",
     )(rows, owners[None], keys[None])
 
@@ -318,9 +313,6 @@
         out[...] = total[index * rows : (index + 1) * rows].astype(out.dtype)
 
 
-TILE = 256
-
-
 def sum_pieces(pieces, base, place, outs, dtype, first=0, chunks=None):
     columns, rings = lax.axis_size(BLK[1]), lax.axis_size(BLK[0])
     chunks = rings if chunks is None else chunks
@@ -359,9 +351,7 @@
         def add(pieces, base):
             return sum_pieces(pieces, base, self.place, 1, jnp.float32)[0]
 
-        sums = add(self.pieces, None)
-        sums = add([self.up[0], self.down[0]], sums)
-        sums = add([self.up[1], self.down[1]], sums)
+        sums = add([*self.pieces, *self.up, *self.down], None)
         rings = lax.axis_size(BLK[0])
         last = [self.up_far, self.down_far]
         far = sum_pieces(last, sums, self.place, 2, jnp.bfloat16, rings // 2, 1)

time: 215 us -> 142 us (0.66)
  the two profiles are of different devices: /device:TPU:8 before, /device:TPU:32 now
where the time goes in v3:
time: 142 us
  Pallas kernels  51.9 us (37%)
  starting transfers between devices  45.6 us (32%)
  waiting for transfers between devices  33.5 us (24%)
  local copies, waits for them, and re-layouts  7.87 us (6%)
  other arithmetic  1.9 us (1%)
    pallas_call x3, Pallas kernels, sum_pieces(): pl.pallas_call(functools.partial(sums_kernel, len(pieces), int(base is no...  22.4 us
    ppermute x14, starting transfers between devices, shifted(): return lax.ppermute(x, axis, [(i, (i + by) % size) for i in range(size)])  18.8 us
    ppermute x14, waiting for transfers between devices, shifted(): return lax.ppermute(x, axis, [(i, (i + by) % size) for i in range(size)])  14.8 us
    all_to_all x1, starting transfers between devices, body(): arrived = lax.all_to_all(sums, BLK, split_axis=0, concat_axis=0, tiled=True)  10.1 us
    all_to_all x1, starting transfers between devices, body(): lax.all_to_all(summed, BLK, split_axis=0, concat_axis=0, tiled=True)  8.98 us
    all_to_all x1, waiting for transfers between devices, body(): arrived = lax.all_to_all(sums, BLK, split_axis=0, concat_axis=0, tiled=True)  7.33 us
    pallas_call x3, Pallas kernels, ring_add(): pl.pallas_call(add_kernel, out_shape=(result, result), grid=(2,), in_spec...  6.38 us
    all_to_all x1, waiting for transfers between devices, body(): lax.all_to_all(pieces, 'lblk', split_axis=0, concat_axis=0, tiled=True)  6.02 us
  transfers between devices with their start and end apart: 18, of which 8 were waited for; matrix products, arithmetic and copies ran while one was open for 3% of the time, Pallas kernels for 28%

profile of v3, /device:TPU:32, one launch (start us, length us, event | category | flops | bytes accessed | tf_op | source)
XLA Modules:
  0.0 141.5 jit_solution(8969701574309630278)
XLA Ops:
  0.6 3.9 %pack.1 = (bf16[528,1024]{1,0:T(8,128)(2,1)}, bf16[528,1024]{1,0:T(8,128)(2,1)}) custom-call(bf16[1024,1024]{1,0:T(8,128)(2,1)} %bitcast.15, s32[1,1024]{1,0:T(1,128)} %bitcast.20, s32[1,1024]{1,0:T(1,128)} %key_ref.3), custom_call_target="tpu_custom_call" | custom-call | tf_op jit(solution)/shard_map/pack/pallas_call | solution.py:277
  4.6 1.6 %collective-permute-start = (bf16[528,1024]{1,0:T(8,128)(2,1)}, bf16[528,1024]{1,0:T(8,128)(2,1)}, u32[]{:S(2)}, u32[]{:S(2)}) collective-permute-start(bf16[528,1024]{1,0:T(8,128)(2,1)} %get-tuple-element.22.refs_0_.refs_6_), channel_id=1, source_target_pairs={{0,8},{8,16},{16,24},{24,0},{1,9},{9,17},{17,25},{25,1},{2,10},{10... | collective-permute-start | bytes 3244040 | tf_op jit(solution)/shard_map/ppermute | solution.py:199
  6.2 1.7 %collective-permute-start.2 = (bf16[528,1024]{1,0:T(8,128)(2,1)}, bf16[528,1024]{1,0:T(8,128)(2,1)}, u32[]{:S(2)}, u32[]{:S(2)}) collective-permute-start(bf16[528,1024]{1,0:T(8,128)(2,1)} %get-tuple-element.24.refs_1_.refs_7_), channel_id=1, source_target_pairs={{0,24},{8,0},{16,8},{24,16},{1,25},{9,1},{17,9},{25,17},{2,26},{10... | collective-permute-start | bytes 3244040 | tf_op jit(solution)/shard_map/ppermute | solution.py:199
  9.8 4.7 %modes.1 = f32[32,8,128]{2,1,0:T(8,128)} custom-call(bf16[1024,1024]{1,0:T(8,128)(2,1)} %bitcast.16, s32[1,1024]{1,0:T(1,128)} %bitcast.21, s32[1,1024]{1,0:T(1,128)} %key_ref.3, s32[32,1]{1,0:T(8,128)} %copy.17.order_ref, f32[64,1024]{1,0:T(8,128)} %pad_maximum_fusion.wave_ref), custom_call_target="tpu_custom_call" | custom-call | tf_op jit(solution)/shard_map/modes/pallas_call | solution.py:81
  14.6 10.1 %all-to-all-start = ((f32[32,8,128]{2,1,0:T(8,128)}), f32[32,8,128]{2,1,0:T(8,128)S(1)}, u32[]{:S(2)}, u32[]{:S(2)}) async-start(f32[32,8,128]{2,1,0:T(8,128)} %modes.1), calls=%async_computation | async-start | bytes 262144 | tf_op jit(solution)/shard_map/all_to_all | solution.py:389
  24.7 1.5 %collective-permute-start.4 = (bf16[528,1024]{1,0:T(8,128)(2,1)}, bf16[528,1024]{1,0:T(8,128)(2,1)}, u32[]{:S(2)}, u32[]{:S(2)}) collective-permute-start(bf16[528,1024]{1,0:T(8,128)(2,1)} %get-tuple-element.24.refs_1_.refs_7_), channel_id=1, source_target_pairs={{0,8},{8,16},{16,24},{24,0},{1,9},{9,17},{17,25},{25,1},{2,10},{10... | collective-permute-start | bytes 3244040 | tf_op jit(solution)/shard_map/ppermute | solution.py:199
  26.3 1.8 %collective-permute-start.5 = (bf16[528,1024]{1,0:T(8,128)(2,1)S(1)}, bf16[528,1024]{1,0:T(8,128)(2,1)}, u32[]{:S(2)}, u32[]{:S(2)}) collective-permute-start(bf16[528,1024]{1,0:T(8,128)(2,1)S(1)} %copy-done.2), channel_id=1, source_target_pairs={{0,24},{8,0},{16,8},{24,16},{1,25},{9,1},{17,9},{25,17},{2,26},{10... | collective-permute-start | bytes 3244040 | tf_op jit(solution)/shard_map/ppermute | solution.py:199
  28.1 7.3 %all-to-all-done.in_ref = f32[32,8,128]{2,1,0:T(8,128)S(1)} async-done(((f32[32,8,128]{2,1,0:T(8,128)}), f32[32,8,128]{2,1,0:T(8,128)S(1)}, u32[]{:S(2)}, u32[]{:S(2)}) %all-to-all-start) | async-done | bytes 131104 | tf_op jit(solution)/shard_map/all_to_all | solution.py:389
  36.7 1.9 %collective-permute-start.3 = (bf16[528,1024]{1,0:T(8,128)(2,1)}, bf16[528,1024]{1,0:T(8,128)(2,1)S(1)}, u32[]{:S(2)}, u32[]{:S(2)}) collective-permute-start(bf16[528,1024]{1,0:T(8,128)(2,1)} %collective-permute-done.2.refs_4_.refs_10_), channel_id=1, source_target_pairs={{0,24},{8,0},{16,8},{24,16},{1,25},{9,1},{17,9},{25,17},{2,26},{10... | collective-permute-start | bytes 3244040 | tf_op jit(solution)/shard_map/ppermute | solution.py:199
  38.6 1.5 %harmonics.1 = bf16[8,8,128]{2,1,0:T(8,128)(2,1)} custom-call(f32[32,8,128]{2,1,0:T(8,128)} %copy-done.3), custom_call_target="tpu_custom_call" | custom-call | tf_op jit(solution)/shard_map/harmonics/pallas_call | solution.py:96
  40.2 4.3 %all-to-all-start.1 = ((bf16[8,8,128]{2,1,0:T(8,128)(2,1)}), bf16[8,8,128]{2,1,0:T(8,128)(2,1)S(1)}, u32[]{:S(2)}, u32[]{:S(2)}) async-start(bf16[8,8,128]{2,1,0:T(8,128)(2,1)} %harmonics.1), calls=%async_computation.1 | async-start | bytes 32768 | tf_op jit(solution)/shard_map/all_to_all | solution.py:392
  44.5 5.4 %all-to-all-done.1.modes_ref = bf16[8,8,128]{2,1,0:T(8,128)(2,1)S(1)} async-done(((bf16[8,8,128]{2,1,0:T(8,128)(2,1)}), bf16[8,8,128]{2,1,0:T(8,128)(2,1)S(1)}, u32[]{:S(2)}, u32[]{:S(2)}) %all-to-all-start.1) | async-done | bytes 16416 | tf_op jit(solution)/shard_map/all_to_all | solution.py:392
  50.4 5.4 %legendre.1 = f32[8,12,256]{2,1,0:T(8,128)} custom-call(s32[1]{0:T(128)} %bitcast.first_ref, bf16[8,8,128]{2,1,0:T(8,128)(2,1)} %copy-done.12, bf16[1,512,2048]{2,1,0:T(8,128)(2,1)} %leg_ref.1, bf16[1,512,2048]{2,1,0:T(8,128)(2,1)} %even_hbm.1, bf16[1,512,2048]{2,1,0:T(8,128)(2,1)} %odd_hbm.1), custom_call_target="tpu_custom_call" | custom-call | tf_op jit(solution)/shard_map/legendre/pallas_call | solution.py:144
  55.9 3.4 %all-to-all-start.2 = ((f32[8,12,256]{2,1,0:T(8,128)}), f32[8,12,256]{2,1,0:T(8,128)S(1)}, u32[]{:S(2)}, u32[]{:S(2)}) async-start(f32[8,12,256]{2,1,0:T(8,128)} %legendre.1), calls=%async_computation.2 | async-start | bytes 262144 | tf_op jit(solution)/shard_map/all_to_all | solution.py:395
  59.3 6.0 %all-to-all-done.2 = f32[8,12,256]{2,1,0:T(8,128)S(1)} async-done(((f32[8,12,256]{2,1,0:T(8,128)}), f32[8,12,256]{2,1,0:T(8,128)S(1)}, u32[]{:S(2)}, u32[]{:S(2)}) %all-to-all-start.2) | async-done | bytes 98336 | tf_op jit(solution)/shard_map/all_to_all | solution.py:395
  66.3 9.0 %all-to-all-start.3 = ((bf16[32,1,96]{2,1,0:T(2,128)(2,1)}), bf16[32,1,96]{2,1,0:T(2,128)(2,1)S(1)}, u32[]{:S(2)}, u32[]{:S(2)}) async-start(bf16[32,1,96]{2,1,0:T(2,128)(2,1)} %copy.19), calls=%async_computation.3 | async-start | bytes 32768 | tf_op jit(solution)/shard_map/all_to_all | solution.py:398
  75.8 11.4 %shard_map.86.refs_4_ = f32[1024,1024]{1,0:T(8,128)} custom-call(s32[2]{0:T(128)} %pad_add_fusion.place_ref, bf16[528,1024]{1,0:T(8,128)(2,1)} %get-tuple-element.22.refs_0_.refs_6_, bf16[528,1024]{1,0:T(8,128)(2,1)} %get-tuple-element.24.refs_1_.refs_7_, bf16[528,1024]{1,0:T(8,128)(2,1)} %collective-permute-done.refs_2_.refs_8_, ...), custom_call_target="tpu_custom_call" | custom-call | tf_op jit(solution)/shard_map/pallas_call | solution.py:328
  89.3 4.1 %shard_map.88 = (bf16[64,1024]{1,0:T(8,128)(2,1)}, bf16[64,1024]{1,0:T(8,128)(2,1)}) custom-call(s32[2]{0:T(128)} %pad_add_fusion.place_ref, bf16[528,1024]{1,0:T(8,128)(2,1)} %copy-done, bf16[528,1024]{1,0:T(8,128)(2,1)} %copy-done.1, bf16[528,1024]{1,0:T(8,128)(2,1)} %copy-done, bf16[528,1024]{1,0:T(8,128)(2,1)} %copy-done.1, f32[1024,1024]{1,0:T(8,128)} %shard_map.86.refs_4_), custom_call_target="tpu_custom_call" | custom-call | tf_op jit(solution)/shard_map/pallas_call | solution.py:328
  93.4 1.5 %collective-permute-start.6 = (bf16[64,1024]{1,0:T(8,128)(2,1)}, bf16[64,1024]{1,0:T(8,128)(2,1)S(1)}, u32[]{:S(2)}, u32[]{:S(2)}) collective-permute-start(bf16[64,1024]{1,0:T(8,128)(2,1)} %get-tuple-element.27), channel_id=1, source_target_pairs={{0,32},{32,64},{64,96},{96,128},{128,160},{160,192},{192,224},{224... | collective-permute-start | bytes 393224 | tf_op jit(solution)/shard_map/ppermute | solution.py:199
  95.4 6.9 %shard_map.87 = (f32[128,1024]{1,0:T(8,128)}, f32[128,1024]{1,0:T(8,128)}, f32[128,1024]{1,0:T(8,128)}, f32[128,1024]{1,0:T(8,128)}, f32[128,1024]{1,0:T(8,128)}...) custom-call(s32[2]{0:T(128)} %pad_add_fusion.place_ref, bf16[528,1024]{1,0:T(8,128)(2,1)} %copy-done, ...), custom_call_target="tpu_custom_call" | custom-call | tf_op jit(solution)/shard_map/pallas_call | solution.py:328
  103.1 2.1 %ring_add.3 = (bf16[128,1024]{1,0:T(8,128)(2,1)}, bf16[128,1024]{1,0:T(8,128)(2,1)}) custom-call(bf16[64,1024]{1,0:T(8,128)(2,1)} %copy-done.10, bf16[64,1024]{1,0:T(8,128)(2,1)} %copy-done.11, f32[128,1024]{1,0:T(8,128)} %get-tuple-element.30.up_own_ref, f32[128,1024]{1,0:T(8,128)} %get-tuple-element.31.down_own_ref), custom_call_target="tpu_custom_call" | custom-call | tf_op jit(solution)/shard_map/ring_add/pallas_call | solution.py:221
  105.1 1.5 %collective-permute-start.8 = (bf16[128,1024]{1,0:T(8,128)(2,1)}, bf16[128,1024]{1,0:T(8,128)(2,1)S(1)}, u32[]{:S(2)}, u32[]{:S(2)}) collective-permute-start(bf16[128,1024]{1,0:T(8,128)(2,1)} %get-tuple-element.32), channel_id=1, source_target_pairs={{0,32},{32,64},{64,96},{96,128},{128,160},{160,192},{192,224},{224... | collective-permute-start | bytes 786440 | tf_op jit(solution)/shard_map/ppermute | solution.py:199
  107.2 5.1 %collective-permute-done.8.up_ref = bf16[128,1024]{1,0:T(8,128)(2,1)S(1)} collective-permute-done((bf16[128,1024]{1,0:T(8,128)(2,1)}, bf16[128,1024]{1,0:T(8,128)(2,1)S(1)}, u32[]{:S(2)}, u32[]{:S(2)}) %collective-permute-start.8) | collective-permute-done | bytes 262176 | tf_op jit(solution)/shard_map/ppermute | solution.py:199
  112.2 1.7 %collective-permute-done.9.down_ref = bf16[128,1024]{1,0:T(8,128)(2,1)S(1)} collective-permute-done((bf16[128,1024]{1,0:T(8,128)(2,1)}, bf16[128,1024]{1,0:T(8,128)(2,1)S(1)}, u32[]{:S(2)}, u32[]{:S(2)}) %collective-permute-start.9) | collective-permute-done | bytes 262176 | tf_op jit(solution)/shard_map/ppermute | solution.py:199
  114.7 2.2 %ring_add.4 = (bf16[128,1024]{1,0:T(8,128)(2,1)}, bf16[128,1024]{1,0:T(8,128)(2,1)}) custom-call(bf16[128,1024]{1,0:T(8,128)(2,1)} %copy-done.5, bf16[128,1024]{1,0:T(8,128)(2,1)} %copy-done.8, f32[128,1024]{1,0:T(8,128)} %get-tuple-element.34.up_own_ref, f32[128,1024]{1,0:T(8,128)} %get-tuple-element.35.down_own_ref), custom_call_target="tpu_custom_call" | custom-call | tf_op jit(solution)/shard_map/ring_add/pallas_call | solution.py:221
  116.8 2.9 %collective-permute-start.10 = (bf16[128,1024]{1,0:T(8,128)(2,1)}, bf16[128,1024]{1,0:T(8,128)(2,1)S(1)}, u32[]{:S(2)}, u32[]{:S(2)}) collective-permute-start(bf16[128,1024]{1,0:T(8,128)(2,1)} %get-tuple-element.36), channel_id=1, source_target_pairs={{0,32},{32,64},{64,96},{96,128},{128,160},{160,192},{192,224},{224... | collective-permute-start | bytes 786440 | tf_op jit(solution)/shard_map/ppermute | solution.py:199
  119.8 4.2 %collective-permute-done.10.up_ref = bf16[128,1024]{1,0:T(8,128)(2,1)S(1)} collective-permute-done((bf16[128,1024]{1,0:T(8,128)(2,1)}, bf16[128,1024]{1,0:T(8,128)(2,1)S(1)}, u32[]{:S(2)}, u32[]{:S(2)}) %collective-permute-start.10) | collective-permute-done | bytes 262176 | tf_op jit(solution)/shard_map/ppermute | solution.py:199
  124.0 3.3 %collective-permute-done.11.down_ref = bf16[128,1024]{1,0:T(8,128)(2,1)S(1)} collective-permute-done((bf16[128,1024]{1,0:T(8,128)(2,1)}, bf16[128,1024]{1,0:T(8,128)(2,1)S(1)}, u32[]{:S(2)}, u32[]{:S(2)}) %collective-permute-start.11) | collective-permute-done | bytes 262176 | tf_op jit(solution)/shard_map/ppermute | solution.py:199
  128.0 2.2 %ring_add.5 = (bf16[128,1024]{1,0:T(8,128)(2,1)}, bf16[128,1024]{1,0:T(8,128)(2,1)}) custom-call(bf16[128,1024]{1,0:T(8,128)(2,1)} %copy-done.6, bf16[128,1024]{1,0:T(8,128)(2,1)} %copy-done.9, f32[128,1024]{1,0:T(8,128)} %get-tuple-element.38.up_own_ref, f32[128,1024]{1,0:T(8,128)} %get-tuple-element.39.down_own_ref), custom_call_target="tpu_custom_call" | custom-call | tf_op jit(solution)/shard_map/ring_add/pallas_call | solution.py:221
  130.2 2.0 %collective-permute-start.12 = (bf16[128,1024]{1,0:T(8,128)(2,1)}, bf16[128,1024]{1,0:T(8,128)(2,1)S(1)}, u32[]{:S(2)}, u32[]{:S(2)}) collective-permute-start(bf16[128,1024]{1,0:T(8,128)(2,1)} %get-tuple-element.40), channel_id=1, source_target_pairs={{0,32},{32,64},{64,96},{96,128},{128,160},{160,192},{192,224},{224... | collective-permute-start | bytes 786440 | tf_op jit(solution)/shard_map/ppermute | solution.py:199
  132.9 5.4 %fields.1 = f32[2,2,1,8,8192]{4,3,2,1,0:T(8,128)} custom-call(f32[12,8,32]{2,1,0:T(8,128)} %bitcast.18, s32[1,32]{1,0:T(1,128)} %bitcast.22, f32[64,1024]{1,0:T(8,128)} %pad_maximum_fusion.wave_ref), custom_call_target="tpu_custom_call" | custom-call | tf_op jit(solution)/shard_map/fields/pallas_call | solution.py:187
  139.5 2.0 %maps.1 = f32[2,1,8,8192]{3,2,1,0:T(8,128)} custom-call(f32[128,1024]{1,0:T(8,128)} %get-tuple-element.26.own_ref, bf16[128,1024]{1,0:T(8,128)(2,1)} %copy-done.4, bf16[128,1024]{1,0:T(8,128)(2,1)} %copy-done.7), custom_call_target="tpu_custom_call" | custom-call | tf_op jit(solution)/shard_map/maps/pallas_call | solution.py:371
  (54 shorter events, 12.7 us)
Async XLA Ops:
  0.6 7.2 %copy-start.13 = (s32[32]{0:T(128)S(1)}, s32[32]{0:T(128)}, u32[]{:S(2)}) copy-start(s32[32]{0:T(128)} %param.10) | copy-start | bytes 388
  4.6 30.8 %collective-permute-start = (bf16[528,1024]{1,0:T(8,128)(2,1)}, bf16[528,1024]{1,0:T(8,128)(2,1)}, u32[]{:S(2)}, u32[]{:S(2)}) collective-permute-start(bf16[528,1024]{1,0:T(8,128)(2,1)} %get-tuple-element.22.refs_0_.refs_6_), channel_id=1, source_target_pairs={{0,8},{8,16},{16,24},{24,0},{1,9},{9,17},{17,25},{25,1},{2,10},{10... | collective-permute-start | bytes 3244040 | tf_op jit(solution)/shard_map/ppermute | solution.py:199
  6.2 30.6 %collective-permute-start.2 = (bf16[528,1024]{1,0:T(8,128)(2,1)}, bf16[528,1024]{1,0:T(8,128)(2,1)}, u32[]{:S(2)}, u32[]{:S(2)}) collective-permute-start(bf16[528,1024]{1,0:T(8,128)(2,1)} %get-tuple-element.24.refs_1_.refs_7_), channel_id=1, source_target_pairs={{0,24},{8,0},{16,8},{24,16},{1,25},{9,1},{17,9},{25,17},{2,26},{10... | collective-permute-start | bytes 3244040 | tf_op jit(solution)/shard_map/ppermute | solution.py:199
  9.8 16.4 %copy-start.2 = (bf16[528,1024]{1,0:T(8,128)(2,1)S(1)}, bf16[528,1024]{1,0:T(8,128)(2,1)}, u32[]{:S(2)}) copy-start(bf16[528,1024]{1,0:T(8,128)(2,1)} %get-tuple-element.22.refs_0_.refs_6_) | copy-start | bytes 3244036
  14.6 20.8 %all-to-all-start = ((f32[32,8,128]{2,1,0:T(8,128)}), f32[32,8,128]{2,1,0:T(8,128)S(1)}, u32[]{:S(2)}, u32[]{:S(2)}) async-start(f32[32,8,128]{2,1,0:T(8,128)} %modes.1), calls=%async_computation | async-start | bytes 262144 | tf_op jit(solution)/shard_map/all_to_all | solution.py:389
  24.7 51.1 %collective-permute-start.4 = (bf16[528,1024]{1,0:T(8,128)(2,1)}, bf16[528,1024]{1,0:T(8,128)(2,1)}, u32[]{:S(2)}, u32[]{:S(2)}) collective-permute-start(bf16[528,1024]{1,0:T(8,128)(2,1)} %get-tuple-element.24.refs_1_.refs_7_), channel_id=1, source_target_pairs={{0,8},{8,16},{16,24},{24,0},{1,9},{9,17},{17,25},{25,1},{2,10},{10... | collective-permute-start | bytes 3244040 | tf_op jit(solution)/shard_map/ppermute | solution.py:199
  26.3 49.6 %collective-permute-start.5 = (bf16[528,1024]{1,0:T(8,128)(2,1)S(1)}, bf16[528,1024]{1,0:T(8,128)(2,1)}, u32[]{:S(2)}, u32[]{:S(2)}) collective-permute-start(bf16[528,1024]{1,0:T(8,128)(2,1)S(1)} %copy-done.2), channel_id=1, source_target_pairs={{0,24},{8,0},{16,8},{24,16},{1,25},{9,1},{17,9},{25,17},{2,26},{10... | collective-permute-start | bytes 3244040 | tf_op jit(solution)/shard_map/ppermute | solution.py:199
  35.4 3.2 %copy-start.3 = (f32[32,8,128]{2,1,0:T(8,128)}, f32[32,8,128]{2,1,0:T(8,128)S(1)}, u32[]{:S(2)}) copy-start(f32[32,8,128]{2,1,0:T(8,128)S(1)} %all-to-all-done.in_ref) | copy-start | bytes 393220
  35.4 51.9 %collective-permute-start.1 = (bf16[528,1024]{1,0:T(8,128)(2,1)}, bf16[528,1024]{1,0:T(8,128)(2,1)S(1)}, u32[]{:S(2)}, u32[]{:S(2)}) collective-permute-start(bf16[528,1024]{1,0:T(8,128)(2,1)} %collective-permute-done.refs_2_.refs_8_), channel_id=1, source_target_pairs={{0,8},{8,16},{16,24},{24,0},{1,9},{9,17},{17,25},{25,1},{2,10},{10... | collective-permute-start | bytes 3244040 | tf_op jit(solution)/shard_map/ppermute | solution.py:199
  36.7 50.6 %collective-permute-start.3 = (bf16[528,1024]{1,0:T(8,128)(2,1)}, bf16[528,1024]{1,0:T(8,128)(2,1)S(1)}, u32[]{:S(2)}, u32[]{:S(2)}) collective-permute-start(bf16[528,1024]{1,0:T(8,128)(2,1)} %collective-permute-done.2.refs_4_.refs_10_), channel_id=1, source_target_pairs={{0,24},{8,0},{16,8},{24,16},{1,25},{9,1},{17,9},{25,17},{2,26},{10... | collective-permute-start | bytes 3244040 | tf_op jit(solution)/shard_map/ppermute | solution.py:199
  40.2 9.7 %all-to-all-start.1 = ((bf16[8,8,128]{2,1,0:T(8,128)(2,1)}), bf16[8,8,128]{2,1,0:T(8,128)(2,1)S(1)}, u32[]{:S(2)}, u32[]{:S(2)}) async-start(bf16[8,8,128]{2,1,0:T(8,128)(2,1)} %harmonics.1), calls=%async_computation.1 | async-start | bytes 32768 | tf_op jit(solution)/shard_map/all_to_all | solution.py:392
  49.8 0.6 copy-start.12
  55.9 9.4 %all-to-all-start.2 = ((f32[8,12,256]{2,1,0:T(8,128)}), f32[8,12,256]{2,1,0:T(8,128)S(1)}, u32[]{:S(2)}, u32[]{:S(2)}) async-start(f32[8,12,256]{2,1,0:T(8,128)} %legendre.1), calls=%async_computation.2 | async-start | bytes 262144 | tf_op jit(solution)/shard_map/all_to_all | solution.py:395
  66.3 29.1 %all-to-all-start.3 = ((bf16[32,1,96]{2,1,0:T(2,128)(2,1)}), bf16[32,1,96]{2,1,0:T(2,128)(2,1)S(1)}, u32[]{:S(2)}, u32[]{:S(2)}) async-start(bf16[32,1,96]{2,1,0:T(2,128)(2,1)} %copy.19), calls=%async_computation.3 | async-start | bytes 32768 | tf_op jit(solution)/shard_map/all_to_all | solution.py:398
  87.3 1.0 copy-start
  88.3 1.0 copy-start.1
  93.4 8.9 %collective-permute-start.6 = (bf16[64,1024]{1,0:T(8,128)(2,1)}, bf16[64,1024]{1,0:T(8,128)(2,1)S(1)}, u32[]{:S(2)}, u32[]{:S(2)}) collective-permute-start(bf16[64,1024]{1,0:T(8,128)(2,1)} %get-tuple-element.27), channel_id=1, source_target_pairs={{0,32},{32,64},{64,96},{96,128},{128,160},{160,192},{192,224},{224... | collective-permute-start | bytes 393224 | tf_op jit(solution)/shard_map/ppermute | solution.py:199
  94.9 7.5 %collective-permute-start.7 = (bf16[64,1024]{1,0:T(8,128)(2,1)}, bf16[64,1024]{1,0:T(8,128)(2,1)S(1)}, u32[]{:S(2)}, u32[]{:S(2)}) collective-permute-start(bf16[64,1024]{1,0:T(8,128)(2,1)} %get-tuple-element.28), channel_id=1, source_target_pairs={{0,224},{32,0},{64,32},{96,64},{128,96},{160,128},{192,160},{224,1... | collective-permute-start | bytes 393224 | tf_op jit(solution)/shard_map/ppermute | solution.py:199
  102.3 0.7 copy-start.10
  102.4 0.7 copy-start.11
  105.1 7.1 %collective-permute-start.8 = (bf16[128,1024]{1,0:T(8,128)(2,1)}, bf16[128,1024]{1,0:T(8,128)(2,1)S(1)}, u32[]{:S(2)}, u32[]{:S(2)}) collective-permute-start(bf16[128,1024]{1,0:T(8,128)(2,1)} %get-tuple-element.32), channel_id=1, source_target_pairs={{0,32},{32,64},{64,96},{96,128},{128,160},{160,192},{192,224},{224... | collective-permute-start | bytes 786440 | tf_op jit(solution)/shard_map/ppermute | solution.py:199
  106.6 7.3 %collective-permute-start.9 = (bf16[128,1024]{1,0:T(8,128)(2,1)}, bf16[128,1024]{1,0:T(8,128)(2,1)S(1)}, u32[]{:S(2)}, u32[]{:S(2)}) collective-permute-start(bf16[128,1024]{1,0:T(8,128)(2,1)} %get-tuple-element.33), channel_id=1, source_target_pairs={{0,224},{32,0},{64,32},{96,64},{128,96},{160,128},{192,160},{224,1... | collective-permute-start | bytes 786440 | tf_op jit(solution)/shard_map/ppermute | solution.py:199
  112.2 1.7 %copy-start.5 = (bf16[128,1024]{1,0:T(8,128)(2,1)}, bf16[128,1024]{1,0:T(8,128)(2,1)S(1)}, u32[]{:S(2)}) copy-start(bf16[128,1024]{1,0:T(8,128)(2,1)S(1)} %collective-permute-done.8.up_ref) | copy-start | bytes 786436
  113.9 0.7 copy-start.8
  116.8 7.1 %collective-permute-start.10 = (bf16[128,1024]{1,0:T(8,128)(2,1)}, bf16[128,1024]{1,0:T(8,128)(2,1)S(1)}, u32[]{:S(2)}, u32[]{:S(2)}) collective-permute-start(bf16[128,1024]{1,0:T(8,128)(2,1)} %get-tuple-element.36), channel_id=1, source_target_pairs={{0,32},{32,64},{64,96},{96,128},{128,160},{160,192},{192,224},{224... | collective-permute-start | bytes 786440 | tf_op jit(solution)/shard_map/ppermute | solution.py:199
  119.8 7.5 %collective-permute-start.11 = (bf16[128,1024]{1,0:T(8,128)(2,1)}, bf16[128,1024]{1,0:T(8,128)(2,1)S(1)}, u32[]{:S(2)}, u32[]{:S(2)}) collective-permute-start(bf16[128,1024]{1,0:T(8,128)(2,1)} %get-tuple-element.37), channel_id=1, source_target_pairs={{0,224},{32,0},{64,32},{96,64},{128,96},{160,128},{192,160},{224,1... | collective-permute-start | bytes 786440 | tf_op jit(solution)/shard_map/ppermute | solution.py:199
  124.0 3.3 %copy-start.6 = (bf16[128,1024]{1,0:T(8,128)(2,1)}, bf16[128,1024]{1,0:T(8,128)(2,1)S(1)}, u32[]{:S(2)}) copy-start(bf16[128,1024]{1,0:T(8,128)(2,1)S(1)} %collective-permute-done.10.up_ref) | copy-start | bytes 786436
  127.3 0.7 copy-start.9
  130.2 8.1 %collective-permute-start.12 = (bf16[128,1024]{1,0:T(8,128)(2,1)}, bf16[128,1024]{1,0:T(8,128)(2,1)S(1)}, u32[]{:S(2)}, u32[]{:S(2)}) collective-permute-start(bf16[128,1024]{1,0:T(8,128)(2,1)} %get-tuple-element.40), channel_id=1, source_target_pairs={{0,32},{32,64},{64,96},{96,128},{128,160},{160,192},{192,224},{224... | collective-permute-start | bytes 786440 | tf_op jit(solution)/shard_map/ppermute | solution.py:199
  132.2 6.6 %collective-permute-start.13 = (bf16[128,1024]{1,0:T(8,128)(2,1)}, bf16[128,1024]{1,0:T(8,128)(2,1)S(1)}, u32[]{:S(2)}, u32[]{:S(2)}) collective-permute-start(bf16[128,1024]{1,0:T(8,128)(2,1)} %get-tuple-element.41), channel_id=1, source_target_pairs={{0,224},{32,0},{64,32},{96,64},{128,96},{160,128},{192,160},{224,1... | collective-permute-start | bytes 786440 | tf_op jit(solution)/shard_map/ppermute | solution.py:199
  138.3 0.7 copy-start.4
  138.8 0.7 copy-start.7

commit v4 on v3

--- a/solution.py
+++ b/solution.py
@@ -34,10 +34,12 @@
 
 
 def wave_tables(azimuth_orders):
-    phase = lax.broadcasted_iota(jnp.int32, (azimuth_orders.shape[0], SEG), 1)
-    phase = phase * azimuth_orders[:, None] % NPHI
-    angles = phase.astype(jnp.float32) * (2.0 * math.pi / NPHI)
-    return jnp.concatenate([jnp.cos(angles), jnp.sin(angles)], axis=0)
+    orders = azimuth_orders.shape[0]
+    trig = lax.broadcasted_iota(jnp.int32, (2, orders, SEG), 0)
+    pixel = lax.broadcasted_iota(jnp.int32, (2, orders, SEG), 2)
+    phase = pixel * azimuth_orders[None, :, None] - trig * (NPHI // 4)
+    angles = (phase & (NPHI - 1)).astype(jnp.float32) * (2.0 * math.pi / NPHI)
+    return jnp.cos(angles).reshape(2 * orders, SEG)
 
 
 def eighth_turn(index):
@@ -45,21 +47,25 @@
     return jnp.cos(angle), jnp.sin(angle)
 
 
-def modes_kernel(slices, rows_ref, owner_ref, key_ref, order_ref, wave_ref, out_ref):
-    orders = order_ref.shape[0]
+def modes_kernel(slices, rows_ref, owner_ref, key_ref, wave_ref, out_ref):
+    orders = wave_ref.shape[0] // 2
     w_high, w_low = halves(wave_ref[...])
     rows = rows_ref[...]
     seg = dot32(w_high, rows, NT) + dot32(w_low, rows, NT)
     cos_part, sin_part = seg[:orders], seg[orders:]
     key = key_ref[...]
-    turn_cos, turn_sin = eighth_turn(order_ref[...] * (key & (POS - 1)))
-    modes = jnp.concatenate(
-        [
-            cos_part * turn_cos - sin_part * turn_sin,
-            sin_part * turn_cos + cos_part * turn_sin,
-        ],
-        axis=0,
-    )
+    half = wave_ref[:, SEG // 2 : SEG // 2 + 1]
+    turn_cos, turn_sin = half[:orders], half[orders:]
+    for bit in range(3):
+        turn_cos, turn_sin = turn_cos * turn_cos - turn_sin * turn_sin, 2.0 * turn_cos * turn_sin
+        turned = (key & (1 << bit)) != 0
+        step_cos = jnp.where(turned, turn_cos, 1.0)
+        step_sin = jnp.where(turned, turn_sin, 0.0)
+        cos_part, sin_part = (
+            cos_part * step_cos - sin_part * step_sin,
+            sin_part * step_cos + cos_part * step_sin,
+        )
+    modes = jnp.concatenate([cos_part, sin_part], axis=0)
     cycles = slices * R_DEV
     slot = (key >> 6) * cycles + owner_ref[...] * R_DEV + ((key >> 3) & (R_DEV - 1))
     pick = lax.broadcasted_iota(jnp.int32, (2 * cycles, PR), 0) == slot
@@ -76,13 +82,13 @@
                 ]
 
 
-def local_modes(rows, owners, keys, azimuth_orders, waves, groups):
-    orders = azimuth_orders.shape[0]
+def local_modes(rows, owners, keys, waves, groups):
+    orders = waves.shape[0] // 2
     return pl.pallas_call(
         functools.partial(modes_kernel, groups),
         out_shape=jax.ShapeDtypeStruct((orders, groups * R_DEV * 4 // 128, 128), jnp.float32),
         name="modes",
-    )(rows, owners, keys, azimuth_orders[:, None], waves)
+    )(rows, owners, keys, waves)
 
 
 def harmonics_kernel(in_ref, out_ref):
@@ -257,34 +263,23 @@
     key = key_ref[...]
     place = (key & 64) + (key & 7) * R_DEV + ((key >> 3) & 7)
     slot = owner_ref[...] * KEYS + place
-    step = pl.program_id(0)
-    row = lax.broadcasted_iota(jnp.int32, (EXTRA, lanes), 0)
+    row = lax.broadcasted_iota(jnp.int32, (EXTRA, size), 0)
     for part, out in enumerate(outs):
+        own = slot[:, part * size : (part + 1) * size]
+        tail = jnp.where(row == 0, own // DIGIT, jnp.where(row == 1, own % DIGIT, 0))
         out[:size] = rows_ref[part * size : (part + 1) * size]
-        tail = jnp.zeros((EXTRA, lanes), jnp.int32)
-        for tile in range(size // lanes):
-            start = part * size + tile * lanes
-            own = slot[:, start : start + lanes]
-            digits = jnp.where(row == 0, own // DIGIT, jnp.where(row == 1, own % DIGIT, 0))
-            tail = jnp.where(step == tile, digits, tail)
-        out[size:] = tail.astype(jnp.float32).astype(out.dtype)
+        out[size:] = jnp.zeros((EXTRA, lanes), out.dtype)
+        out[size:, :size] = tail.astype(jnp.float32).astype(out.dtype)
 
 
 def row_pieces(rows, owners, keys, parts):
-    count, lanes = rows.shape
-    piece = jax.ShapeDtypeStruct((count // parts + EXTRA, lanes), rows.dtype)
-    line = pl.BlockSpec((1, count), lambda n: (0, 0))
-    return pl.pallas_call(
-        pack_kernel,
-        out_shape=(piece,) * parts,
-        grid=(lanes // TILE,),
-        in_specs=[pl.BlockSpec((count, TILE), lambda n: (0, n)), line, line],
-        out_specs=(pl.BlockSpec((piece.shape[0], TILE), lambda n: (0, n)),) * parts,
-        name="pack",
-    )(rows, owners[None], keys[None])
-
-
-def sums_kernel(count, has_base, columns, rings, first, place_ref, *refs):
+    piece = jax.ShapeDtypeStruct((rows.shape[0] // parts + EXTRA, rows.shape[1]), rows.dtype)
+    return pl.pallas_call(pack_kernel, out_shape=(piece,) * parts, name="pack")(
+        rows, owners[None], keys[None]
+    )
+
+
+def sums_kernel(count, has_base, columns, rings, place_ref, *refs):
     pieces, tails = refs[:count], refs[count : 2 * count]
     outs, pick_ref = refs[2 * count + has_base : -1], refs[-1]
     slots = pick_ref.shape[0]
@@ -298,7 +293,7 @@
             slot = tail[0:1] * DIGIT + tail[1:2]
             owner = slot // KEYS
             distance = (owner // columns - my_z) & (rings - 1)
-            mine = (distance - first) * KEYS + (slot & (KEYS - 1))
+            mine = distance * KEYS + (slot & (KEYS - 1))
             mine = jnp.where((owner & (columns - 1)) == my_y, mine, -1)
             pick = lax.broadcasted_iota(jnp.int32, (slots, size), 0) == mine
             pick_ref[:, index * size : (index + 1) * size] = jnp.where(pick, 1.0, 0.0).astype(
@@ -308,29 +303,29 @@
     total = refs[2 * count][...] if has_base else 0.0
     for index, piece in enumerate(pieces):
         total = total + dot32(pick_ref[:, index * size : (index + 1) * size], piece[...], NN)
-    rows = slots // len(outs)
-    for index, out in enumerate(outs):
-        out[...] = total[index * rows : (index + 1) * rows].astype(out.dtype)
-
-
-def sum_pieces(pieces, base, place, outs, dtype, first=0, chunks=None):
+    start = 0
+    for out in outs:
+        out[...] = total[start : start + out.shape[0]].astype(out.dtype)
+        start += out.shape[0]
+
+
+def sum_pieces(pieces, base, place, outs):
     columns, rings = lax.axis_size(BLK[1]), lax.axis_size(BLK[0])
-    chunks = rings if chunks is None else chunks
     size, lanes = pieces[0].shape[0] - EXTRA, pieces[0].shape[1]
-    slots = chunks * KEYS
+    slots = rings * KEYS
     specs = [pl.BlockSpec(memory_space=pltpu.SMEM)]
     specs += [pl.BlockSpec((size, TILE), lambda n: (0, n)) for _ in pieces]
     specs += [pl.BlockSpec((EXTRA, lanes), lambda n: (size // EXTRA, 0)) for _ in pieces]
     operands = [*pieces, *pieces]
     if base is not None:
-        specs.append(pl.BlockSpec((slots, TILE), lambda n: (first // chunks, n)))
+        specs.append(pl.BlockSpec((slots, TILE), lambda n: (0, n)))
         operands.append(base)
     return pl.pallas_call(
-        functools.partial(sums_kernel, len(pieces), int(base is not None), columns, rings, first),
-        out_shape=tuple(jax.ShapeDtypeStruct((slots // outs, lanes), dtype) for _ in range(outs)),
+        functools.partial(sums_kernel, len(pieces), int(base is not None), columns, rings),
+        out_shape=tuple(jax.ShapeDtypeStruct((rows, lanes), dtype) for rows, dtype in outs),
         grid=(lanes // TILE,),
         in_specs=specs,
-        out_specs=tuple(pl.BlockSpec((slots // outs, TILE), lambda n: (0, n)) for _ in range(outs)),
+        out_specs=tuple(pl.BlockSpec((rows, TILE), lambda n: (0, n)) for rows, _ in outs),
         scratch_shapes=[pltpu.VMEM((slots, size * len(pieces)), jnp.bfloat16)],
     )(place, *operands)
 
@@ -348,31 +343,36 @@
         self.down_far = shifted(after(self.down[0], token), BLK[1], -1)
 
     def finish(self, token):
-        def add(pieces, base):
-            return sum_pieces(pieces, base, self.place, 1, jnp.float32)[0]
-
-        sums = add([*self.pieces, *self.up, *self.down], None)
         rings = lax.axis_size(BLK[0])
-        last = [self.up_far, self.down_far]
-        far = sum_pieces(last, sums, self.place, 2, jnp.bfloat16, rings // 2, 1)
-        chunks = sum_pieces(last, sums, self.place, rings, jnp.float32)
-        return ring_sums(chunks, far, BLK[0], token)
+        whole = [(rings * KEYS, jnp.float32)]
+        (sums,) = sum_pieces(self.pieces, None, self.place, whole)
+        (sums,) = sum_pieces([*self.up, *self.down], sums, self.place, whole)
+        one, half = (KEYS, jnp.float32), (KEYS // 2, jnp.bfloat16)
+        side = [one] * (rings // 2)
+        outs = [*side, half, half, *side[1:]]
+        parts = sum_pieces([self.up_far, self.down_far], sums, self.place, outs)
+        middle = rings // 2
+        chunks = [*parts[:middle], None, *parts[middle + 2 :]]
+        return ring_sums(chunks, parts[middle : middle + 2], BLK[0], token)
 
 
 def maps_kernel(own_ref, up_ref, down_ref, out_ref):
     total = own_ref[...] + up_ref[...].astype(jnp.float32) + down_ref[...].astype(jnp.float32)
-    for shell in range(2):
-        for position in range(POS):
-            row = (shell * POS + position) * R_DEV
-            out_ref[shell, 0, :, position * SEG : (position + 1) * SEG] = total[row : row + R_DEV]
+    for position in range(POS):
+        row = position * R_DEV
+        out_ref[0, 0, :, position * SEG : (position + 1) * SEG] = total[row : row + R_DEV]
 
 
 def map_output(own, up, down):
+    shell = pl.BlockSpec((KEYS // 2, SEG), lambda s: (s, 0))
     return pl.pallas_call(
         maps_kernel,
         out_shape=jax.ShapeDtypeStruct((2, 1, R_DEV, NPHI), jnp.float32),
+        grid=(2,),
+        in_specs=[shell, shell, shell],
+        out_specs=pl.BlockSpec((1, 1, R_DEV, NPHI), lambda s: (s, 0, 0, 0)),
         name="maps",
-    )(own, up.astype(jnp.bfloat16), down.astype(jnp.bfloat16))
+    )(own, up, down)
 
 
 def body(partial_rows, row_owner, row_key, azimuth_orders, legendre_table, spin_even, spin_odd):
@@ -385,7 +385,7 @@
     waves = wave_tables(azimuth_orders)
 
     columns = ColumnSums(rows, owners, keys)
-    sums = local_modes(rows, owners[None], keys[None], azimuth_orders, waves, groups)
+    sums = local_modes(rows, owners[None], keys[None], waves, groups)
     arrived = lax.all_to_all(sums, BLK, split_axis=0, concat_axis=0, tiled=True)
     columns.forward(arrived)
     modes = harmonics_for_all(arrived, blocks)

time: 142 us -> 144 us (1.014)
  the two profiles are of different devices: /device:TPU:32 before, /device:TPU:8 now
where the time goes in v4:
time: 144 us; the launch traced here: 143 us
  Pallas kernels  50.8 us (35%)
  starting transfers between devices  49.4 us (34%)
  waiting for transfers between devices  34.6 us (24%)
  local copies, waits for them, and re-layouts  5.38 us (4%)
  other arithmetic  2.37 us (2%)
    pallas_call x3, Pallas kernels, sum_pieces(): pl.pallas_call(functools.partial(sums_kernel, len(pieces), int(base is no...  22.5 us
    ppermute x14, starting transfers between devices, shifted(): return lax.ppermute(x, axis, [(i, (i + by) % size) for i in range(size)])  19.4 us
    ppermute x14, waiting for transfers between devices, shifted(): return lax.ppermute(x, axis, [(i, (i + by) % size) for i in range(size)])  14.9 us
    all_to_all x1, starting transfers between devices, body(): arrived = lax.all_to_all(sums, BLK, split_axis=0, concat_axis=0, tiled=True)  11.6 us
    all_to_all x1, starting transfers between devices, body(): lax.all_to_all(summed, BLK, split_axis=0, concat_axis=0, tiled=True)  10.8 us
    all_to_all x1, waiting for transfers between devices, body(): arrived = lax.all_to_all(sums, BLK, split_axis=0, concat_axis=0, tiled=True)  8.29 us
    pallas_call x3, Pallas kernels, ring_add(): pl.pallas_call(add_kernel, out_shape=(result, result), grid=(2,), in_spec...  6.4 us
    all_to_all x1, waiting for transfers between devices, body(): lax.all_to_all(pieces, 'lblk', split_axis=0, concat_axis=0, tiled=True)  6.02 us
  transfers between devices with their start and end apart: 18, of which 9 were waited for; matrix products, arithmetic and copies ran while one was open for 3% of the time, Pallas kernels for 27%

profile of v4, /device:TPU:8, one launch (start us, length us, event | category | flops | bytes accessed | tf_op | source)
XLA Modules:
  0.0 143.3 jit_solution(16263794039470888477)
XLA Ops:
  0.6 3.1 %pack.1 = (bf16[528,1024]{1,0:T(8,128)(2,1)}, bf16[528,1024]{1,0:T(8,128)(2,1)}) custom-call(bf16[1024,1024]{1,0:T(8,128)(2,1)} %bitcast.14, s32[1,1024]{1,0:T(1,128)} %bitcast.19, s32[1,1024]{1,0:T(1,128)} %key_ref.3), custom_call_target="tpu_custom_call" | custom-call | tf_op jit(solution)/shard_map/pack/pallas_call | solution.py:277
  3.7 1.6 %collective-permute-start = (bf16[528,1024]{1,0:T(8,128)(2,1)}, bf16[528,1024]{1,0:T(8,128)(2,1)S(1)}, u32[]{:S(2)}, u32[]{:S(2)}) collective-permute-start(bf16[528,1024]{1,0:T(8,128)(2,1)} %get-tuple-element.22.refs_0_.refs_2_), channel_id=1, source_target_pairs={{0,8},{8,16},{16,24},{24,0},{1,9},{9,17},{17,25},{25,1},{2,10},{10... | collective-permute-start | bytes 3244040 | tf_op jit(solution)/shard_map/ppermute | solution.py:205
  6.1 1.7 %multiply_cosine_fusion.wave_ref = f32[64,1024]{1,0:T(8,128)} fusion(s32[64]{0:T(128)S(1)} %iota.19, s32[64]{0:T(128)S(1)} %mul.32), kind=kLoop, calls=%fused_computation | loop fusion | flops 327680 | bytes 262656 | tf_op jit(solution)/shard_map/cos | solution.py:42
  7.8 4.5 %modes.1 = f32[32,8,128]{2,1,0:T(8,128)} custom-call(bf16[1024,1024]{1,0:T(8,128)(2,1)} %bitcast.15, s32[1,1024]{1,0:T(1,128)} %bitcast.20, s32[1,1024]{1,0:T(1,128)} %key_ref.3, f32[64,1024]{1,0:T(8,128)} %multiply_cosine_fusion.wave_ref), custom_call_target="tpu_custom_call" | custom-call | tf_op jit(solution)/shard_map/modes/pallas_call | solution.py:87
  12.3 11.6 %all-to-all-start = ((f32[32,8,128]{2,1,0:T(8,128)}), f32[32,8,128]{2,1,0:T(8,128)S(1)}, u32[]{:S(2)}, u32[]{:S(2)}) async-start(f32[32,8,128]{2,1,0:T(8,128)} %modes.1), calls=%async_computation | async-start | bytes 262144 | tf_op jit(solution)/shard_map/all_to_all | solution.py:389
  23.9 1.5 %collective-permute-start.4 = (bf16[528,1024]{1,0:T(8,128)(2,1)}, bf16[528,1024]{1,0:T(8,128)(2,1)}, u32[]{:S(2)}, u32[]{:S(2)}) collective-permute-start(bf16[528,1024]{1,0:T(8,128)(2,1)} %get-tuple-element.24.refs_1_.refs_3_), channel_id=1, source_target_pairs={{0,8},{8,16},{16,24},{24,0},{1,9},{9,17},{17,25},{25,1},{2,10},{10... | collective-permute-start | bytes 3244040 | tf_op jit(solution)/shard_map/ppermute | solution.py:205
  26.0 8.3 %all-to-all-done.in_ref = f32[32,8,128]{2,1,0:T(8,128)S(1)} async-done(((f32[32,8,128]{2,1,0:T(8,128)}), f32[32,8,128]{2,1,0:T(8,128)S(1)}, u32[]{:S(2)}, u32[]{:S(2)}) %all-to-all-start) | async-done | bytes 131104 | tf_op jit(solution)/shard_map/all_to_all | solution.py:389
  36.4 1.5 %harmonics.1 = bf16[8,8,128]{2,1,0:T(8,128)(2,1)} custom-call(f32[32,8,128]{2,1,0:T(8,128)} %copy-done.3), custom_call_target="tpu_custom_call" | custom-call | tf_op jit(solution)/shard_map/harmonics/pallas_call | solution.py:102
  38.0 4.3 %all-to-all-start.1 = ((bf16[8,8,128]{2,1,0:T(8,128)(2,1)}), bf16[8,8,128]{2,1,0:T(8,128)(2,1)S(1)}, u32[]{:S(2)}, u32[]{:S(2)}) async-start(bf16[8,8,128]{2,1,0:T(8,128)(2,1)} %harmonics.1), calls=%async_computation.1 | async-start | bytes 32768 | tf_op jit(solution)/shard_map/all_to_all | solution.py:392
  42.3 5.4 %all-to-all-done.1.modes_ref = bf16[8,8,128]{2,1,0:T(8,128)(2,1)S(1)} async-done(((bf16[8,8,128]{2,1,0:T(8,128)(2,1)}), bf16[8,8,128]{2,1,0:T(8,128)(2,1)S(1)}, u32[]{:S(2)}, u32[]{:S(2)}) %all-to-all-start.1) | async-done | bytes 16416 | tf_op jit(solution)/shard_map/all_to_all | solution.py:392
  48.2 5.4 %legendre.1 = f32[8,12,256]{2,1,0:T(8,128)} custom-call(s32[1]{0:T(128)} %bitcast.first_ref, bf16[8,8,128]{2,1,0:T(8,128)(2,1)} %copy-done.12, bf16[1,512,2048]{2,1,0:T(8,128)(2,1)} %leg_ref.1, bf16[1,512,2048]{2,1,0:T(8,128)(2,1)} %even_hbm.1, bf16[1,512,2048]{2,1,0:T(8,128)(2,1)} %odd_hbm.1), custom_call_target="tpu_custom_call" | custom-call | tf_op jit(solution)/shard_map/legendre/pallas_call | solution.py:150
  53.7 3.4 %all-to-all-start.2 = ((f32[8,12,256]{2,1,0:T(8,128)}), f32[8,12,256]{2,1,0:T(8,128)S(1)}, u32[]{:S(2)}, u32[]{:S(2)}) async-start(f32[8,12,256]{2,1,0:T(8,128)} %legendre.1), calls=%async_computation.2 | async-start | bytes 262144 | tf_op jit(solution)/shard_map/all_to_all | solution.py:395
  57.1 6.0 %all-to-all-done.2 = f32[8,12,256]{2,1,0:T(8,128)S(1)} async-done(((f32[8,12,256]{2,1,0:T(8,128)}), f32[8,12,256]{2,1,0:T(8,128)S(1)}, u32[]{:S(2)}, u32[]{:S(2)}) %all-to-all-start.2) | async-done | bytes 98336 | tf_op jit(solution)/shard_map/all_to_all | solution.py:395
  64.1 10.8 %all-to-all-start.3 = ((bf16[32,1,96]{2,1,0:T(2,128)(2,1)}), bf16[32,1,96]{2,1,0:T(2,128)(2,1)S(1)}, u32[]{:S(2)}, u32[]{:S(2)}) async-start(bf16[32,1,96]{2,1,0:T(2,128)(2,1)} %copy.14), calls=%async_computation.3 | async-start | bytes 32768 | tf_op jit(solution)/shard_map/all_to_all | solution.py:398
  75.5 6.2 %shard_map.86.refs_8_ = f32[1024,1024]{1,0:T(8,128)} custom-call(s32[2]{0:T(128)} %pad_add_fusion.place_ref, bf16[528,1024]{1,0:T(8,128)(2,1)} %get-tuple-element.22.refs_0_.refs_2_, bf16[528,1024]{1,0:T(8,128)(2,1)} %get-tuple-element.24.refs_1_.refs_3_, bf16[528,1024]{1,0:T(8,128)(2,1)} %get-tuple-element.22.refs_0_.refs_2_, ...), custom_call_target="tpu_custom_call" | custom-call | tf_op jit(solution)/shard_map/pallas_call | solution.py:323
  81.7 9.7 %shard_map.87.refs_4_ = f32[1024,1024]{1,0:T(8,128)} custom-call(s32[2]{0:T(128)} %pad_add_fusion.place_ref, bf16[528,1024]{1,0:T(8,128)(2,1)} %copy-done, bf16[528,1024]{1,0:T(8,128)(2,1)} %collective-permute-done.4.refs_1_.refs_5_, bf16[528,1024]{1,0:T(8,128)(2,1)} %copy-done.1, bf16[528,1024]{1,0:T(8,128)(2,1)} %collective-permute-done.5.refs_3_.refs_7_, ...), custom_call_target="tpu_custom_call" | custom-call | tf_op jit(solution)/shard_map/pallas_call | solution.py:323
  91.4 6.6 %shard_map.88 = (f32[128,1024]{1,0:T(8,128)}, f32[128,1024]{1,0:T(8,128)}, f32[128,1024]{1,0:T(8,128)}, f32[128,1024]{1,0:T(8,128)}, bf16[64,1024]{1,0:T(8,128)(...) custom-call(s32[2]{0:T(128)} %pad_add_fusion.place_ref, ...), custom_call_target="tpu_custom_call" | custom-call | tf_op jit(solution)/shard_map/pallas_call | solution.py:323
  98.1 1.5 %collective-permute-start.6 = (bf16[64,1024]{1,0:T(8,128)(2,1)}, bf16[64,1024]{1,0:T(8,128)(2,1)S(1)}, u32[]{:S(2)}, u32[]{:S(2)}) collective-permute-start(bf16[64,1024]{1,0:T(8,128)(2,1)} %get-tuple-element.27), channel_id=1, source_target_pairs={{0,32},{32,64},{64,96},{96,128},{128,160},{160,192},{192,224},{224... | collective-permute-start | bytes 393224 | tf_op jit(solution)/shard_map/ppermute | solution.py:205
  99.6 1.8 %collective-permute-start.7 = (bf16[64,1024]{1,0:T(8,128)(2,1)}, bf16[64,1024]{1,0:T(8,128)(2,1)S(1)}, u32[]{:S(2)}, u32[]{:S(2)}) collective-permute-start(bf16[64,1024]{1,0:T(8,128)(2,1)} %get-tuple-element.28), channel_id=1, source_target_pairs={{0,224},{32,0},{64,32},{96,64},{128,96},{160,128},{192,160},{224,1... | collective-permute-start | bytes 393224 | tf_op jit(solution)/shard_map/ppermute | solution.py:205
  101.4 3.1 %collective-permute-done.6.up_ref = bf16[64,1024]{1,0:T(8,128)(2,1)S(1)} collective-permute-done((bf16[64,1024]{1,0:T(8,128)(2,1)}, bf16[64,1024]{1,0:T(8,128)(2,1)S(1)}, u32[]{:S(2)}, u32[]{:S(2)}) %collective-permute-start.6) | collective-permute-done | bytes 131104 | tf_op jit(solution)/shard_map/ppermute | solution.py:205
  105.4 2.1 %ring_add.3 = (bf16[128,1024]{1,0:T(8,128)(2,1)}, bf16[128,1024]{1,0:T(8,128)(2,1)}) custom-call(bf16[64,1024]{1,0:T(8,128)(2,1)} %copy-done.10, bf16[64,1024]{1,0:T(8,128)(2,1)} %copy-done.11, f32[128,1024]{1,0:T(8,128)} %get-tuple-element.30.up_own_ref, f32[128,1024]{1,0:T(8,128)} %get-tuple-element.31.down_own_ref), custom_call_target="tpu_custom_call" | custom-call | tf_op jit(solution)/shard_map/ring_add/pallas_call | solution.py:227
  107.5 1.5 %collective-permute-start.8 = (bf16[128,1024]{1,0:T(8,128)(2,1)}, bf16[128,1024]{1,0:T(8,128)(2,1)S(1)}, u32[]{:S(2)}, u32[]{:S(2)}) collective-permute-start(bf16[128,1024]{1,0:T(8,128)(2,1)} %get-tuple-element.32), channel_id=1, source_target_pairs={{0,32},{32,64},{64,96},{96,128},{128,160},{160,192},{192,224},{224... | collective-permute-start | bytes 786440 | tf_op jit(solution)/shard_map/ppermute | solution.py:205
  109.0 1.8 %collective-permute-start.9 = (bf16[128,1024]{1,0:T(8,128)(2,1)}, bf16[128,1024]{1,0:T(8,128)(2,1)S(1)}, u32[]{:S(2)}, u32[]{:S(2)}) collective-permute-start(bf16[128,1024]{1,0:T(8,128)(2,1)} %get-tuple-element.33), channel_id=1, source_target_pairs={{0,224},{32,0},{64,32},{96,64},{128,96},{160,128},{192,160},{224,1... | collective-permute-start | bytes 786440 | tf_op jit(solution)/shard_map/ppermute | solution.py:205
  110.7 4.6 %collective-permute-done.8.up_ref = bf16[128,1024]{1,0:T(8,128)(2,1)S(1)} collective-permute-done((bf16[128,1024]{1,0:T(8,128)(2,1)}, bf16[128,1024]{1,0:T(8,128)(2,1)S(1)}, u32[]{:S(2)}, u32[]{:S(2)}) %collective-permute-start.8) | collective-permute-done | bytes 262176 | tf_op jit(solution)/shard_map/ppermute | solution.py:205
  116.3 2.2 %ring_add.4 = (bf16[128,1024]{1,0:T(8,128)(2,1)}, bf16[128,1024]{1,0:T(8,128)(2,1)}) custom-call(bf16[128,1024]{1,0:T(8,128)(2,1)} %copy-done.5, bf16[128,1024]{1,0:T(8,128)(2,1)} %copy-done.8, f32[128,1024]{1,0:T(8,128)} %get-tuple-element.34.up_own_ref, f32[128,1024]{1,0:T(8,128)} %get-tuple-element.35.down_own_ref), custom_call_target="tpu_custom_call" | custom-call | tf_op jit(solution)/shard_map/ring_add/pallas_call | solution.py:227
  118.5 3.2 %collective-permute-start.10 = (bf16[128,1024]{1,0:T(8,128)(2,1)}, bf16[128,1024]{1,0:T(8,128)(2,1)S(1)}, u32[]{:S(2)}, u32[]{:S(2)}) collective-permute-start(bf16[128,1024]{1,0:T(8,128)(2,1)} %get-tuple-element.36), channel_id=1, source_target_pairs={{0,32},{32,64},{64,96},{96,128},{128,160},{160,192},{192,224},{224... | collective-permute-start | bytes 786440 | tf_op jit(solution)/shard_map/ppermute | solution.py:205
  121.8 4.6 %collective-permute-done.10.up_ref = bf16[128,1024]{1,0:T(8,128)(2,1)S(1)} collective-permute-done((bf16[128,1024]{1,0:T(8,128)(2,1)}, bf16[128,1024]{1,0:T(8,128)(2,1)S(1)}, u32[]{:S(2)}, u32[]{:S(2)}) %collective-permute-start.10) | collective-permute-done | bytes 262176 | tf_op jit(solution)/shard_map/ppermute | solution.py:205
  126.3 2.0 %collective-permute-done.11.down_ref = bf16[128,1024]{1,0:T(8,128)(2,1)S(1)} collective-permute-done((bf16[128,1024]{1,0:T(8,128)(2,1)}, bf16[128,1024]{1,0:T(8,128)(2,1)S(1)}, u32[]{:S(2)}, u32[]{:S(2)}) %collective-permute-start.11) | collective-permute-done | bytes 262176 | tf_op jit(solution)/shard_map/ppermute | solution.py:205
  129.1 2.2 %ring_add.5 = (bf16[128,1024]{1,0:T(8,128)(2,1)}, bf16[128,1024]{1,0:T(8,128)(2,1)}) custom-call(bf16[128,1024]{1,0:T(8,128)(2,1)} %copy-done.6, bf16[128,1024]{1,0:T(8,128)(2,1)} %copy-done.9, f32[128,1024]{1,0:T(8,128)} %get-tuple-element.38.up_own_ref, f32[128,1024]{1,0:T(8,128)} %get-tuple-element.39.down_own_ref), custom_call_target="tpu_custom_call" | custom-call | tf_op jit(solution)/shard_map/ring_add/pallas_call | solution.py:227
  131.2 2.0 %collective-permute-start.12 = (bf16[128,1024]{1,0:T(8,128)(2,1)}, bf16[128,1024]{1,0:T(8,128)(2,1)S(1)}, u32[]{:S(2)}, u32[]{:S(2)}) collective-permute-start(bf16[128,1024]{1,0:T(8,128)(2,1)} %get-tuple-element.40), channel_id=1, source_target_pairs={{0,32},{32,64},{64,96},{96,128},{128,160},{160,192},{192,224},{224... | collective-permute-start | bytes 786440 | tf_op jit(solution)/shard_map/ppermute | solution.py:205
  135.2 5.4 %fields.1 = f32[2,2,1,8,8192]{4,3,2,1,0:T(8,128)} custom-call(f32[12,8,32]{2,1,0:T(8,128)} %bitcast.17, s32[1,32]{1,0:T(1,128)} %bitcast.21, f32[64,1024]{1,0:T(8,128)} %multiply_cosine_fusion.wave_ref), custom_call_target="tpu_custom_call" | custom-call | tf_op jit(solution)/shard_map/fields/pallas_call | solution.py:193
  141.4 2.0 %maps.1 = f32[2,1,8,8192]{3,2,1,0:T(8,128)} custom-call(f32[128,1024]{1,0:T(8,128)} %get-tuple-element.26.own_ref, bf16[128,1024]{1,0:T(8,128)(2,1)} %copy-done.4, bf16[128,1024]{1,0:T(8,128)(2,1)} %copy-done.7), custom_call_target="tpu_custom_call" | custom-call | tf_op jit(solution)/shard_map/maps/pallas_call | solution.py:368
  (57 shorter events, 11.2 us)
Async XLA Ops:
  0.6 5.4 %copy-start.13 = (s32[32]{0:T(128)S(1)}, s32[32]{0:T(128)}, u32[]{:S(2)}) copy-start(s32[32]{0:T(128)} %param.10) | copy-start | bytes 388
  3.7 30.6 %collective-permute-start = (bf16[528,1024]{1,0:T(8,128)(2,1)}, bf16[528,1024]{1,0:T(8,128)(2,1)S(1)}, u32[]{:S(2)}, u32[]{:S(2)}) collective-permute-start(bf16[528,1024]{1,0:T(8,128)(2,1)} %get-tuple-element.22.refs_0_.refs_2_), channel_id=1, source_target_pairs={{0,8},{8,16},{16,24},{24,0},{1,9},{9,17},{17,25},{25,1},{2,10},{10... | collective-permute-start | bytes 3244040 | tf_op jit(solution)/shard_map/ppermute | solution.py:205
  5.3 29.7 %collective-permute-start.2 = (bf16[528,1024]{1,0:T(8,128)(2,1)}, bf16[528,1024]{1,0:T(8,128)(2,1)S(1)}, u32[]{:S(2)}, u32[]{:S(2)}) collective-permute-start(bf16[528,1024]{1,0:T(8,128)(2,1)} %get-tuple-element.24.refs_1_.refs_3_), channel_id=1, source_target_pairs={{0,24},{8,0},{16,8},{24,16},{1,25},{9,1},{17,9},{25,17},{2,26},{10... | collective-permute-start | bytes 3244040 | tf_op jit(solution)/shard_map/ppermute | solution.py:205
  7.8 17.6 %copy-start.2 = (bf16[528,1024]{1,0:T(8,128)(2,1)S(1)}, bf16[528,1024]{1,0:T(8,128)(2,1)}, u32[]{:S(2)}) copy-start(bf16[528,1024]{1,0:T(8,128)(2,1)} %get-tuple-element.22.refs_0_.refs_2_) | copy-start | bytes 3244036
  12.3 22.0 %all-to-all-start = ((f32[32,8,128]{2,1,0:T(8,128)}), f32[32,8,128]{2,1,0:T(8,128)S(1)}, u32[]{:S(2)}, u32[]{:S(2)}) async-start(f32[32,8,128]{2,1,0:T(8,128)} %modes.1), calls=%async_computation | async-start | bytes 262144 | tf_op jit(solution)/shard_map/all_to_all | solution.py:389
  23.9 57.8 %collective-permute-start.4 = (bf16[528,1024]{1,0:T(8,128)(2,1)}, bf16[528,1024]{1,0:T(8,128)(2,1)}, u32[]{:S(2)}, u32[]{:S(2)}) collective-permute-start(bf16[528,1024]{1,0:T(8,128)(2,1)} %get-tuple-element.24.refs_1_.refs_3_), channel_id=1, source_target_pairs={{0,8},{8,16},{16,24},{24,0},{1,9},{9,17},{17,25},{25,1},{2,10},{10... | collective-permute-start | bytes 3244040 | tf_op jit(solution)/shard_map/ppermute | solution.py:205
  25.4 56.3 %collective-permute-start.5 = (bf16[528,1024]{1,0:T(8,128)(2,1)S(1)}, bf16[528,1024]{1,0:T(8,128)(2,1)}, u32[]{:S(2)}, u32[]{:S(2)}) collective-permute-start(bf16[528,1024]{1,0:T(8,128)(2,1)S(1)} %copy-done.2), channel_id=1, source_target_pairs={{0,24},{8,0},{16,8},{24,16},{1,25},{9,1},{17,9},{25,17},{2,26},{10... | collective-permute-start | bytes 3244040 | tf_op jit(solution)/shard_map/ppermute | solution.py:205
  34.3 2.1 %copy-start.3 = (f32[32,8,128]{2,1,0:T(8,128)}, f32[32,8,128]{2,1,0:T(8,128)S(1)}, u32[]{:S(2)}) copy-start(f32[32,8,128]{2,1,0:T(8,128)S(1)} %all-to-all-done.in_ref) | copy-start | bytes 393220
  34.3 19.4 %copy-start = (bf16[528,1024]{1,0:T(8,128)(2,1)}, bf16[528,1024]{1,0:T(8,128)(2,1)S(1)}, u32[]{:S(2)}) copy-start(bf16[528,1024]{1,0:T(8,128)(2,1)S(1)} %collective-permute-done.refs_0_.refs_4_) | copy-start | bytes 3244036
  34.3 57.1 %collective-permute-start.1 = (bf16[528,1024]{1,0:T(8,128)(2,1)S(1)}, bf16[528,1024]{1,0:T(8,128)(2,1)}, u32[]{:S(2)}, u32[]{:S(2)}) collective-permute-start(bf16[528,1024]{1,0:T(8,128)(2,1)S(1)} %collective-permute-done.refs_0_.refs_4_), channel_id=1, source_target_pairs={{0,8},{8,16},{16,24},{24,0},{1,9},{9,17},{17,25},{25,1},{2,10},{10... | collective-permute-start | bytes 3244040 | tf_op jit(solution)/shard_map/ppermute | solution.py:205
  35.0 18.7 %copy-start.1 = (bf16[528,1024]{1,0:T(8,128)(2,1)}, bf16[528,1024]{1,0:T(8,128)(2,1)S(1)}, u32[]{:S(2)}) copy-start(bf16[528,1024]{1,0:T(8,128)(2,1)S(1)} %collective-permute-done.2.refs_2_.refs_6_) | copy-start | bytes 3244036
  35.0 56.4 %collective-permute-start.3 = (bf16[528,1024]{1,0:T(8,128)(2,1)S(1)}, bf16[528,1024]{1,0:T(8,128)(2,1)}, u32[]{:S(2)}, u32[]{:S(2)}) collective-permute-start(bf16[528,1024]{1,0:T(8,128)(2,1)S(1)} %collective-permute-done.2.refs_2_.refs_6_), channel_id=1, source_target_pairs={{0,24},{8,0},{16,8},{24,16},{1,25},{9,1},{17,9},{25,17},{2,26},{10... | collective-permute-start | bytes 3244040 | tf_op jit(solution)/shard_map/ppermute | solution.py:205
  38.0 9.7 %all-to-all-start.1 = ((bf16[8,8,128]{2,1,0:T(8,128)(2,1)}), bf16[8,8,128]{2,1,0:T(8,128)(2,1)S(1)}, u32[]{:S(2)}, u32[]{:S(2)}) async-start(bf16[8,8,128]{2,1,0:T(8,128)(2,1)} %harmonics.1), calls=%async_computation.1 | async-start | bytes 32768 | tf_op jit(solution)/shard_map/all_to_all | solution.py:392
  47.6 0.6 copy-start.12
  53.7 9.4 %all-to-all-start.2 = ((f32[8,12,256]{2,1,0:T(8,128)}), f32[8,12,256]{2,1,0:T(8,128)S(1)}, u32[]{:S(2)}, u32[]{:S(2)}) async-start(f32[8,12,256]{2,1,0:T(8,128)} %legendre.1), calls=%async_computation.2 | async-start | bytes 262144 | tf_op jit(solution)/shard_map/all_to_all | solution.py:395
  64.1 37.3 %all-to-all-start.3 = ((bf16[32,1,96]{2,1,0:T(2,128)(2,1)}), bf16[32,1,96]{2,1,0:T(2,128)(2,1)S(1)}, u32[]{:S(2)}, u32[]{:S(2)}) async-start(bf16[32,1,96]{2,1,0:T(2,128)(2,1)} %copy.14), calls=%async_computation.3 | async-start | bytes 32768 | tf_op jit(solution)/shard_map/all_to_all | solution.py:398
  98.1 6.5 %collective-permute-start.6 = (bf16[64,1024]{1,0:T(8,128)(2,1)}, bf16[64,1024]{1,0:T(8,128)(2,1)S(1)}, u32[]{:S(2)}, u32[]{:S(2)}) collective-permute-start(bf16[64,1024]{1,0:T(8,128)(2,1)} %get-tuple-element.27), channel_id=1, source_target_pairs={{0,32},{32,64},{64,96},{96,128},{128,160},{160,192},{192,224},{224... | collective-permute-start | bytes 393224 | tf_op jit(solution)/shard_map/ppermute | solution.py:205
  99.6 5.2 %collective-permute-start.7 = (bf16[64,1024]{1,0:T(8,128)(2,1)}, bf16[64,1024]{1,0:T(8,128)(2,1)S(1)}, u32[]{:S(2)}, u32[]{:S(2)}) collective-permute-start(bf16[64,1024]{1,0:T(8,128)(2,1)} %get-tuple-element.28), channel_id=1, source_target_pairs={{0,224},{32,0},{64,32},{96,64},{128,96},{160,128},{192,160},{224,1... | collective-permute-start | bytes 393224 | tf_op jit(solution)/shard_map/ppermute | solution.py:205
  104.5 0.7 copy-start.10
  104.8 0.7 copy-start.11
  107.5 7.8 %collective-permute-start.8 = (bf16[128,1024]{1,0:T(8,128)(2,1)}, bf16[128,1024]{1,0:T(8,128)(2,1)S(1)}, u32[]{:S(2)}, u32[]{:S(2)}) collective-permute-start(bf16[128,1024]{1,0:T(8,128)(2,1)} %get-tuple-element.32), channel_id=1, source_target_pairs={{0,32},{32,64},{64,96},{96,128},{128,160},{160,192},{192,224},{224... | collective-permute-start | bytes 786440 | tf_op jit(solution)/shard_map/ppermute | solution.py:205
  109.0 6.7 %collective-permute-start.9 = (bf16[128,1024]{1,0:T(8,128)(2,1)}, bf16[128,1024]{1,0:T(8,128)(2,1)S(1)}, u32[]{:S(2)}, u32[]{:S(2)}) collective-permute-start(bf16[128,1024]{1,0:T(8,128)(2,1)} %get-tuple-element.33), channel_id=1, source_target_pairs={{0,224},{32,0},{64,32},{96,64},{128,96},{160,128},{192,160},{224,1... | collective-permute-start | bytes 786440 | tf_op jit(solution)/shard_map/ppermute | solution.py:205
  115.3 0.7 copy-start.5
  115.6 0.7 copy-start.8
  118.5 7.8 %collective-permute-start.10 = (bf16[128,1024]{1,0:T(8,128)(2,1)}, bf16[128,1024]{1,0:T(8,128)(2,1)S(1)}, u32[]{:S(2)}, u32[]{:S(2)}) collective-permute-start(bf16[128,1024]{1,0:T(8,128)(2,1)} %get-tuple-element.36), channel_id=1, source_target_pairs={{0,32},{32,64},{64,96},{96,128},{128,160},{160,192},{192,224},{224... | collective-permute-start | bytes 786440 | tf_op jit(solution)/shard_map/ppermute | solution.py:205
  121.8 6.6 %collective-permute-start.11 = (bf16[128,1024]{1,0:T(8,128)(2,1)}, bf16[128,1024]{1,0:T(8,128)(2,1)S(1)}, u32[]{:S(2)}, u32[]{:S(2)}) collective-permute-start(bf16[128,1024]{1,0:T(8,128)(2,1)} %get-tuple-element.37), channel_id=1, source_target_pairs={{0,224},{32,0},{64,32},{96,64},{128,96},{160,128},{192,160},{224,1... | collective-permute-start | bytes 786440 | tf_op jit(solution)/shard_map/ppermute | solution.py:205
  126.3 2.0 %copy-start.6 = (bf16[128,1024]{1,0:T(8,128)(2,1)}, bf16[128,1024]{1,0:T(8,128)(2,1)S(1)}, u32[]{:S(2)}) copy-start(bf16[128,1024]{1,0:T(8,128)(2,1)S(1)} %collective-permute-done.10.up_ref) | copy-start | bytes 786436
  128.3 0.7 copy-start.9
  131.2 9.4 %collective-permute-start.12 = (bf16[128,1024]{1,0:T(8,128)(2,1)}, bf16[128,1024]{1,0:T(8,128)(2,1)S(1)}, u32[]{:S(2)}, u32[]{:S(2)}) collective-permute-start(bf16[128,1024]{1,0:T(8,128)(2,1)} %get-tuple-element.40), channel_id=1, source_target_pairs={{0,32},{32,64},{64,96},{96,128},{128,160},{160,192},{192,224},{224... | collective-permute-start | bytes 786440 | tf_op jit(solution)/shard_map/ppermute | solution.py:205
  133.2 7.3 %collective-permute-start.13 = (bf16[128,1024]{1,0:T(8,128)(2,1)}, bf16[128,1024]{1,0:T(8,128)(2,1)S(1)}, u32[]{:S(2)}, u32[]{:S(2)}) collective-permute-start(bf16[128,1024]{1,0:T(8,128)(2,1)} %get-tuple-element.41), channel_id=1, source_target_pairs={{0,224},{32,0},{64,32},{96,64},{128,96},{160,128},{192,160},{224,1... | collective-permute-start | bytes 786440 | tf_op jit(solution)/shard_map/ppermute | solution.py:205
  140.6 0.7 copy-start.4
  140.6 0.8 copy-start.7
